TPU v7x, 512 devices: a whole 4x4x16 slice. The times are simulated.
512 devices in a mesh: dp: 8 (over y, core), expert: 64 (over x, z).
Axes of the slice: x: 4, y: 4, z: 16, core: 2. Of those that a mesh axis runs over, the one named last changes fastest.
Arguments:
- tokens: bfloat16 [32768, 1024], P(('dp', 'expert')), may hold values from -6 to 6
- expert_ids: int32 [32768, 8], P(('dp', 'expert')), may hold values from 0 to 63, all different within a row; in each aligned block of 64 rows (0 to 63, 64 to 127, ...) at most 10 rows name the same one
- route_weight: float32 [32768, 8], P(('dp', 'expert')), may hold values from 0.05 to 0.5
- out_grad: bfloat16 [32768, 1024], P(('dp', 'expert')), may hold values from -6 to 6
- gate_weight: bfloat16 [64, 1024, 384], P('expert', 'dp'), may hold values from -0.1875 to 0.1875
- up_weight: bfloat16 [64, 1024, 384], P('expert', 'dp'), may hold values from -0.1875 to 0.1875
- down_weight: bfloat16 [64, 384, 1024], P('expert', None, 'dp'), may hold values from -0.3125 to 0.3125
Outputs:
- layer_out: bfloat16 [32768, 1024], P(('dp', 'expert'))
- token_grad: bfloat16 [32768, 1024], P(('dp', 'expert'))
- route_grad: float32 [32768, 8], P(('dp', 'expert'))
- gate_grad: float32 [64, 1024, 384], P('expert', 'dp')
- up_grad: float32 [64, 1024, 384], P('expert', 'dp')
- down_grad: float32 [64, 384, 1024], P('expert', None, 'dp')
Inputs may be any that keep to these rules, and one draw needn't show every extreme that they name: `expert_ids`: each token names 8 different experts. Among the 64 tokens of one device no expert is named by more than 10 tokens, and in every draw some expert is named by exactly 10 tokens of some device.
All inputs are finite; a program needn't handle non-finite values.
Results may differ from a plain program's by a relative error of at most 0.012.
Values may be sent and summed in bfloat16 or wider, within the bound.
No kernel may reach another device: no remote copies, remote signals or barrier semaphores. Data moves between devices by JAX's collectives and lax.ppermute only.
A program may use at most 64 MiB of HBM per device.

v0:
```python
import jax
import jax.numpy as jnp
from jax import lax
from jax.sharding import PartitionSpec as P


def layout(live_counts, slot_cap, padded_rows):
    owners = live_counts.shape[0]
    ends = jnp.cumsum(live_counts).astype(jnp.int32)
    starts = ends - live_counts
    total = ends[owners - 1]
    positions = jnp.arange(padded_rows, dtype=jnp.int32)
    source = jnp.minimum(
        jnp.sum((positions[:, None] >= ends[None, :]).astype(jnp.int32), 1), owners - 1
    )
    matches = source[:, None] == jnp.arange(owners, dtype=jnp.int32)[None, :]
    offset = positions - jnp.sum(jnp.where(matches, starts[None, :], 0), 1)
    valid = positions < total
    pick_rows = jnp.where(valid, source * slot_cap + offset, 0)
    slot_pos = jnp.arange(owners * slot_cap, dtype=jnp.int32) % slot_cap
    live_back = slot_pos < jnp.repeat(live_counts, slot_cap)
    back_rows = jnp.where(live_back, jnp.repeat(starts, slot_cap) + slot_pos, 0)
    return (pick_rows, valid, back_rows, live_back, total)


def compact(received, pick_rows, valid):
    feat_width = received.shape[2]
    rows = received.reshape(-1, feat_width)[pick_rows]
    return jnp.where(valid[:, None], rows, jnp.zeros_like(rows))


def spread(rows, back_rows, live_back, owners, slot_cap):
    picked = rows[back_rows]
    picked = jnp.where(live_back[:, None], picked, jnp.zeros_like(picked))
    return picked.reshape(owners, slot_cap, rows.shape[1])


def shards(tokens, expert_ids, route_weight, out_grad, gate_weight, up_weight, down_weight):
    block_rows = 128
    tok_rows, feat_width = tokens.shape
    top_picks = expert_ids.shape[1]
    hidden_units = gate_weight.shape[2]
    owners = lax.axis_size("expert")
    slot_cap = max(2, 5 * tok_rows * top_picks // (4 * owners))
    slot_total = owners * slot_cap
    padded_rows = -(-slot_total // block_rows) * block_rows
    flat_ids = expert_ids.reshape(-1)
    one_hot = (flat_ids[:, None] == jnp.arange(owners, dtype=jnp.int32)[None, :]).astype(jnp.int32)
    slot_rank = jnp.sum((jnp.cumsum(one_hot, 0) - one_hot) * one_hot, 1)
    pair_slots = flat_ids * slot_cap + slot_rank
    send_counts = jnp.sum(one_hot, 0).reshape(owners, 1)
    x_send = (
        jnp.zeros((slot_total, feat_width), jnp.bfloat16)
        .at[pair_slots]
        .set(jnp.repeat(tokens, top_picks, 0))
        .reshape(owners, slot_cap, feat_width)
    )
    pair_grad = (
        route_weight.reshape(-1, 1) * jnp.repeat(out_grad, top_picks, 0).astype(jnp.float32)
    ).astype(jnp.bfloat16)
    dy_send = (
        jnp.zeros((slot_total, feat_width), jnp.bfloat16)
        .at[pair_slots]
        .set(pair_grad)
        .reshape(owners, slot_cap, feat_width)
    )
    gate_full, up_full, down_full = (
        lax.all_gather(gate_weight, "dp", axis=1, tiled=True),
        lax.all_gather(up_weight, "dp", axis=1, tiled=True),
        lax.all_gather(down_weight, "dp", axis=2, tiled=True),
    )
    gate_full = gate_full[0]
    up_full = up_full[0]
    down_full = down_full[0]
    x_recv, recv_counts = (
        lax.all_to_all(x_send, "expert", split_axis=0, concat_axis=0, tiled=True),
        lax.all_to_all(send_counts, "expert", split_axis=0, concat_axis=0, tiled=True),
    )
    pick_rows, valid, back_rows, live_back, total = layout(recv_counts[:, 0], slot_cap, padded_rows)
    live_blocks = (total + block_rows - 1) // block_rows
    x_rows = compact(x_recv, pick_rows, valid)

    def forward_block(block_id, carry):
        y_buf, h_buf, g_buf, u_buf = carry
        row_start = block_id * block_rows
        x_blk = lax.dynamic_slice_in_dim(x_rows, row_start, block_rows, 0)
        gate_act = jnp.dot(x_blk, gate_full, preferred_element_type=jnp.float32)
        up_act = jnp.dot(x_blk, up_full, preferred_element_type=jnp.float32)
        hidden = (gate_act * jax.nn.sigmoid(gate_act) * up_act).astype(jnp.bfloat16)
        y_blk = jnp.dot(hidden, down_full, preferred_element_type=jnp.float32).astype(jnp.bfloat16)
        return (
            lax.dynamic_update_slice_in_dim(y_buf, y_blk, row_start, 0),
            lax.dynamic_update_slice_in_dim(h_buf, hidden, row_start, 0),
            lax.dynamic_update_slice_in_dim(g_buf, gate_act, row_start, 0),
            lax.dynamic_update_slice_in_dim(u_buf, up_act, row_start, 0),
        )

    forward_init = (
        jnp.zeros((padded_rows, feat_width), jnp.bfloat16),
        jnp.zeros((padded_rows, hidden_units), jnp.bfloat16),
        jnp.zeros((padded_rows, hidden_units), jnp.float32),
        jnp.zeros((padded_rows, hidden_units), jnp.float32),
    )
    y_rows, h_rows, g_rows, u_rows = lax.fori_loop(0, live_blocks, forward_block, forward_init)
    y_back = lax.all_to_all(
        spread(y_rows, back_rows, live_back, owners, slot_cap),
        "expert",
        split_axis=0,
        concat_axis=0,
        tiled=True,
    )
    dy_recv = lax.all_to_all(dy_send, "expert", split_axis=0, concat_axis=0, tiled=True)
    dy_rows = compact(dy_recv, pick_rows, valid)
    contract_last = (((1,), (1,)), ((), ()))
    contract_rows = (((0,), (0,)), ((), ()))

    def backward_block(block_id, carry):
        dx_buf, act_buf = carry
        row_start = block_id * block_rows
        dy_blk = lax.dynamic_slice_in_dim(dy_rows, row_start, block_rows, 0)
        gate_act = lax.dynamic_slice_in_dim(g_rows, row_start, block_rows, 0)
        up_act = lax.dynamic_slice_in_dim(u_rows, row_start, block_rows, 0)
        sigmoid_g = jax.nn.sigmoid(gate_act)
        hidden_grad = lax.dot_general(
            dy_blk, down_full, contract_last, preferred_element_type=jnp.float32
        )
        gate_back = (
            hidden_grad * up_act * sigmoid_g * (1.0 + gate_act * (1.0 - sigmoid_g))
        ).astype(jnp.bfloat16)
        up_back = (hidden_grad * gate_act * sigmoid_g).astype(jnp.bfloat16)
        dx_blk = (
            lax.dot_general(gate_back, gate_full, contract_last, preferred_element_type=jnp.float32)
            + lax.dot_general(up_back, up_full, contract_last, preferred_element_type=jnp.float32)
        ).astype(jnp.bfloat16)
        act_back = jnp.concatenate([gate_back, up_back], 1)
        return (
            lax.dynamic_update_slice_in_dim(dx_buf, dx_blk, row_start, 0),
            lax.dynamic_update_slice_in_dim(act_buf, act_back, row_start, 0),
        )

    backward_init = (
        jnp.zeros((padded_rows, feat_width), jnp.bfloat16),
        jnp.zeros((padded_rows, 2 * hidden_units), jnp.bfloat16),
    )
    dx_rows, act_rows = lax.fori_loop(0, live_blocks, backward_block, backward_init)
    grad_total = jnp.concatenate(
        [
            lax.dot_general(x_rows, act_rows, contract_rows, preferred_element_type=jnp.float32),
            lax.dot_general(dy_rows, h_rows, contract_rows, preferred_element_type=jnp.float32),
        ],
        1,
    )
    dx_back = lax.all_to_all(
        spread(dx_rows, back_rows, live_back, owners, slot_cap),
        "expert",
        split_axis=0,
        concat_axis=0,
        tiled=True,
    )
    y_pairs = y_back.reshape(-1, feat_width)[pair_slots].reshape(tok_rows, top_picks, feat_width)
    dx_pairs = dx_back.reshape(-1, feat_width)[pair_slots].reshape(tok_rows, top_picks, feat_width)
    layer_out = jnp.sum(route_weight[:, :, None] * y_pairs.astype(jnp.float32), 1).astype(
        jnp.bfloat16
    )
    route_grad = jnp.einsum("td,tkd->tk", out_grad, y_pairs, preferred_element_type=jnp.float32)
    token_grad = jnp.sum(dx_pairs.astype(jnp.float32), 1).astype(jnp.bfloat16)
    local_rows = feat_width // lax.axis_size("dp")
    summed = lax.psum(grad_total.astype(jnp.bfloat16), "dp").astype(jnp.float32)
    mine = lax.dynamic_slice_in_dim(summed, lax.axis_index("dp") * local_rows, local_rows, 0)
    gate_grad = mine[:, :hidden_units][None]
    up_grad = mine[:, hidden_units : 2 * hidden_units][None]
    down_grad = mine[:, 2 * hidden_units :].T[None]
    return (layer_out, token_grad, route_grad, gate_grad, up_grad, down_grad)


def solution(mesh):
    placed = (
        P(("dp", "expert"), None),
        P(("dp", "expert"), None),
        P(("dp", "expert"), None),
        P(("dp", "expert"), None),
        P("expert", "dp", None),
        P("expert", "dp", None),
        P("expert", None, "dp"),
    )
    return jax.shard_map(
        shards,
        mesh=mesh,
        in_specs=placed,
        out_specs=(
            P(("dp", "expert"), None),
            P(("dp", "expert"), None),
            P(("dp", "expert"), None),
            P("expert", "dp", None),
            P("expert", "dp", None),
            P("expert", None, "dp"),
        ),
        check_vma=False,
    )
```

profile of v0, /device:TPU:6, one launch (start us, length us, event | category | flops | bytes accessed | tf_op | source)
XLA Modules:
  0.0 552.7 jit_solution(12986864640239789348)
XLA Ops:
  10.6 18.8 %all-to-all-start = ((s32[64,1,1]{2,1,0:T(1,128)}), s32[64,1,1]{2,1,0:T(1,128)S(1)}, u32[]{:S(2)}, u32[]{:S(2)}) async-start(s32[64,1,1]{2,1,0:T(1,128)} %copy.48), calls=%async_computation | async-start | bytes 65536 | tf_op jit(solution)/shard_map/all_to_all | solution.py:77
  37.2 4.6 all-to-all-done
  41.9 10.5 %all-to-all-start.3 = ((bf16[64,10,1024]{2,1,0:T(8,128)(2,1)}), bf16[64,10,1024]{2,1,0:T(8,128)(2,1)S(1)}, u32[]{:S(2)}, u32[]{:S(2)}) async-start(bf16[64,10,1024]{2,1,0:T(8,128)(2,1)} %reshape.248), calls=%async_computation.3 | async-start | bytes 4194304 | tf_op jit(solution)/shard_map/all_to_all | solution.py:112
  52.4 3.7 scatter_custom_fusion
  56.0 3.6 reshape.242
  59.6 90.4 %all-to-all-done.3 = bf16[64,10,1024]{2,1,0:T(8,128)(2,1)S(1)} async-done(((bf16[64,10,1024]{2,1,0:T(8,128)(2,1)}), bf16[64,10,1024]{2,1,0:T(8,128)(2,1)S(1)}, u32[]{:S(2)}, u32[]{:S(2)}) %all-to-all-start.3) | async-done | bytes 1310752 | tf_op jit(solution)/shard_map/all_to_all | solution.py:112
  150.0 7.5 %all-to-all-start.1 = ((bf16[64,10,1024]{2,1,0:T(8,128)(2,1)}), bf16[64,10,1024]{2,1,0:T(8,128)(2,1)}, u32[]{:S(2)}, u32[]{:S(2)}) async-start(bf16[64,10,1024]{2,1,0:T(8,128)(2,1)} %reshape.242), calls=%async_computation.1 | async-start | bytes 4194304 | tf_op jit(solution)/shard_map/all_to_all | solution.py:76
  157.6 13.9 %all_gather.9 = bf16[1,1024,384]{2,1,0:T(8,128)(2,1)S(1)} all-gather(bf16[1,128,384]{2,1,0:T(8,128)(2,1)S(1)} %copy-done.13), channel_id=1, replica_groups=mesh['dp'=8,'expert'=64] {'dp'}, dimensions={1}, use_global_device_ids=true | all-gather | bytes 884736 | tf_op jit(solution)/shard_map/all_gather | solution.py:68
  171.5 13.4 %all_gather.10 = bf16[1,1024,384]{2,1,0:T(8,128)(2,1)S(1)} all-gather(bf16[1,128,384]{2,1,0:T(8,128)(2,1)S(1)} %copy-done.14), channel_id=1, replica_groups=mesh['dp'=8,'expert'=64] {'dp'}, dimensions={1}, use_global_device_ids=true | all-gather | bytes 884736 | tf_op jit(solution)/shard_map/all_gather | solution.py:69
  184.9 14.1 %all_gather.11 = bf16[1,384,1024]{2,1,0:T(8,128)(2,1)} all-gather(bf16[1,384,128]{2,1,0:T(8,128)(2,1)S(1)} %copy-done.15), channel_id=1, replica_groups=mesh['dp'=8,'expert'=64] {'dp'}, dimensions={2}, use_global_device_ids=true | all-gather | bytes 884736 | tf_op jit(solution)/shard_map/all_gather | solution.py:70
  206.3 3.5 gather_fusion.3
  209.8 45.2 %all-to-all-done.1 = bf16[64,10,1024]{2,1,0:T(8,128)(2,1)} async-done(((bf16[64,10,1024]{2,1,0:T(8,128)(2,1)}), bf16[64,10,1024]{2,1,0:T(8,128)(2,1)}, u32[]{:S(2)}, u32[]{:S(2)}) %all-to-all-start.1) | async-done | bytes 1310752 | tf_op jit(solution)/shard_map/all_to_all | solution.py:76
  257.6 3.5 gather_fusion
  261.1 3.5 broadcast_select_fusion.2
  266.8 21.5 %while.28 = (s32[]{:T(128)}, bf16[640,1024]{1,0:T(8,128)(2,1)S(1)}, bf16[640,384]{1,0:T(8,128)(2,1)S(1)}, f32[640,384]{1,0:T(8,128)}, f32[640,384]{1,0:T(8,128)}...) while((s32[]{:T(128)}, bf16[640,1024]{1,0:T(8,128)(2,1)S(1)}, ...), condition=%wide.region_9.10_spmd, body=%wide.region_8.9_spmd.sunk | while | flops 302415872 | bytes 7768279 | solution.py:104
  290.6 16.3 %while.29 = (s32[]{:T(128)}, bf16[640,1024]{1,0:T(8,128)(2,1)S(1)}, bf16[640,768]{1,0:T(8,128)(2,1)}, s32[]{:T(128)}, bf16[640,1024]{1,0:T(8,128)(2,1)}, /*index...) while((s32[]{:T(128)}, bf16[640,1024]{1,0:T(8,128)(2,1)S(1)}, ...), condition=%wide.region_13.14_spmd, body=%wide.region_12.13_spmd.sunk | while | flops 303284224 | bytes 8258775 | solution.py:145
  306.9 3.5 gather_fusion.4
  310.4 3.6 gather.28
  313.9 3.5 gather_fusion.1
  317.5 3.7 gather.24
  321.2 3.3 broadcast_select_fusion
  324.5 104.4 %all_to_all.32 = bf16[64,10,1024]{2,1,0:T(8,128)(2,1)} all-to-all(bf16[64,10,1024]{2,1,0:T(8,128)(2,1)S(1)} %get-tuple-element.204), channel_id=1, replica_groups=mesh['dp'=8,'expert'=64] {'expert'}, dimensions={0} | all-to-all | bytes 2621440 | tf_op jit(solution)/shard_map/all_to_all | solution.py:153
  428.9 9.3 %all-to-all-start.2 = ((bf16[64,10,1024]{2,1,0:T(8,128)(2,1)}), bf16[64,10,1024]{2,1,0:T(8,128)(2,1)}, u32[]{:S(2)}, u32[]{:S(2)}) async-start(bf16[64,10,1024]{2,1,0:T(8,128)(2,1)} %get-tuple-element.205), calls=%async_computation.2 | async-start | bytes 4194304 | tf_op jit(solution)/shard_map/all_to_all | solution.py:105
  444.2 84.9 %all-reduce.2.cloned.1.call-done = bf16[1024,1152]{0,1:T(8,128)(2,1)} async-done(((bf16[1024,1152]{0,1:T(8,128)(2,1)}), bf16[1024,1152]{0,1:T(8,128)(2,1)}) %all-reduce.2.cloned.1.call-update) | async-done | bytes 2359312 | tf_op jit(solution)/shard_map/psum | solution.py:168
  (152 shorter events, 85.0 us)
Async XLA Ops:
  7.2 45.2 %copy-start = (bf16[64,1024]{1,0:T(8,128)(2,1)S(1)}, bf16[64,1024]{1,0:T(8,128)(2,1)}, u32[]{:S(2)}) copy-start(bf16[64,1024]{1,0:T(8,128)(2,1)} %param.11) | copy-start | bytes 393220
  10.6 31.3 %all-to-all-start = ((s32[64,1,1]{2,1,0:T(1,128)}), s32[64,1,1]{2,1,0:T(1,128)S(1)}, u32[]{:S(2)}, u32[]{:S(2)}) async-start(s32[64,1,1]{2,1,0:T(1,128)} %copy.48), calls=%async_computation | async-start | bytes 65536 | tf_op jit(solution)/shard_map/all_to_all | solution.py:77
  41.9 108.2 %all-to-all-start.3 = ((bf16[64,10,1024]{2,1,0:T(8,128)(2,1)}), bf16[64,10,1024]{2,1,0:T(8,128)(2,1)S(1)}, u32[]{:S(2)}, u32[]{:S(2)}) async-start(bf16[64,10,1024]{2,1,0:T(8,128)(2,1)} %reshape.248), calls=%async_computation.3 | async-start | bytes 4194304 | tf_op jit(solution)/shard_map/all_to_all | solution.py:112
  59.6 98.0 %copy-start.13 = (bf16[1,128,384]{2,1,0:T(8,128)(2,1)S(1)}, bf16[1,128,384]{2,1,0:T(8,128)(2,1)}, u32[]{:S(2)}) copy-start(bf16[1,128,384]{2,1,0:T(8,128)(2,1)} %param.15) | copy-start | bytes 294916
  59.6 111.9 %copy-start.14 = (bf16[1,128,384]{2,1,0:T(8,128)(2,1)S(1)}, bf16[1,128,384]{2,1,0:T(8,128)(2,1)}, u32[]{:S(2)}) copy-start(bf16[1,128,384]{2,1,0:T(8,128)(2,1)} %param.16) | copy-start | bytes 294916
  150.0 7.6 %copy-start.5 = (bf16[64,10,1024]{2,1,0:T(8,128)(2,1)}, bf16[64,10,1024]{2,1,0:T(8,128)(2,1)S(1)}, u32[]{:S(2)}) copy-start(bf16[64,10,1024]{2,1,0:T(8,128)(2,1)S(1)} %all-to-all-done.3) | copy-start | bytes 3932164
  150.0 104.9 %all-to-all-start.1 = ((bf16[64,10,1024]{2,1,0:T(8,128)(2,1)}), bf16[64,10,1024]{2,1,0:T(8,128)(2,1)}, u32[]{:S(2)}, u32[]{:S(2)}) async-start(bf16[64,10,1024]{2,1,0:T(8,128)(2,1)} %reshape.242), calls=%async_computation.1 | async-start | bytes 4194304 | tf_op jit(solution)/shard_map/all_to_all | solution.py:76
  157.6 27.3 %copy-start.15 = (bf16[1,384,128]{2,1,0:T(8,128)(2,1)S(1)}, bf16[1,384,128]{2,1,0:T(8,128)(2,1)}, u32[]{:S(2)}) copy-start(bf16[1,384,128]{2,1,0:T(8,128)(2,1)} %param.17) | copy-start | bytes 294916
  266.8 3.3 copy-start.3
  271.1 3.3 copy-start.3
  275.4 3.3 copy-start.3
  279.7 3.3 copy-start.3
  284.0 3.3 copy-start.3
  290.6 2.2 copy-start.2
  293.8 2.2 copy-start.2
  297.1 2.2 copy-start.2
  300.4 2.2 copy-start.2
  303.6 2.2 copy-start.2
  317.5 3.7 copy-start.4
  428.9 9.6 %copy-start.7 = (bf16[640,1024]{1,0:T(8,128)(2,1)S(1)}, bf16[640,1024]{1,0:T(8,128)(2,1)}, u32[]{:S(2)}) copy-start(bf16[640,1024]{1,0:T(8,128)(2,1)} %get-tuple-element.444) | copy-start | bytes 3932164
  428.9 9.6 %copy-start.9 = (bf16[640,384]{1,0:T(8,128)(2,1)S(1)}, bf16[640,384]{1,0:T(8,128)(2,1)}, u32[]{:S(2)}) copy-start(bf16[640,384]{1,0:T(8,128)(2,1)} %copy-done.8) | copy-start | bytes 1474564
  428.9 109.6 %all-to-all-start.2 = ((bf16[64,10,1024]{2,1,0:T(8,128)(2,1)}), bf16[64,10,1024]{2,1,0:T(8,128)(2,1)}, u32[]{:S(2)}, u32[]{:S(2)}) async-start(bf16[64,10,1024]{2,1,0:T(8,128)(2,1)} %get-tuple-element.205), calls=%async_computation.2 | async-start | bytes 4194304 | tf_op jit(solution)/shard_map/all_to_all | solution.py:105
  438.2 90.9 %all-reduce.2.cloned.1.call-start = ((), (), s32[]{:S(2)}) async-start(), calls=%async_computation.5 | async-start | bytes 4718592 | tf_op jit(solution)/shard_map/psum | solution.py:168
  541.1 3.4 copy-start.12
  (5 other events, 6.0 us)
Sparse Core Ops, SparseCore 0:
  444.3 84.7 all-reduce.1
where the time goes:
time: 554 us; the launch traced here: 553 us
  waiting for transfers between devices  225 us (41%)
  blocking collectives  146 us (26%)
  local copies, waits for them, and re-layouts  60.7 us (11%)
  starting transfers between devices  46.4 us (8%)
  matrix products  34.6 us (6%)
  other arithmetic  24.7 us (4%)
  between operations  15.1 us (3%)
    all_to_all x1, blocking collectives, shards(): lax.all_to_all(spread(dx_rows, back_rows, live_back, owners, slot_cap), '...  104 us
    all_to_all x1, waiting for transfers between devices, shards(): lax.all_to_all(dy_send, 'expert', split_axis=0, concat_axis=0, tiled=True)  90.4 us
    psum x1, waiting for transfers between devices, shards(): summed = lax.psum(grad_total.astype(jnp.bfloat16), 'dp').astype(jnp.float32)  84.9 us
    all_to_all x1, waiting for transfers between devices, shards(): lax.all_to_all(x_send, 'expert', split_axis=0, concat_axis=0, tiled=True)  45.2 us
    all_to_all x1, starting transfers between devices, shards(): lax.all_to_all(send_counts, 'expert', split_axis=0, concat_axis=0, tiled=...  18.8 us
    gather x4, local copies, waits for them, and re-layouts, spread(): picked = rows[back_rows]  14.3 us
    all_gather x1, blocking collectives, shards(): lax.all_gather(down_weight, 'dp', axis=2, tiled=True)  14.1 us
    all_gather x1, blocking collectives, shards(): lax.all_gather(gate_weight, 'dp', axis=1, tiled=True)  13.9 us
  transfers between devices with their start and end apart: 5, of which 4 were waited for; matrix products, arithmetic and copies ran while one was open for 7% of the time, Pallas kernels for 0%

commit v1 on v0

v1 whole, which is shorter than its diff:
```python
import jax
import jax.numpy as jnp
from jax import lax
from jax.experimental import pallas as pl
from jax.experimental.pallas import tpu as pltpu
from jax.sharding import Mesh
from jax.sharding import PartitionSpec as P

BF = jnp.bfloat16
F32 = jnp.float32
NX, NZ, NDP = 4, 16, 8
CAP = 10
SLOTS = NZ * CAP
AUX = 128


def dot(a, b, ca, cb):
    return lax.dot_general(a, b, (((ca,), (cb,)), ((), ())), preferred_element_type=F32)


def moe_kernel(col_ref, pos_ref, w_ref, xd_ref, wt_ref, grad_ref, part_ref, sel_all, rows_all):
    e = pl.program_id(0)
    tok = xd_ref.shape[0]
    feat = (xd_ref.shape[1] - AUX) // 2
    hid = wt_ref.shape[3] // 3
    picked = pos_ref[0] == lax.broadcasted_iota(jnp.int32, (SLOTS, tok), 0)
    sel = jnp.where(picked, 1.0, 0.0).astype(BF)
    w = jnp.sum(jnp.where(picked, w_ref[0], 0.0), axis=1, keepdims=True)
    xe = dot(sel, xd_ref[:, :feat], 1, 0).astype(BF)
    de = dot(sel, xd_ref[:, feat + AUX :], 1, 0).astype(BF)
    wt = wt_ref[:, 0].reshape(feat, 3 * hid)
    gu = dot(xe, wt[:, : 2 * hid], 1, 0)
    hd = dot(de, wt[:, 2 * hid :], 1, 0)
    g = gu[:, :hid]
    u = gu[:, hid:]
    s = jax.nn.sigmoid(g)
    gs = g * s
    h = gs * u
    rg = jnp.sum(h * hd, axis=1, keepdims=True)
    wh = (w * h).astype(BF)
    hg = w * hd
    gb = (hg * u * s * (1.0 + g * (1.0 - s))).astype(BF)
    ub = (hg * gs).astype(BF)
    act = jnp.concatenate([gb, ub], axis=1)
    base = pl.multiple_of(e * SLOTS, SLOTS)
    here = pl.ds(base, SLOTS)
    sel_all[here, :] = sel
    rows_all[here, :feat] = dot(wh, wt[:, 2 * hid :], 1, 1).astype(BF)
    rows_all[here, feat + AUX :] = dot(act, wt[:, : 2 * hid], 1, 1).astype(BF)
    lane = lax.broadcasted_iota(jnp.int32, (SLOTS, AUX), 1)
    mine = col_ref[0] + e
    rg_hi = rg.astype(BF).astype(F32)
    aux = jnp.where(lane == mine, rg_hi, 0.0) + jnp.where(lane == mine + AUX // 2, rg - rg_hi, 0.0)
    rows_all[here, feat : feat + AUX] = aux.astype(BF)
    grad_ref[:, 0, :, : 2 * hid] = dot(xe, act, 0, 0).astype(BF).reshape(NDP, feat // NDP, 2 * hid)
    grad_ref[:, 0, :, 2 * hid :] = dot(de, wh, 0, 0).astype(BF).reshape(NDP, feat // NDP, hid)

    @pl.when(e == NX - 1)
    def _():
        for lo in range(0, 2 * feat + AUX, 544):
            part_ref[:, lo : lo + 544] = dot(
                sel_all[...], rows_all[:, lo : lo + 544], 0, 0
            ).astype(BF)


def experts(col, pos, w, xd, wt):
    tok, width = xd.shape
    feat = (width - AUX) // 2
    hid3 = wt.shape[3]
    rows = feat // NDP
    slots = NX * SLOTS
    flops = 2 * slots * (tok * width * 2 + 9 * feat * hid3 // 3)
    return pl.pallas_call(
        moe_kernel,
        grid_spec=pltpu.PrefetchScalarGridSpec(
            num_scalar_prefetch=1,
            grid=(NX,),
            in_specs=[
                pl.BlockSpec((1, 1, tok), lambda e, c: (e, 0, 0)),
                pl.BlockSpec((1, 1, tok), lambda e, c: (e, 0, 0)),
                pl.BlockSpec((tok, width), lambda e, c: (0, 0)),
                pl.BlockSpec((NDP, 1, rows, hid3), lambda e, c: (0, e, 0, 0)),
            ],
            out_specs=[
                pl.BlockSpec((NDP, 1, rows, hid3), lambda e, c: (0, e, 0, 0)),
                pl.BlockSpec((tok, width), lambda e, c: (0, 0)),
            ],
            scratch_shapes=[
                pltpu.VMEM((slots, tok), BF),
                pltpu.VMEM((slots, width), BF),
            ],
        ),
        out_shape=[
            jax.ShapeDtypeStruct((NDP, NX, rows, hid3), BF),
            jax.ShapeDtypeStruct((tok, width), BF),
        ],
        cost_estimate=pl.CostEstimate(
            flops=flops, bytes_accessed=30_000_000, transcendentals=slots * hid3 // 3
        ),
    )(col, pos, w, xd, wt)


def shift(value, step):
    return lax.ppermute(value, "z", [(i, (i + step) % NZ) for i in range(NZ)])


def add(a, b):
    return (a.astype(F32) + b.astype(F32)).astype(BF)


def shards(tokens, expert_ids, route_weight, out_grad, gate_weight, up_weight, down_weight):
    rows, feat = tokens.shape
    hid = gate_weight.shape[2]
    z = lax.axis_index("z")
    half = AUX // 2
    wl = jnp.concatenate([gate_weight[0], up_weight[0], down_weight[0].T], axis=1)
    wa = lax.all_gather(wl, ("y", "c", "x"), axis=0, tiled=True)
    place = (expert_ids % NZ) * NX + expert_ids // NZ
    hot = place[:, :, None] == jnp.arange(half, dtype=jnp.int32)
    dense = jnp.sum(jnp.where(hot, route_weight[:, :, None], 0.0), 1)
    hi = lax.reduce_precision(dense, 8, 7)
    pay = jnp.concatenate([tokens, hi.astype(BF), (dense - hi).astype(BF), out_grad], axis=1)
    blocks = [pay]
    right = left = pay
    for step in range(1, NZ // 2):
        right = shift(right, 1)
        left = shift(left, -1)
        blocks += [right, left]
    cut = feat + AUX
    blocks.append(jnp.concatenate([shift(right[:, :cut], 1), shift(left[:, cut:], -1)], axis=1))
    xd = jnp.concatenate(blocks, axis=0)
    wz = xd[:, feat : feat + half].astype(F32) + xd[:, feat + half : cut].astype(F32)
    wz = lax.dynamic_slice_in_dim(wz, z * NX, NX, 1).T
    live = wz > 0.0
    pos = jnp.where(live, jnp.cumsum(live.astype(jnp.int32), axis=1) - 1, -1)
    col = (z * NX).astype(jnp.int32).reshape(1)
    grads, part = experts(
        col, pos[:, None, :], wz[:, None, :], xd, wa.reshape(NDP, NX, feat // NDP, 3 * hid)
    )
    summed = lax.psum_scatter(
        grads.reshape(-1, 3 * hid), ("y", "c", "x"), scatter_dimension=0, tiled=True
    )

    def block(i):
        return part[i * rows : (i + 1) * rows]

    last = block(NZ - 1)
    toward_right = shift(last[:, :cut], 1)
    toward_left = shift(last[:, cut:], -1)
    far = block(2 * (NZ // 2 - 1))
    toward_right = jnp.concatenate([add(toward_right, far[:, :cut]), far[:, cut:]], axis=1)
    far = block(2 * (NZ // 2 - 1) - 1)
    toward_left = jnp.concatenate([far[:, :cut], add(toward_left, far[:, cut:])], axis=1)
    for step in range(NZ // 2 - 1, 0, -1):
        toward_right = shift(toward_right, 1)
        toward_left = shift(toward_left, -1)
        if step > 1:
            toward_right = add(toward_right, block(2 * (step - 1)))
            toward_left = add(toward_left, block(2 * (step - 1) - 1))
    total = (
        block(0).astype(F32) + toward_right.astype(F32) + toward_left.astype(F32)
    )
    layer_out = total[:, :feat].astype(BF)
    token_grad = total[:, cut:].astype(BF)
    pair = total[:, feat : feat + half] + total[:, feat + half : cut]
    route_grad = jnp.sum(jnp.where(hot, pair[:, None, :], 0.0), 2)
    summed = summed.astype(F32)
    gate_grad = summed[:, :hid][None]
    up_grad = summed[:, hid : 2 * hid][None]
    down_grad = summed[:, 2 * hid :].T[None]
    return layer_out, token_grad, route_grad, gate_grad, up_grad, down_grad


def solution(mesh):
    grid = Mesh(mesh.devices.reshape(-1, 2, NX, NZ), ("y", "c", "x", "z"))
    dp, ex = ("y", "c"), ("x", "z")
    rowwise = P(dp + ex, None)
    return jax.shard_map(
        shards,
        mesh=grid,
        in_specs=(rowwise, rowwise, rowwise, rowwise, P(ex, dp, None), P(ex, dp, None), P(ex, None, dp)),
        out_specs=(rowwise, rowwise, rowwise, P(ex, dp, None), P(ex, dp, None), P(ex, None, dp)),
        check_vma=False,
    )
```

time: 554 us -> 273 us (0.49)
  waiting for transfers between devices: 225 us -> 70 us
  blocking collectives: 146 us -> 0 us
  starting transfers between devices: 46.4 us -> 122 us
  matrix products: 34.6 us -> 0 us
  local copies, waits for them, and re-layouts: 60.7 us -> 26.4 us
  Pallas kernels: 0 us -> 22.4 us
  other arithmetic: 24.7 us -> 15.9 us
    all_to_all x4 -> x0, waiting for transfers between devices: 140 us -> none  [the longest x1 90.4 us: shards(): lax.all_to_all(dy_send, 'expert', split_axis=0, concat_axis=0, tiled=True)]
    ppermute x0 -> x32, starting transfers between devices: none -> 122 us  [shift(): return lax.ppermute(value, 'z', [(i, (i + step) % NZ) for i in range(NZ)])]
    all_to_all x1 -> x0, blocking collectives: 104 us -> none  [shards(): lax.all_to_all(spread(dx_rows, back_rows, live_back, owners, slot_cap), '...]
    psum x1 -> x0, waiting for transfers between devices: 84.9 us -> none  [shards(): summed = lax.psum(grad_total.astype(jnp.bfloat16), 'dp').astype(jnp.float32)]
    ppermute x0 -> x32, waiting for transfers between devices: none -> 66 us  [shift(): return lax.ppermute(value, 'z', [(i, (i + step) % NZ) for i in range(NZ)])]
    all_to_all x4 -> x0, starting transfers between devices: 46.1 us -> none  [the longest x1 18.8 us: shards(): lax.all_to_all(send_counts, 'expert', split_axis=0, concat_axis=0, tiled=...]
    all_gather x3 -> x0, blocking collectives: 41.4 us -> none  [the longest x1 14.1 us: shards(): lax.all_gather(down_weight, 'dp', axis=2, tiled=True)]
    dot_general x33 -> x0, matrix products: 34.6 us -> none  [the longest x5 10 us: forward_block(): gate_act = jnp.dot(x_blk, gate_full, preferred_element_type=jnp.float32)]
  transfers between devices with their start and end apart: 5 -> 34, of which waited for: 4 -> 26; matrix products, arithmetic and copies ran while one was open for 7% -> 8% of each run, Pallas kernels for 0% -> 0%
where the time goes in v1:
time: 273 us; the launch traced here: 271 us
  starting transfers between devices  122 us (45%)
  waiting for transfers between devices  70 us (26%)
  local copies, waits for them, and re-layouts  26.4 us (10%)
  Pallas kernels  22.4 us (8%)
  other arithmetic  15.9 us (6%)
  between operations  14.6 us (5%)
    ppermute x32, starting transfers between devices, shift(): return lax.ppermute(value, 'z', [(i, (i + step) % NZ) for i in range(NZ)])  122 us
    ppermute x32, waiting for transfers between devices, shift(): return lax.ppermute(value, 'z', [(i, (i + step) % NZ) for i in range(NZ)])  66 us
    pallas_call x1, Pallas kernels, experts(): pl.pallas_call(moe_kernel, grid_spec=pltpu.PrefetchScalarGridSpec(num_sca...  22.4 us
    all_gather x1, local copies, waits for them, and re-layouts, shards(): wa = lax.all_gather(wl, ('y', 'c', 'x'), axis=0, tiled=True)  12.8 us
    convert_element_type x8, other arithmetic, add(): return (a.astype(F32) + b.astype(F32)).astype(BF)  9.03 us
    unnamed x22, local copies, waits for them, and re-layouts  6.65 us
  transfers between devices with their start and end apart: 34, of which 26 were waited for; matrix products, arithmetic and copies ran while one was open for 8% of the time, Pallas kernels for 0%

profile of v1, /device:TPU:6, one launch (start us, length us, event | category | flops | bytes accessed | tf_op | source)
XLA Modules:
  0.0 271.1 jit_solution(8354580142969025376)
XLA Ops:
  13.8 11.4 %collective-permute-start.1 = (bf16[64,2176]{1,0:T(8,128)(2,1)S(1)}, bf16[64,2176]{1,0:T(8,128)(2,1)S(1)}, u32[]{:S(2)}, u32[]{:S(2)}) collective-permute-start(bf16[64,2176]{1,0:T(8,128)(2,1)S(1)} %concatenate.18), channel_id=1, source_target_pairs={{0,15},{1,0},{2,1},{3,2},{4,3},{5,4},{6,5},{7,6},{8,7},{9,8},{10,9... | collective-permute-start | bytes 835592 | tf_op jit(solution)/shard_map/ppermute | solution.py:104
  27.2 3.9 %collective-permute-done.1 = bf16[64,2176]{1,0:T(8,128)(2,1)S(1)} collective-permute-done((bf16[64,2176]{1,0:T(8,128)(2,1)S(1)}, bf16[64,2176]{1,0:T(8,128)(2,1)S(1)}, u32[]{:S(2)}, u32[]{:S(2)}) %collective-permute-start.1) | collective-permute-done | bytes 278560 | tf_op jit(solution)/shard_map/ppermute | solution.py:104
  31.1 5.6 %collective-permute-start.3 = (bf16[64,2176]{1,0:T(8,128)(2,1)S(1)}, bf16[64,2176]{1,0:T(8,128)(2,1)S(1)}, u32[]{:S(2)}, u32[]{:S(2)}) collective-permute-start(bf16[64,2176]{1,0:T(8,128)(2,1)S(1)} %collective-permute-done.1), channel_id=1, source_target_pairs={{0,15},{1,0},{2,1},{3,2},{4,3},{5,4},{6,5},{7,6},{8,7},{9,8},{10,9... | collective-permute-start | bytes 835592 | tf_op jit(solution)/shard_map/ppermute | solution.py:104
  41.7 5.6 %collective-permute-start.5 = (bf16[64,2176]{1,0:T(8,128)(2,1)S(1)}, bf16[64,2176]{1,0:T(8,128)(2,1)S(1)}, u32[]{:S(2)}, u32[]{:S(2)}) collective-permute-start(bf16[64,2176]{1,0:T(8,128)(2,1)S(1)} %collective-permute-done.3), channel_id=1, source_target_pairs={{0,15},{1,0},{2,1},{3,2},{4,3},{5,4},{6,5},{7,6},{8,7},{9,8},{10,9... | collective-permute-start | bytes 835592 | tf_op jit(solution)/shard_map/ppermute | solution.py:104
  51.5 5.6 %collective-permute-start.7 = (bf16[64,2176]{1,0:T(8,128)(2,1)S(1)}, bf16[64,2176]{1,0:T(8,128)(2,1)S(1)}, u32[]{:S(2)}, u32[]{:S(2)}) collective-permute-start(bf16[64,2176]{1,0:T(8,128)(2,1)S(1)} %collective-permute-done.5), channel_id=1, source_target_pairs={{0,15},{1,0},{2,1},{3,2},{4,3},{5,4},{6,5},{7,6},{8,7},{9,8},{10,9... | collective-permute-start | bytes 835592 | tf_op jit(solution)/shard_map/ppermute | solution.py:104
  61.2 5.6 %collective-permute-start.9 = (bf16[64,2176]{1,0:T(8,128)(2,1)S(1)}, bf16[64,2176]{1,0:T(8,128)(2,1)S(1)}, u32[]{:S(2)}, u32[]{:S(2)}) collective-permute-start(bf16[64,2176]{1,0:T(8,128)(2,1)S(1)} %collective-permute-done.7), channel_id=1, source_target_pairs={{0,15},{1,0},{2,1},{3,2},{4,3},{5,4},{6,5},{7,6},{8,7},{9,8},{10,9... | collective-permute-start | bytes 835592 | tf_op jit(solution)/shard_map/ppermute | solution.py:104
  70.8 5.6 %collective-permute-start.11 = (bf16[64,2176]{1,0:T(8,128)(2,1)S(1)}, bf16[64,2176]{1,0:T(8,128)(2,1)S(1)}, u32[]{:S(2)}, u32[]{:S(2)}) collective-permute-start(bf16[64,2176]{1,0:T(8,128)(2,1)S(1)} %collective-permute-done.9), channel_id=1, source_target_pairs={{0,15},{1,0},{2,1},{3,2},{4,3},{5,4},{6,5},{7,6},{8,7},{9,8},{10,9... | collective-permute-start | bytes 835592 | tf_op jit(solution)/shard_map/ppermute | solution.py:104
  80.5 5.6 %collective-permute-start.13 = (bf16[64,2176]{1,0:T(8,128)(2,1)S(1)}, bf16[64,2176]{1,0:T(8,128)(2,1)S(1)}, u32[]{:S(2)}, u32[]{:S(2)}) collective-permute-start(bf16[64,2176]{1,0:T(8,128)(2,1)S(1)} %collective-permute-done.11), channel_id=1, source_target_pairs={{0,15},{1,0},{2,1},{3,2},{4,3},{5,4},{6,5},{7,6},{8,7},{9,8},{10,9... | collective-permute-start | bytes 835592 | tf_op jit(solution)/shard_map/ppermute | solution.py:104
  91.0 5.6 %collective-permute-start.15 = (bf16[64,1024]{1,0:T(8,128)(2,1)S(1)}, bf16[64,1024]{1,0:T(8,128)(2,1)S(1)}, u32[]{:S(2)}, u32[]{:S(2)}) collective-permute-start(bf16[64,1024]{1,0:T(8,128)(2,1)S(1)} %slice.140), channel_id=1, source_target_pairs={{0,15},{1,0},{2,1},{3,2},{4,3},{5,4},{6,5},{7,6},{8,7},{9,8},{10,9... | collective-permute-start | bytes 393224 | tf_op jit(solution)/shard_map/ppermute | solution.py:104
  99.1 5.8 %collective-permute-done.14 = bf16[64,1152]{1,0:T(8,128)(2,1)S(1)} collective-permute-done((bf16[64,1152]{1,0:T(8,128)(2,1)S(1)}, bf16[64,1152]{1,0:T(8,128)(2,1)S(1)}, u32[]{:S(2)}, u32[]{:S(2)}) %collective-permute-start.14) | collective-permute-done | bytes 147488 | tf_op jit(solution)/shard_map/ppermute | solution.py:104
  111.2 12.8 %copy.39 = bf16[4096,1152]{1,0:T(8,128)(2,1)} copy(bf16[4096,1152]{0,1:T(8,128)(2,1)} %all-gather.2.cloned.1.call-done) | data formatting | bytes 18874368 | tf_op jit(solution)/shard_map/all_gather | solution.py:117
  123.9 22.4 %shard_map.118 = (bf16[8,4,128,1152]{3,2,1,0:T(8,128)(2,1)}, bf16[1024,2176]{1,0:T(8,128)(2,1)}) custom-call(s32[1]{0:T(128)} %bitcast.col_ref, s32[4,1,1024]{2,1,0:T(1,128)} %copy.40.pos_ref, f32[4,1,1024]{2,1,0:T(1,128)} %copy.41.w_ref, bf16[1024,2176]{1,0:T(8,128)(2,1)} %copy-done, bf16[8,4,128,1152]{3,2,1,0:T(8,128)(2,1)} %bitcast.28), custom_call_target="tpu_custom_call" | custom-call | flops 10234101760 | bytes 30000000 | tf_op jit(solution)/shard_map/pallas_call | solution.py:73
  150.3 3.9 %collective-permute-start.16 = (bf16[64,1152]{1,0:T(8,128)(2,1)S(1)}, bf16[64,1152]{1,0:T(8,128)(2,1)S(1)}, u32[]{:S(2)}, u32[]{:S(2)}) collective-permute-start(bf16[64,1152]{1,0:T(8,128)(2,1)S(1)} %get-tuple-element.38), channel_id=1, source_target_pairs={{0,1},{1,2},{2,3},{3,4},{4,5},{5,6},{6,7},{7,8},{8,9},{9,10},{10,1... | collective-permute-start | bytes 442376 | tf_op jit(solution)/shard_map/ppermute | solution.py:104
  165.0 8.2 %collective-permute-done.17 = bf16[64,2176]{1,0:T(8,128)(2,1)S(1)} collective-permute-done((bf16[64,2176]{1,0:T(8,128)(2,1)S(1)}, bf16[64,2176]{1,0:T(8,128)(2,1)S(1)}, u32[]{:S(2)}, u32[]{:S(2)}) %collective-permute-start.17) | collective-permute-done | bytes 278560 | tf_op jit(solution)/shard_map/ppermute | solution.py:104
  176.4 5.1 %collective-permute-start.26 = (bf16[64,2176]{1,0:T(8,128)(2,1)S(1)}, bf16[64,2176]{1,0:T(8,128)(2,1)S(1)}, u32[]{:S(2)}, u32[]{:S(2)}) collective-permute-start(bf16[64,2176]{1,0:T(8,128)(2,1)S(1)} %get-tuple-element.37), channel_id=1, source_target_pairs={{0,15},{1,0},{2,1},{3,2},{4,3},{5,4},{6,5},{7,6},{8,7},{9,8},{10,9... | collective-permute-start | bytes 835592 | tf_op jit(solution)/shard_map/ppermute | solution.py:104
  181.5 4.9 %collective-permute-done.18 = bf16[64,2176]{1,0:T(8,128)(2,1)S(1)} collective-permute-done((bf16[64,2176]{1,0:T(8,128)(2,1)S(1)}, bf16[64,2176]{1,0:T(8,128)(2,1)S(1)}, u32[]{:S(2)}, u32[]{:S(2)}) %collective-permute-start.18) | collective-permute-done | bytes 278560 | tf_op jit(solution)/shard_map/ppermute | solution.py:104
  190.8 5.6 %collective-permute-start.27 = (bf16[64,2176]{1,0:T(8,128)(2,1)S(1)}, bf16[64,2176]{1,0:T(8,128)(2,1)S(1)}, u32[]{:S(2)}, u32[]{:S(2)}) collective-permute-start(bf16[64,2176]{1,0:T(8,128)(2,1)S(1)} %get-tuple-element.35), channel_id=1, source_target_pairs={{0,15},{1,0},{2,1},{3,2},{4,3},{5,4},{6,5},{7,6},{8,7},{9,8},{10,9... | collective-permute-start | bytes 835592 | tf_op jit(solution)/shard_map/ppermute | solution.py:104
  196.4 4.1 %collective-permute-done.19 = bf16[64,2176]{1,0:T(8,128)(2,1)S(1)} collective-permute-done((bf16[64,2176]{1,0:T(8,128)(2,1)S(1)}, bf16[64,2176]{1,0:T(8,128)(2,1)S(1)}, u32[]{:S(2)}, u32[]{:S(2)}) %collective-permute-start.19) | collective-permute-done | bytes 278560 | tf_op jit(solution)/shard_map/ppermute | solution.py:104
  204.7 5.6 %collective-permute-start.28 = (bf16[64,2176]{1,0:T(8,128)(2,1)S(1)}, bf16[64,2176]{1,0:T(8,128)(2,1)S(1)}, u32[]{:S(2)}, u32[]{:S(2)}) collective-permute-start(bf16[64,2176]{1,0:T(8,128)(2,1)S(1)} %get-tuple-element.33), channel_id=1, source_target_pairs={{0,15},{1,0},{2,1},{3,2},{4,3},{5,4},{6,5},{7,6},{8,7},{9,8},{10,9... | collective-permute-start | bytes 835592 | tf_op jit(solution)/shard_map/ppermute | solution.py:104
  217.8 5.6 %collective-permute-start.29 = (bf16[64,2176]{1,0:T(8,128)(2,1)S(1)}, bf16[64,2176]{1,0:T(8,128)(2,1)S(1)}, u32[]{:S(2)}, u32[]{:S(2)}) collective-permute-start(bf16[64,2176]{1,0:T(8,128)(2,1)S(1)} %get-tuple-element.31), channel_id=1, source_target_pairs={{0,15},{1,0},{2,1},{3,2},{4,3},{5,4},{6,5},{7,6},{8,7},{9,8},{10,9... | collective-permute-start | bytes 835592 | tf_op jit(solution)/shard_map/ppermute | solution.py:104
  228.7 4.4 %collective-permute-start.22 = (bf16[64,2176]{1,0:T(8,128)(2,1)S(1)}, bf16[64,2176]{1,0:T(8,128)(2,1)S(1)}, u32[]{:S(2)}, u32[]{:S(2)}) collective-permute-start(bf16[64,2176]{1,0:T(8,128)(2,1)S(1)} %get-tuple-element.28), channel_id=1, source_target_pairs={{0,1},{1,2},{2,3},{3,4},{4,5},{5,6},{6,7},{7,8},{8,9},{9,10},{10,1... | collective-permute-start | bytes 835592 | tf_op jit(solution)/shard_map/ppermute | solution.py:104
  242.7 3.7 %collective-permute-start.23 = (bf16[64,2176]{1,0:T(8,128)(2,1)S(1)}, bf16[64,2176]{1,0:T(8,128)(2,1)S(1)}, u32[]{:S(2)}, u32[]{:S(2)}) collective-permute-start(bf16[64,2176]{1,0:T(8,128)(2,1)S(1)} %get-tuple-element.26), channel_id=1, source_target_pairs={{0,1},{1,2},{2,3},{3,4},{4,5},{5,6},{6,7},{7,8},{8,9},{9,10},{10,1... | collective-permute-start | bytes 835592 | tf_op jit(solution)/shard_map/ppermute | solution.py:104
  246.5 3.3 %collective-permute-start.31 = (bf16[64,2176]{1,0:T(8,128)(2,1)S(1)}, bf16[64,2176]{1,0:T(8,128)(2,1)S(1)}, u32[]{:S(2)}, u32[]{:S(2)}) collective-permute-start(bf16[64,2176]{1,0:T(8,128)(2,1)S(1)} %get-tuple-element.27), channel_id=1, source_target_pairs={{0,15},{1,0},{2,1},{3,2},{4,3},{5,4},{6,5},{7,6},{8,7},{9,8},{10,9... | collective-permute-start | bytes 835592 | tf_op jit(solution)/shard_map/ppermute | solution.py:104
  257.7 4.0 %reduce-scatter.2.cloned.1.call-done = bf16[128,1152]{1,0:T(8,128)(2,1)} async-done(((bf16[4096,1152]{1,0:T(8,128)(2,1)}), bf16[128,1152]{1,0:T(8,128)(2,1)}) %reduce-scatter.2.cloned.1.call-update) | async-done | bytes 294928 | tf_op jit(solution)/shard_map/reduce_scatter | solution.py:140
  (109 shorter events, 102.6 us)
Async XLA Ops:
  7.2 104.0 %all-gather.2.cloned.1.call-start = ((), (), s32[]{:S(2)}) async-start(), calls=%async_computation.1 | async-start | bytes 9732096 | tf_op jit(solution)/shard_map/all_gather | solution.py:117
  10.9 250.7 %reduce-scatter.2.cloned.1.call-start = ((), (), s32[]{:S(2)}) async-start(), calls=%async_computation.2 | async-start | bytes 9732096 | tf_op jit(solution)/shard_map/reduce_scatter | solution.py:140
  13.8 17.3 %collective-permute-start.1 = (bf16[64,2176]{1,0:T(8,128)(2,1)S(1)}, bf16[64,2176]{1,0:T(8,128)(2,1)S(1)}, u32[]{:S(2)}, u32[]{:S(2)}) collective-permute-start(bf16[64,2176]{1,0:T(8,128)(2,1)S(1)} %concatenate.18), channel_id=1, source_target_pairs={{0,15},{1,0},{2,1},{3,2},{4,3},{5,4},{6,5},{7,6},{8,7},{9,8},{10,9... | collective-permute-start | bytes 835592 | tf_op jit(solution)/shard_map/ppermute | solution.py:104
  25.2 11.5 %collective-permute-start = (bf16[64,2176]{1,0:T(8,128)(2,1)S(1)}, bf16[64,2176]{1,0:T(8,128)(2,1)S(1)}, u32[]{:S(2)}, u32[]{:S(2)}) collective-permute-start(bf16[64,2176]{1,0:T(8,128)(2,1)S(1)} %concatenate.18), channel_id=1, source_target_pairs={{0,1},{1,2},{2,3},{3,4},{4,5},{5,6},{6,7},{7,8},{8,9},{9,10},{10,1... | collective-permute-start | bytes 835592 | tf_op jit(solution)/shard_map/ppermute | solution.py:104
  31.1 10.6 %collective-permute-start.3 = (bf16[64,2176]{1,0:T(8,128)(2,1)S(1)}, bf16[64,2176]{1,0:T(8,128)(2,1)S(1)}, u32[]{:S(2)}, u32[]{:S(2)}) collective-permute-start(bf16[64,2176]{1,0:T(8,128)(2,1)S(1)} %collective-permute-done.1), channel_id=1, source_target_pairs={{0,15},{1,0},{2,1},{3,2},{4,3},{5,4},{6,5},{7,6},{8,7},{9,8},{10,9... | collective-permute-start | bytes 835592 | tf_op jit(solution)/shard_map/ppermute | solution.py:104
  36.7 10.6 %collective-permute-start.2 = (bf16[64,2176]{1,0:T(8,128)(2,1)S(1)}, bf16[64,2176]{1,0:T(8,128)(2,1)S(1)}, u32[]{:S(2)}, u32[]{:S(2)}) collective-permute-start(bf16[64,2176]{1,0:T(8,128)(2,1)S(1)} %collective-permute-done), channel_id=1, source_target_pairs={{0,1},{1,2},{2,3},{3,4},{4,5},{5,6},{6,7},{7,8},{8,9},{9,10},{10,1... | collective-permute-start | bytes 835592 | tf_op jit(solution)/shard_map/ppermute | solution.py:104
  41.7 9.8 %collective-permute-start.5 = (bf16[64,2176]{1,0:T(8,128)(2,1)S(1)}, bf16[64,2176]{1,0:T(8,128)(2,1)S(1)}, u32[]{:S(2)}, u32[]{:S(2)}) collective-permute-start(bf16[64,2176]{1,0:T(8,128)(2,1)S(1)} %collective-permute-done.3), channel_id=1, source_target_pairs={{0,15},{1,0},{2,1},{3,2},{4,3},{5,4},{6,5},{7,6},{8,7},{9,8},{10,9... | collective-permute-start | bytes 835592 | tf_op jit(solution)/shard_map/ppermute | solution.py:104
  47.4 9.8 %collective-permute-start.4 = (bf16[64,2176]{1,0:T(8,128)(2,1)S(1)}, bf16[64,2176]{1,0:T(8,128)(2,1)S(1)}, u32[]{:S(2)}, u32[]{:S(2)}) collective-permute-start(bf16[64,2176]{1,0:T(8,128)(2,1)S(1)} %collective-permute-done.2), channel_id=1, source_target_pairs={{0,1},{1,2},{2,3},{3,4},{4,5},{5,6},{6,7},{7,8},{8,9},{9,10},{10,1... | collective-permute-start | bytes 835592 | tf_op jit(solution)/shard_map/ppermute | solution.py:104
  57.1 9.7 %collective-permute-start.6 = (bf16[64,2176]{1,0:T(8,128)(2,1)S(1)}, bf16[64,2176]{1,0:T(8,128)(2,1)S(1)}, u32[]{:S(2)}, u32[]{:S(2)}) collective-permute-start(bf16[64,2176]{1,0:T(8,128)(2,1)S(1)} %collective-permute-done.4), channel_id=1, source_target_pairs={{0,1},{1,2},{2,3},{3,4},{4,5},{5,6},{6,7},{7,8},{8,9},{9,10},{10,1... | collective-permute-start | bytes 835592 | tf_op jit(solution)/shard_map/ppermute | solution.py:104
  70.8 9.7 %collective-permute-start.11 = (bf16[64,2176]{1,0:T(8,128)(2,1)S(1)}, bf16[64,2176]{1,0:T(8,128)(2,1)S(1)}, u32[]{:S(2)}, u32[]{:S(2)}) collective-permute-start(bf16[64,2176]{1,0:T(8,128)(2,1)S(1)} %collective-permute-done.9), channel_id=1, source_target_pairs={{0,15},{1,0},{2,1},{3,2},{4,3},{5,4},{6,5},{7,6},{8,7},{9,8},{10,9... | collective-permute-start | bytes 835592 | tf_op jit(solution)/shard_map/ppermute | solution.py:104
  76.4 9.7 %collective-permute-start.10 = (bf16[64,2176]{1,0:T(8,128)(2,1)S(1)}, bf16[64,2176]{1,0:T(8,128)(2,1)S(1)}, u32[]{:S(2)}, u32[]{:S(2)}) collective-permute-start(bf16[64,2176]{1,0:T(8,128)(2,1)S(1)} %collective-permute-done.8), channel_id=1, source_target_pairs={{0,1},{1,2},{2,3},{3,4},{4,5},{5,6},{6,7},{7,8},{8,9},{9,10},{10,1... | collective-permute-start | bytes 835592 | tf_op jit(solution)/shard_map/ppermute | solution.py:104
  80.5 10.5 %collective-permute-start.13 = (bf16[64,2176]{1,0:T(8,128)(2,1)S(1)}, bf16[64,2176]{1,0:T(8,128)(2,1)S(1)}, u32[]{:S(2)}, u32[]{:S(2)}) collective-permute-start(bf16[64,2176]{1,0:T(8,128)(2,1)S(1)} %collective-permute-done.11), channel_id=1, source_target_pairs={{0,15},{1,0},{2,1},{3,2},{4,3},{5,4},{6,5},{7,6},{8,7},{9,8},{10,9... | collective-permute-start | bytes 835592 | tf_op jit(solution)/shard_map/ppermute | solution.py:104
  86.1 10.5 %collective-permute-start.12 = (bf16[64,2176]{1,0:T(8,128)(2,1)S(1)}, bf16[64,2176]{1,0:T(8,128)(2,1)S(1)}, u32[]{:S(2)}, u32[]{:S(2)}) collective-permute-start(bf16[64,2176]{1,0:T(8,128)(2,1)S(1)} %collective-permute-done.10), channel_id=1, source_target_pairs={{0,1},{1,2},{2,3},{3,4},{4,5},{5,6},{6,7},{7,8},{8,9},{9,10},{10,1... | collective-permute-start | bytes 835592 | tf_op jit(solution)/shard_map/ppermute | solution.py:104
  150.3 9.8 %collective-permute-start.16 = (bf16[64,1152]{1,0:T(8,128)(2,1)S(1)}, bf16[64,1152]{1,0:T(8,128)(2,1)S(1)}, u32[]{:S(2)}, u32[]{:S(2)}) collective-permute-start(bf16[64,1152]{1,0:T(8,128)(2,1)S(1)} %get-tuple-element.38), channel_id=1, source_target_pairs={{0,1},{1,2},{2,3},{3,4},{4,5},{5,6},{6,7},{7,8},{8,9},{9,10},{10,1... | collective-permute-start | bytes 442376 | tf_op jit(solution)/shard_map/ppermute | solution.py:104
  161.1 12.1 %collective-permute-start.17 = (bf16[64,2176]{1,0:T(8,128)(2,1)S(1)}, bf16[64,2176]{1,0:T(8,128)(2,1)S(1)}, u32[]{:S(2)}, u32[]{:S(2)}) collective-permute-start(bf16[64,2176]{1,0:T(8,128)(2,1)S(1)} %pad_maximum_fusion.1), channel_id=1, source_target_pairs={{0,1},{1,2},{2,3},{3,4},{4,5},{5,6},{6,7},{7,8},{8,9},{9,10},{10,1... | collective-permute-start | bytes 835592 | tf_op jit(solution)/shard_map/ppermute | solution.py:104
  174.5 12.0 %collective-permute-start.18 = (bf16[64,2176]{1,0:T(8,128)(2,1)S(1)}, bf16[64,2176]{1,0:T(8,128)(2,1)S(1)}, u32[]{:S(2)}, u32[]{:S(2)}) collective-permute-start(bf16[64,2176]{1,0:T(8,128)(2,1)S(1)} %get-tuple-element.36), channel_id=1, source_target_pairs={{0,1},{1,2},{2,3},{3,4},{4,5},{5,6},{6,7},{7,8},{8,9},{9,10},{10,1... | collective-permute-start | bytes 835592 | tf_op jit(solution)/shard_map/ppermute | solution.py:104
  176.4 11.2 %collective-permute-start.26 = (bf16[64,2176]{1,0:T(8,128)(2,1)S(1)}, bf16[64,2176]{1,0:T(8,128)(2,1)S(1)}, u32[]{:S(2)}, u32[]{:S(2)}) collective-permute-start(bf16[64,2176]{1,0:T(8,128)(2,1)S(1)} %get-tuple-element.37), channel_id=1, source_target_pairs={{0,15},{1,0},{2,1},{3,2},{4,3},{5,4},{6,5},{7,6},{8,7},{9,8},{10,9... | collective-permute-start | bytes 835592 | tf_op jit(solution)/shard_map/ppermute | solution.py:104
  188.8 11.6 %collective-permute-start.19 = (bf16[64,2176]{1,0:T(8,128)(2,1)S(1)}, bf16[64,2176]{1,0:T(8,128)(2,1)S(1)}, u32[]{:S(2)}, u32[]{:S(2)}) collective-permute-start(bf16[64,2176]{1,0:T(8,128)(2,1)S(1)} %get-tuple-element.34), channel_id=1, source_target_pairs={{0,1},{1,2},{2,3},{3,4},{4,5},{5,6},{6,7},{7,8},{8,9},{9,10},{10,1... | collective-permute-start | bytes 835592 | tf_op jit(solution)/shard_map/ppermute | solution.py:104
  190.8 10.9 %collective-permute-start.27 = (bf16[64,2176]{1,0:T(8,128)(2,1)S(1)}, bf16[64,2176]{1,0:T(8,128)(2,1)S(1)}, u32[]{:S(2)}, u32[]{:S(2)}) collective-permute-start(bf16[64,2176]{1,0:T(8,128)(2,1)S(1)} %get-tuple-element.35), channel_id=1, source_target_pairs={{0,15},{1,0},{2,1},{3,2},{4,3},{5,4},{6,5},{7,6},{8,7},{9,8},{10,9... | collective-permute-start | bytes 835592 | tf_op jit(solution)/shard_map/ppermute | solution.py:104
  202.8 10.7 %collective-permute-start.20 = (bf16[64,2176]{1,0:T(8,128)(2,1)S(1)}, bf16[64,2176]{1,0:T(8,128)(2,1)S(1)}, u32[]{:S(2)}, u32[]{:S(2)}) collective-permute-start(bf16[64,2176]{1,0:T(8,128)(2,1)S(1)} %get-tuple-element.32), channel_id=1, source_target_pairs={{0,1},{1,2},{2,3},{3,4},{4,5},{5,6},{6,7},{7,8},{8,9},{9,10},{10,1... | collective-permute-start | bytes 835592 | tf_op jit(solution)/shard_map/ppermute | solution.py:104
  204.7 10.0 %collective-permute-start.28 = (bf16[64,2176]{1,0:T(8,128)(2,1)S(1)}, bf16[64,2176]{1,0:T(8,128)(2,1)S(1)}, u32[]{:S(2)}, u32[]{:S(2)}) collective-permute-start(bf16[64,2176]{1,0:T(8,128)(2,1)S(1)} %get-tuple-element.33), channel_id=1, source_target_pairs={{0,15},{1,0},{2,1},{3,2},{4,3},{5,4},{6,5},{7,6},{8,7},{9,8},{10,9... | collective-permute-start | bytes 835592 | tf_op jit(solution)/shard_map/ppermute | solution.py:104
  215.9 10.1 %collective-permute-start.21 = (bf16[64,2176]{1,0:T(8,128)(2,1)S(1)}, bf16[64,2176]{1,0:T(8,128)(2,1)S(1)}, u32[]{:S(2)}, u32[]{:S(2)}) collective-permute-start(bf16[64,2176]{1,0:T(8,128)(2,1)S(1)} %get-tuple-element.30), channel_id=1, source_target_pairs={{0,1},{1,2},{2,3},{3,4},{4,5},{5,6},{6,7},{7,8},{8,9},{9,10},{10,1... | collective-permute-start | bytes 835592 | tf_op jit(solution)/shard_map/ppermute | solution.py:104
  228.7 10.1 %collective-permute-start.22 = (bf16[64,2176]{1,0:T(8,128)(2,1)S(1)}, bf16[64,2176]{1,0:T(8,128)(2,1)S(1)}, u32[]{:S(2)}, u32[]{:S(2)}) collective-permute-start(bf16[64,2176]{1,0:T(8,128)(2,1)S(1)} %get-tuple-element.28), channel_id=1, source_target_pairs={{0,1},{1,2},{2,3},{3,4},{4,5},{5,6},{6,7},{7,8},{8,9},{9,10},{10,1... | collective-permute-start | bytes 835592 | tf_op jit(solution)/shard_map/ppermute | solution.py:104
  242.7 9.7 %collective-permute-start.23 = (bf16[64,2176]{1,0:T(8,128)(2,1)S(1)}, bf16[64,2176]{1,0:T(8,128)(2,1)S(1)}, u32[]{:S(2)}, u32[]{:S(2)}) collective-permute-start(bf16[64,2176]{1,0:T(8,128)(2,1)S(1)} %get-tuple-element.26), channel_id=1, source_target_pairs={{0,1},{1,2},{2,3},{3,4},{4,5},{5,6},{6,7},{7,8},{8,9},{9,10},{10,1... | collective-permute-start | bytes 835592 | tf_op jit(solution)/shard_map/ppermute | solution.py:104
  (11 other events, 90.6 us)
Sparse Core Ops, SparseCore 0:
  11.0 80.3 all-gather.1
  146.5 115.0 reduce-scatter.1

commit v2 on v1

v2 whole, which is shorter than its diff:
```python
import jax
import jax.numpy as jnp
from jax import lax
from jax.experimental import pallas as pl
from jax.experimental.pallas import tpu as pltpu
from jax.sharding import Mesh
from jax.sharding import PartitionSpec as P

BF = jnp.bfloat16
F32 = jnp.float32
NX, NY, NZ, NC = 4, 4, 16, 2
NDP = NY * NC
HOPS = NZ // 2
CAP = 10
SLOTS = NZ * CAP
AUX = 128
PLANES = 8


def dot(a, b, ca, cb):
    return lax.dot_general(a, b, (((ca,), (cb,)), ((), ())), preferred_element_type=F32)


def moe_kernel(ids_ref, xa_ref, xb_ref, wt_ref, keep_ref, send_ref, pa_ref, pb_ref, pos_s, w_s, sel_s, rows_s):
    e = pl.program_id(0)
    col = ids_ref[0]
    core = ids_ref[1]
    tok = xa_ref.shape[0]
    feat = xb_ref.shape[1]
    hid = wt_ref.shape[3] // 3

    @pl.when(e == 0)
    def _():
        row = lax.broadcasted_iota(jnp.int32, (PLANES, AUX), 0)
        lane = lax.broadcasted_iota(jnp.int32, (PLANES, AUX), 1)
        want = (row < NX) & ((lane == col + row) | (lane == col + row + AUX // 2))
        w = dot(jnp.where(want, 1.0, 0.0).astype(BF), xa_ref[:, feat:], 1, 1)
        w_s[...] = w
        live = jnp.where(w > 0.0, 1.0, 0.0)
        r = lax.broadcasted_iota(jnp.int32, (128, 128), 0)
        c = lax.broadcasted_iota(jnp.int32, (128, 128), 1)
        upper = jnp.where(r <= c, 1.0, 0.0).astype(BF)
        before = jnp.full((PLANES, 1), -1.0, F32)
        for lo in range(0, tok, 128):
            part = live[:, lo : lo + 128]
            rank = dot(part.astype(BF), upper, 1, 0) + before
            pos_s[:, lo : lo + 128] = jnp.where(part > 0.0, rank, -1.0).astype(jnp.int32)
            before = before + jnp.sum(part, axis=1, keepdims=True)

    picked = pos_s[pl.ds(e, 1), :] == lax.broadcasted_iota(jnp.int32, (SLOTS, tok), 0)
    sel = jnp.where(picked, 1.0, 0.0).astype(BF)
    w = jnp.sum(jnp.where(picked, w_s[pl.ds(e, 1), :], 0.0), axis=1, keepdims=True)
    xe = dot(sel, xa_ref[:, :feat], 1, 0).astype(BF)
    de = dot(sel, xb_ref[...], 1, 0).astype(BF)
    wt = wt_ref[:, 0].reshape(feat, 3 * hid)
    gu = dot(xe, wt[:, : 2 * hid], 1, 0)
    hd = dot(de, wt[:, 2 * hid :], 1, 0)
    g = gu[:, :hid]
    u = gu[:, hid:]
    s = jax.nn.sigmoid(g)
    gs = g * s
    h = gs * u
    rg = jnp.sum(h * hd, axis=1, keepdims=True)
    wh = (w * h).astype(BF)
    hg = w * hd
    gb = (hg * u * s * (1.0 + g * (1.0 - s))).astype(BF)
    ub = (hg * gs).astype(BF)
    act = jnp.concatenate([gb, ub], axis=1)
    here = pl.ds(pl.multiple_of(e * SLOTS, SLOTS), SLOTS)
    sel_s[here, :] = sel
    rows_s[here, :feat] = dot(wh, wt[:, 2 * hid :], 1, 1).astype(BF)
    lane = lax.broadcasted_iota(jnp.int32, (SLOTS, AUX), 1)
    mine = col + e
    rg_hi = rg.astype(BF).astype(F32)
    aux = jnp.where(lane == mine, rg_hi, 0.0) + jnp.where(lane == mine + AUX // 2, rg - rg_hi, 0.0)
    rows_s[here, feat : feat + AUX] = aux.astype(BF)
    rows_s[here, feat + AUX :] = dot(act, wt[:, : 2 * hid], 1, 1).astype(BF)
    step = feat // NDP

    def halves(v):
        even = jnp.concatenate([v[:, i * step : (i + 1) * step] for i in range(0, NDP, 2)], axis=1)
        odd = jnp.concatenate([v[:, i * step : (i + 1) * step] for i in range(1, NDP, 2)], axis=1)
        return jnp.where(core == 0, even, odd), jnp.where(core == 0, odd, even)

    xk, xs = halves(xe)
    dk, ds = halves(de)
    keep_ref[:, 0, :, : 2 * hid] = dot(xk, act, 0, 0).astype(BF).reshape(NY, step, 2 * hid)
    keep_ref[:, 0, :, 2 * hid :] = dot(dk, wh, 0, 0).astype(BF).reshape(NY, step, hid)
    send_ref[:, 0, :, : 2 * hid] = dot(xs, act, 0, 0).astype(BF).reshape(NY, step, 2 * hid)
    send_ref[:, 0, :, 2 * hid :] = dot(ds, wh, 0, 0).astype(BF).reshape(NY, step, hid)

    @pl.when(e == NX - 1)
    def _():
        for lo in range(0, feat + AUX, 384):
            pa_ref[:, lo : lo + 384] = dot(sel_s[...], rows_s[:, lo : lo + 384], 0, 0).astype(BF)
        for lo in range(0, feat, 512):
            off = feat + AUX + lo
            pb_ref[:, lo : lo + 512] = dot(sel_s[...], rows_s[:, off : off + 512], 0, 0).astype(BF)


def experts(ids, xa, xb, wt):
    tok, feat = xb.shape
    hid3 = wt.shape[3]
    rows = feat // NDP
    slots = NX * SLOTS
    width = 2 * feat + AUX
    flops = 2 * slots * (tok * width * 2 + 9 * feat * hid3 // 3)
    whole = lambda e, s: (0, 0)
    return pl.pallas_call(
        moe_kernel,
        grid_spec=pltpu.PrefetchScalarGridSpec(
            num_scalar_prefetch=1,
            grid=(NX,),
            in_specs=[
                pl.BlockSpec((tok, feat + AUX), whole),
                pl.BlockSpec((tok, feat), whole),
                pl.BlockSpec((NDP, 1, rows, hid3), lambda e, s: (0, e, 0, 0)),
            ],
            out_specs=[
                pl.BlockSpec((NY, 1, rows, hid3), lambda e, s: (0, e, 0, 0)),
                pl.BlockSpec((NY, 1, rows, hid3), lambda e, s: (0, e, 0, 0)),
                pl.BlockSpec((tok, feat + AUX), whole),
                pl.BlockSpec((tok, feat), whole),
            ],
            scratch_shapes=[
                pltpu.VMEM((PLANES, tok), jnp.int32),
                pltpu.VMEM((PLANES, tok), F32),
                pltpu.VMEM((slots, tok), BF),
                pltpu.VMEM((slots, width), BF),
            ],
        ),
        out_shape=[
            jax.ShapeDtypeStruct((NY, NX, rows, hid3), BF),
            jax.ShapeDtypeStruct((NY, NX, rows, hid3), BF),
            jax.ShapeDtypeStruct((tok, feat + AUX), BF),
            jax.ShapeDtypeStruct((tok, feat), BF),
        ],
        cost_estimate=pl.CostEstimate(
            flops=flops, bytes_accessed=30_000_000, transcendentals=slots * hid3 // 3
        ),
    )(ids, xa, xb, wt)


def pack_kernel(g_ref, u_ref, d_ref, o_ref):
    hid = g_ref.shape[2]
    o_ref[:, :hid] = g_ref[0]
    o_ref[:, hid : 2 * hid] = u_ref[0]
    o_ref[:, 2 * hid :] = d_ref[0].astype(F32).T.astype(BF)


def pack(g, u, d):
    return pl.pallas_call(
        pack_kernel, out_shape=jax.ShapeDtypeStruct((g.shape[1], 3 * g.shape[2]), BF)
    )(g, u, d)


def unpack_kernel(s_ref, g_ref, u_ref, d_ref):
    hid = g_ref.shape[2]
    g_ref[0] = s_ref[:, :hid].astype(F32)
    u_ref[0] = s_ref[:, hid : 2 * hid].astype(F32)
    d_ref[0] = s_ref[:, 2 * hid :].astype(F32).T


def unpack(s):
    rows, hid = s.shape[0], s.shape[1] // 3
    return pl.pallas_call(
        unpack_kernel,
        out_shape=[
            jax.ShapeDtypeStruct((1, rows, hid), F32),
            jax.ShapeDtypeStruct((1, rows, hid), F32),
            jax.ShapeDtypeStruct((1, hid, rows), F32),
        ],
    )(s)


def around(value, sign):
    pairs = [(z, (z + sign) % NZ) for z in range(NZ)]
    pairs += [(NZ + z, NZ + (z - sign) % NZ) for z in range(NZ)]
    return lax.ppermute(value, ("c", "z"), pairs)


def swap(value):
    return lax.ppermute(value, "c", [(0, 1), (1, 0)])


def add(a, b):
    return (a.astype(F32) + b.astype(F32)).astype(BF)


def shards(tokens, expert_ids, route_weight, out_grad, gate_weight, up_weight, down_weight):
    rows, feat = tokens.shape
    hid = gate_weight.shape[2]
    z = lax.axis_index("z").astype(jnp.int32)
    core = lax.axis_index("c").astype(jnp.int32)
    half = AUX // 2
    pair_rows = 2 * rows
    wa = lax.all_gather(pack(gate_weight, up_weight, down_weight), ("y", "c", "x"), axis=0, tiled=True)
    place = (expert_ids % NZ) * NX + expert_ids // NZ
    hot = place[:, :, None] == jnp.arange(half, dtype=jnp.int32)
    dense = jnp.sum(jnp.where(hot, route_weight[:, :, None], 0.0), 1)
    hi = lax.reduce_precision(dense, 8, 7)
    own_a = jnp.concatenate([tokens, hi.astype(BF), (dense - hi).astype(BF)], axis=1)
    chain_a = chip_a = jnp.concatenate([own_a, swap(own_a)], axis=0)
    chain_b = chip_b = jnp.concatenate([out_grad, swap(out_grad)], axis=0)
    got_a, got_b = [], []
    for _ in range(HOPS):
        chain_a = around(chain_a, 1)
        chain_b = around(chain_b, 1)
        got_a.append(chain_a)
        got_b.append(chain_b)
    got_a[-1] = jnp.where(core == 0, got_a[-1], chip_a)
    got_b[-1] = jnp.where(core == 0, got_b[-1], chip_b)
    keep, send, pa, pb = experts(
        jnp.stack([z * NX, core]),
        jnp.concatenate(got_a, axis=0),
        jnp.concatenate(got_b, axis=0),
        wa.reshape(NDP, NX, feat // NDP, 3 * hid),
    )
    grads = add(keep, swap(send))
    summed = lax.psum_scatter(
        grads.reshape(-1, 3 * hid), ("y", "x"), scatter_dimension=0, tiled=True
    )

    def block(part, hop):
        return part[(hop - 1) * pair_rows : hop * pair_rows]

    none = jnp.zeros((), BF)
    chain_a = jnp.where(core == 0, block(pa, HOPS), none)
    chain_b = jnp.where(core == 0, block(pb, HOPS), none)
    for hop in range(HOPS, 0, -1):
        chain_a = around(chain_a, -1)
        chain_b = around(chain_b, -1)
        if hop > 1:
            chain_a = add(chain_a, block(pa, hop - 1))
            chain_b = add(chain_b, block(pb, hop - 1))
    chain_a = add(chain_a, jnp.where(core == 0, none, block(pa, HOPS)))
    chain_b = add(chain_b, jnp.where(core == 0, none, block(pb, HOPS)))
    total_a = chain_a[:rows].astype(F32) + swap(chain_a[rows:]).astype(F32)
    total_b = chain_b[:rows].astype(F32) + swap(chain_b[rows:]).astype(F32)
    layer_out = total_a[:, :feat].astype(BF)
    token_grad = total_b.astype(BF)
    pair = total_a[:, feat : feat + half] + total_a[:, feat + half :]
    route_grad = jnp.sum(jnp.where(hot, pair[:, None, :], 0.0), 2)
    return (layer_out, token_grad, route_grad, *unpack(summed))


def solution(mesh):
    grid = Mesh(mesh.devices.reshape(NY, NC, NX, NZ), ("y", "c", "x", "z"))
    dp, ex = ("y", "c"), ("x", "z")
    rowwise = P(dp + ex, None)
    weights = (P(ex, dp, None), P(ex, dp, None), P(ex, None, dp))
    return jax.shard_map(
        shards,
        mesh=grid,
        in_specs=(rowwise, rowwise, rowwise, rowwise, *weights),
        out_specs=(rowwise, rowwise, rowwise, *weights),
        check_vma=False,
    )
```

time: 273 us -> 249 us (0.912)
  local copies, waits for them, and re-layouts: 26.4 us -> 9.5 us
  starting transfers between devices: 122 us -> 107 us
  other arithmetic: 15.9 us -> 27.9 us
  waiting for transfers between devices: 70 us -> 61.1 us
  Pallas kernels: 22.4 us -> 26.1 us
    ppermute x32 -> x37, starting transfers between devices: 122 us -> 107 us  [the longest x32 97 us: around(): return lax.ppermute(value, ('c', 'z'), pairs)]
    convert_element_type x8 -> x17, other arithmetic: 9.03 us -> 22.5 us  [add(): return (a.astype(F32) + b.astype(F32)).astype(BF)]
    all_gather x1 -> x0, local copies, waits for them, and re-layouts: 12.8 us -> none  [shards(): wa = lax.all_gather(wl, ('y', 'c', 'x'), axis=0, tiled=True)]
    ppermute x32 -> x37, waiting for transfers between devices: 66 us -> 61 us  [the longest x32 52.3 us: around(): return lax.ppermute(value, ('c', 'z'), pairs)]
    reduce_scatter x1, waiting for transfers between devices: 3.95 us -> 0.01 us  [shards(): lax.psum_scatter(grads.reshape(-1, 3 * hid), ('y', 'x'), scatter_dimensio...]
    pallas_call x0 -> x2, Pallas kernels: none -> 3.61 us  [the longest x1 1.81 us: pack(): pl.pallas_call(pack_kernel, out_shape=jax.ShapeDtypeStruct((g.shape[1], 3...]
    unnamed x22 -> x19, local copies, waits for them, and re-layouts: 6.65 us -> 7.71 us
  transfers between devices with their start and end apart: 34 -> 39, of which waited for: 26 -> 22; matrix products, arithmetic and copies ran while one was open for 8% -> 13% of each run, Pallas kernels for 0% -> 0%
where the time goes in v2:
time: 249 us; the launch traced here: 246 us
  starting transfers between devices  107 us (43%)
  waiting for transfers between devices  61.1 us (25%)
  other arithmetic  27.9 us (11%)
  Pallas kernels  26.1 us (10%)
  between operations  14.7 us (6%)
  local copies, waits for them, and re-layouts  9.5 us (4%)
    ppermute x32, starting transfers between devices, around(): return lax.ppermute(value, ('c', 'z'), pairs)  97 us
    ppermute x32, waiting for transfers between devices, around(): return lax.ppermute(value, ('c', 'z'), pairs)  52.3 us
    convert_element_type x17, other arithmetic, add(): return (a.astype(F32) + b.astype(F32)).astype(BF)  22.5 us
    pallas_call x1, Pallas kernels, experts(): pl.pallas_call(moe_kernel, grid_spec=pltpu.PrefetchScalarGridSpec(num_sca...  22.4 us
    ppermute x5, starting transfers between devices, swap(): return lax.ppermute(value, 'c', [(0, 1), (1, 0)])  10.1 us
    ppermute x5, waiting for transfers between devices, swap(): return lax.ppermute(value, 'c', [(0, 1), (1, 0)])  8.73 us
    unnamed x19, local copies, waits for them, and re-layouts  7.71 us
  transfers between devices with their start and end apart: 39, of which 22 were waited for; matrix products, arithmetic and copies ran while one was open for 13% of the time, Pallas kernels for 0%

profile of v2, /device:TPU:6, one launch (start us, length us, event | category | flops | bytes accessed | tf_op | source)
XLA Modules:
  0.0 246.3 jit_solution(2977883053789468314)
XLA Ops:
  17.2 3.8 %collective-permute-start.10 = (bf16[128,1024]{1,0:T(8,128)(2,1)S(1)}, bf16[128,1024]{1,0:T(8,128)(2,1)S(1)}, u32[]{:S(2)}, u32[]{:S(2)}) collective-permute-start(bf16[128,1024]{1,0:T(8,128)(2,1)S(1)} %constant_dynamic-update-slice_fusion.7), channel_id=1, source_target_pairs={{0,1},{1,2},{2,3},{3,4},{4,5},{5,6},{6,7},{7,8},{8,9},{9,10},{10,1... | collective-permute-start | bytes 786440 | tf_op jit(solution)/shard_map/ppermute | solution.py:179
  21.1 3.8 %collective-permute-start.1 = (bf16[128,1152]{1,0:T(8,128)(2,1)S(1)}, bf16[128,1152]{1,0:T(8,128)(2,1)S(1)}, u32[]{:S(2)}, u32[]{:S(2)}) collective-permute-start(bf16[128,1152]{1,0:T(8,128)(2,1)S(1)} %pad_maximum_fusion), channel_id=1, source_target_pairs={{0,1},{1,2},{2,3},{3,4},{4,5},{5,6},{6,7},{7,8},{8,9},{9,10},{10,1... | collective-permute-start | bytes 884744 | tf_op jit(solution)/shard_map/ppermute | solution.py:179
  25.5 7.4 %collective-permute-done.10 = bf16[128,1024]{1,0:T(8,128)(2,1)S(1)} collective-permute-done((bf16[128,1024]{1,0:T(8,128)(2,1)S(1)}, bf16[128,1024]{1,0:T(8,128)(2,1)S(1)}, u32[]{:S(2)}, u32[]{:S(2)}) %collective-permute-start.10) | collective-permute-done | bytes 262176 | tf_op jit(solution)/shard_map/ppermute | solution.py:179
  38.7 3.7 %collective-permute-done.11 = bf16[128,1024]{1,0:T(8,128)(2,1)S(1)} collective-permute-done((bf16[128,1024]{1,0:T(8,128)(2,1)S(1)}, bf16[128,1024]{1,0:T(8,128)(2,1)S(1)}, u32[]{:S(2)}, u32[]{:S(2)}) %collective-permute-start.11) | collective-permute-done | bytes 262176 | tf_op jit(solution)/shard_map/ppermute | solution.py:179
  48.6 3.3 %collective-permute-done.12 = bf16[128,1024]{1,0:T(8,128)(2,1)S(1)} collective-permute-done((bf16[128,1024]{1,0:T(8,128)(2,1)S(1)}, bf16[128,1024]{1,0:T(8,128)(2,1)S(1)}, u32[]{:S(2)}, u32[]{:S(2)}) %collective-permute-start.12) | collective-permute-done | bytes 262176 | tf_op jit(solution)/shard_map/ppermute | solution.py:179
  91.7 3.3 %collective-permute-done.7 = bf16[128,1152]{1,0:T(8,128)(2,1)S(1)} collective-permute-done((bf16[128,1152]{1,0:T(8,128)(2,1)S(1)}, bf16[128,1152]{1,0:T(8,128)(2,1)S(1)}, u32[]{:S(2)}, u32[]{:S(2)}) %collective-permute-start.7) | collective-permute-done | bytes 294944 | tf_op jit(solution)/shard_map/ppermute | solution.py:179
  99.3 5.5 %collective-permute-done.8 = bf16[128,1152]{1,0:T(8,128)(2,1)S(1)} collective-permute-done((bf16[128,1152]{1,0:T(8,128)(2,1)S(1)}, bf16[128,1152]{1,0:T(8,128)(2,1)S(1)}, u32[]{:S(2)}, u32[]{:S(2)}) %collective-permute-start.8) | collective-permute-done | bytes 294944 | tf_op jit(solution)/shard_map/ppermute | solution.py:179
  105.6 22.4 %shard_map.119 = (bf16[4,4,128,1152]{3,2,1,0:T(8,128)(2,1)}, bf16[4,4,128,1152]{3,2,1,0:T(8,128)(2,1)}, bf16[1024,1152]{1,0:T(8,128)(2,1)}, bf16[1024,1024]{1,0:T(8,128)(2,1)}) custom-call(s32[2]{0:T(128)} %pad_add_fusion.ids_ref, bf16[1024,1152]{1,0:T(8,128)(2,1)} %select_dynamic-update-slice_fusion.xa_ref, bf16[1024,1024]{1,0:T(8,128)(2,1)} %copy-done, ...), custom_call_target="tpu_custom_call" | custom-call | flops 10234101760 | bytes 30000000 | tf_op jit(solution)/shard_map/pallas_call | solution.py:109
  130.0 8.1 %collective-permute-done.36 = bf16[4,4,128,1152]{3,2,1,0:T(8,128)(2,1)S(1)} collective-permute-done((bf16[4,4,128,1152]{3,2,1,0:T(8,128)(2,1)}, bf16[4,4,128,1152]{3,2,1,0:T(8,128)(2,1)S(1)}, u32[]{:S(2)}, u32[]{:S(2)}) %collective-permute-start.36) | collective-permute-done | bytes 4718624 | tf_op jit(solution)/shard_map/ppermute | solution.py:183
  138.1 6.0 %add_convert_fusion = bf16[4,4,128,1152]{3,2,1,0:T(8,128)(2,1)} fusion(bf16[4,4,128,1152]{3,2,1,0:T(8,128)(2,1)S(1)} %collective-permute-done.36, bf16[4,4,128,1152]{3,2,1,0:T(8,128)(2,1)} %get-tuple-element.15), kind=kLoop, calls=%fused_computation | loop fusion | flops 9437184 | bytes 14155776 | tf_op jit(solution)/shard_map/convert_element_type | solution.py:187
  149.9 3.4 %collective-permute-done.27 = bf16[128,1024]{1,0:T(8,128)(2,1)S(1)} collective-permute-done((bf16[128,1024]{1,0:T(8,128)(2,1)S(1)}, bf16[128,1024]{1,0:T(8,128)(2,1)S(1)}, u32[]{:S(2)}, u32[]{:S(2)}) %collective-permute-start.27) | collective-permute-done | bytes 262176 | tf_op jit(solution)/shard_map/ppermute | solution.py:179
  154.4 3.1 %collective-permute-start.28 = (bf16[128,1024]{1,0:T(8,128)(2,1)S(1)}, bf16[128,1024]{1,0:T(8,128)(2,1)S(1)}, u32[]{:S(2)}, u32[]{:S(2)}) collective-permute-start(bf16[128,1024]{1,0:T(8,128)(2,1)S(1)} %add_convert_fusion.16), channel_id=1, source_target_pairs={{0,15},{1,0},{2,1},{3,2},{4,3},{5,4},{6,5},{7,6},{8,7},{9,8},{10,9... | collective-permute-start | bytes 786440 | tf_op jit(solution)/shard_map/ppermute | solution.py:179
  158.6 3.7 %collective-permute-start.19 = (bf16[128,1152]{1,0:T(8,128)(2,1)S(1)}, bf16[128,1152]{1,0:T(8,128)(2,1)S(1)}, u32[]{:S(2)}, u32[]{:S(2)}) collective-permute-start(bf16[128,1152]{1,0:T(8,128)(2,1)S(1)} %add_convert_fusion.8), channel_id=1, source_target_pairs={{0,15},{1,0},{2,1},{3,2},{4,3},{5,4},{6,5},{7,6},{8,7},{9,8},{10,9... | collective-permute-start | bytes 884744 | tf_op jit(solution)/shard_map/ppermute | solution.py:179
  163.7 4.3 %collective-permute-start.29 = (bf16[128,1024]{1,0:T(8,128)(2,1)S(1)}, bf16[128,1024]{1,0:T(8,128)(2,1)S(1)}, u32[]{:S(2)}, u32[]{:S(2)}) collective-permute-start(bf16[128,1024]{1,0:T(8,128)(2,1)S(1)} %add_convert_fusion.15), channel_id=1, source_target_pairs={{0,15},{1,0},{2,1},{3,2},{4,3},{5,4},{6,5},{7,6},{8,7},{9,8},{10,9... | collective-permute-start | bytes 786440 | tf_op jit(solution)/shard_map/ppermute | solution.py:179
  169.1 4.1 %collective-permute-start.20 = (bf16[128,1152]{1,0:T(8,128)(2,1)S(1)}, bf16[128,1152]{1,0:T(8,128)(2,1)S(1)}, u32[]{:S(2)}, u32[]{:S(2)}) collective-permute-start(bf16[128,1152]{1,0:T(8,128)(2,1)S(1)} %add_convert_fusion.7), channel_id=1, source_target_pairs={{0,15},{1,0},{2,1},{3,2},{4,3},{5,4},{6,5},{7,6},{8,7},{9,8},{10,9... | collective-permute-start | bytes 884744 | tf_op jit(solution)/shard_map/ppermute | solution.py:179
  174.2 4.3 %collective-permute-start.30 = (bf16[128,1024]{1,0:T(8,128)(2,1)S(1)}, bf16[128,1024]{1,0:T(8,128)(2,1)S(1)}, u32[]{:S(2)}, u32[]{:S(2)}) collective-permute-start(bf16[128,1024]{1,0:T(8,128)(2,1)S(1)} %add_convert_fusion.14), channel_id=1, source_target_pairs={{0,15},{1,0},{2,1},{3,2},{4,3},{5,4},{6,5},{7,6},{8,7},{9,8},{10,9... | collective-permute-start | bytes 786440 | tf_op jit(solution)/shard_map/ppermute | solution.py:179
  179.6 4.4 %collective-permute-start.21 = (bf16[128,1152]{1,0:T(8,128)(2,1)S(1)}, bf16[128,1152]{1,0:T(8,128)(2,1)S(1)}, u32[]{:S(2)}, u32[]{:S(2)}) collective-permute-start(bf16[128,1152]{1,0:T(8,128)(2,1)S(1)} %add_convert_fusion.6), channel_id=1, source_target_pairs={{0,15},{1,0},{2,1},{3,2},{4,3},{5,4},{6,5},{7,6},{8,7},{9,8},{10,9... | collective-permute-start | bytes 884744 | tf_op jit(solution)/shard_map/ppermute | solution.py:179
  185.0 4.0 %collective-permute-start.31 = (bf16[128,1024]{1,0:T(8,128)(2,1)S(1)}, bf16[128,1024]{1,0:T(8,128)(2,1)S(1)}, u32[]{:S(2)}, u32[]{:S(2)}) collective-permute-start(bf16[128,1024]{1,0:T(8,128)(2,1)S(1)} %add_convert_fusion.13), channel_id=1, source_target_pairs={{0,15},{1,0},{2,1},{3,2},{4,3},{5,4},{6,5},{7,6},{8,7},{9,8},{10,9... | collective-permute-start | bytes 786440 | tf_op jit(solution)/shard_map/ppermute | solution.py:179
  190.1 4.8 %collective-permute-start.22 = (bf16[128,1152]{1,0:T(8,128)(2,1)S(1)}, bf16[128,1152]{1,0:T(8,128)(2,1)S(1)}, u32[]{:S(2)}, u32[]{:S(2)}) collective-permute-start(bf16[128,1152]{1,0:T(8,128)(2,1)S(1)} %add_convert_fusion.5), channel_id=1, source_target_pairs={{0,15},{1,0},{2,1},{3,2},{4,3},{5,4},{6,5},{7,6},{8,7},{9,8},{10,9... | collective-permute-start | bytes 884744 | tf_op jit(solution)/shard_map/ppermute | solution.py:179
  195.9 3.6 %collective-permute-start.32 = (bf16[128,1024]{1,0:T(8,128)(2,1)S(1)}, bf16[128,1024]{1,0:T(8,128)(2,1)S(1)}, u32[]{:S(2)}, u32[]{:S(2)}) collective-permute-start(bf16[128,1024]{1,0:T(8,128)(2,1)S(1)} %add_convert_fusion.12), channel_id=1, source_target_pairs={{0,15},{1,0},{2,1},{3,2},{4,3},{5,4},{6,5},{7,6},{8,7},{9,8},{10,9... | collective-permute-start | bytes 786440 | tf_op jit(solution)/shard_map/ppermute | solution.py:179
  200.6 5.1 %collective-permute-start.23 = (bf16[128,1152]{1,0:T(8,128)(2,1)S(1)}, bf16[128,1152]{1,0:T(8,128)(2,1)S(1)}, u32[]{:S(2)}, u32[]{:S(2)}) collective-permute-start(bf16[128,1152]{1,0:T(8,128)(2,1)S(1)} %add_convert_fusion.4), channel_id=1, source_target_pairs={{0,15},{1,0},{2,1},{3,2},{4,3},{5,4},{6,5},{7,6},{8,7},{9,8},{10,9... | collective-permute-start | bytes 884744 | tf_op jit(solution)/shard_map/ppermute | solution.py:179
  206.8 3.3 %collective-permute-start.33 = (bf16[128,1024]{1,0:T(8,128)(2,1)S(1)}, bf16[128,1024]{1,0:T(8,128)(2,1)S(1)}, u32[]{:S(2)}, u32[]{:S(2)}) collective-permute-start(bf16[128,1024]{1,0:T(8,128)(2,1)S(1)} %add_convert_fusion.11), channel_id=1, source_target_pairs={{0,15},{1,0},{2,1},{3,2},{4,3},{5,4},{6,5},{7,6},{8,7},{9,8},{10,9... | collective-permute-start | bytes 786440 | tf_op jit(solution)/shard_map/ppermute | solution.py:179
  211.1 5.5 %collective-permute-start.24 = (bf16[128,1152]{1,0:T(8,128)(2,1)S(1)}, bf16[128,1152]{1,0:T(8,128)(2,1)S(1)}, u32[]{:S(2)}, u32[]{:S(2)}) collective-permute-start(bf16[128,1152]{1,0:T(8,128)(2,1)S(1)} %add_convert_fusion.3), channel_id=1, source_target_pairs={{0,15},{1,0},{2,1},{3,2},{4,3},{5,4},{6,5},{7,6},{8,7},{9,8},{10,9... | collective-permute-start | bytes 884744 | tf_op jit(solution)/shard_map/ppermute | solution.py:179
  221.8 5.6 %collective-permute-start.25 = (bf16[128,1152]{1,0:T(8,128)(2,1)S(1)}, bf16[128,1152]{1,0:T(8,128)(2,1)S(1)}, u32[]{:S(2)}, u32[]{:S(2)}) collective-permute-start(bf16[128,1152]{1,0:T(8,128)(2,1)S(1)} %add_convert_fusion.2), channel_id=1, source_target_pairs={{0,15},{1,0},{2,1},{3,2},{4,3},{5,4},{6,5},{7,6},{8,7},{9,8},{10,9... | collective-permute-start | bytes 884744 | tf_op jit(solution)/shard_map/ppermute | solution.py:179
  (114 shorter events, 105.0 us)
Async XLA Ops:
  7.2 98.5 %all-gather.2.cloned.1.call-start = ((), (), s32[]{:S(2)}) async-start(), calls=%async_computation.1 | async-start | bytes 9732096 | tf_op jit(solution)/shard_map/all_gather | solution.py:197
  9.0 228.7 %reduce-scatter.2.cloned.1.call-start = ((), (), s32[]{:S(2)}) async-start(), calls=%async_computation.2 | async-start | bytes 5013504 | tf_op jit(solution)/shard_map/reduce_scatter | solution.py:220
  17.2 15.7 %collective-permute-start.10 = (bf16[128,1024]{1,0:T(8,128)(2,1)S(1)}, bf16[128,1024]{1,0:T(8,128)(2,1)S(1)}, u32[]{:S(2)}, u32[]{:S(2)}) collective-permute-start(bf16[128,1024]{1,0:T(8,128)(2,1)S(1)} %constant_dynamic-update-slice_fusion.7), channel_id=1, source_target_pairs={{0,1},{1,2},{2,3},{3,4},{4,5},{5,6},{6,7},{7,8},{8,9},{9,10},{10,1... | collective-permute-start | bytes 786440 | tf_op jit(solution)/shard_map/ppermute | solution.py:179
  21.1 15.0 %collective-permute-start.1 = (bf16[128,1152]{1,0:T(8,128)(2,1)S(1)}, bf16[128,1152]{1,0:T(8,128)(2,1)S(1)}, u32[]{:S(2)}, u32[]{:S(2)}) collective-permute-start(bf16[128,1152]{1,0:T(8,128)(2,1)S(1)} %pad_maximum_fusion), channel_id=1, source_target_pairs={{0,1},{1,2},{2,3},{3,4},{4,5},{5,6},{6,7},{7,8},{8,9},{9,10},{10,1... | collective-permute-start | bytes 884744 | tf_op jit(solution)/shard_map/ppermute | solution.py:179
  32.9 9.5 %collective-permute-start.11 = (bf16[128,1024]{1,0:T(8,128)(2,1)S(1)}, bf16[128,1024]{1,0:T(8,128)(2,1)S(1)}, u32[]{:S(2)}, u32[]{:S(2)}) collective-permute-start(bf16[128,1024]{1,0:T(8,128)(2,1)S(1)} %collective-permute-done.10), channel_id=1, source_target_pairs={{0,1},{1,2},{2,3},{3,4},{4,5},{5,6},{6,7},{7,8},{8,9},{9,10},{10,1... | collective-permute-start | bytes 786440 | tf_op jit(solution)/shard_map/ppermute | solution.py:179
  36.1 9.8 %collective-permute-start.2 = (bf16[128,1152]{1,0:T(8,128)(2,1)S(1)}, bf16[128,1152]{1,0:T(8,128)(2,1)S(1)}, u32[]{:S(2)}, u32[]{:S(2)}) collective-permute-start(bf16[128,1152]{1,0:T(8,128)(2,1)S(1)} %collective-permute-done.1), channel_id=1, source_target_pairs={{0,1},{1,2},{2,3},{3,4},{4,5},{5,6},{6,7},{7,8},{8,9},{9,10},{10,1... | collective-permute-start | bytes 884744 | tf_op jit(solution)/shard_map/ppermute | solution.py:179
  42.4 9.5 %collective-permute-start.12 = (bf16[128,1024]{1,0:T(8,128)(2,1)S(1)}, bf16[128,1024]{1,0:T(8,128)(2,1)S(1)}, u32[]{:S(2)}, u32[]{:S(2)}) collective-permute-start(bf16[128,1024]{1,0:T(8,128)(2,1)S(1)} %collective-permute-done.11), channel_id=1, source_target_pairs={{0,1},{1,2},{2,3},{3,4},{4,5},{5,6},{6,7},{7,8},{8,9},{9,10},{10,1... | collective-permute-start | bytes 786440 | tf_op jit(solution)/shard_map/ppermute | solution.py:179
  45.9 9.8 %collective-permute-start.3 = (bf16[128,1152]{1,0:T(8,128)(2,1)S(1)}, bf16[128,1152]{1,0:T(8,128)(2,1)S(1)}, u32[]{:S(2)}, u32[]{:S(2)}) collective-permute-start(bf16[128,1152]{1,0:T(8,128)(2,1)S(1)} %collective-permute-done.2), channel_id=1, source_target_pairs={{0,1},{1,2},{2,3},{3,4},{4,5},{5,6},{6,7},{7,8},{8,9},{9,10},{10,1... | collective-permute-start | bytes 884744 | tf_op jit(solution)/shard_map/ppermute | solution.py:179
  55.7 9.8 %collective-permute-start.4 = (bf16[128,1152]{1,0:T(8,128)(2,1)S(1)}, bf16[128,1152]{1,0:T(8,128)(2,1)S(1)}, u32[]{:S(2)}, u32[]{:S(2)}) collective-permute-start(bf16[128,1152]{1,0:T(8,128)(2,1)S(1)} %collective-permute-done.3), channel_id=1, source_target_pairs={{0,1},{1,2},{2,3},{3,4},{4,5},{5,6},{6,7},{7,8},{8,9},{9,10},{10,1... | collective-permute-start | bytes 884744 | tf_op jit(solution)/shard_map/ppermute | solution.py:179
  65.5 9.8 %collective-permute-start.5 = (bf16[128,1152]{1,0:T(8,128)(2,1)S(1)}, bf16[128,1152]{1,0:T(8,128)(2,1)S(1)}, u32[]{:S(2)}, u32[]{:S(2)}) collective-permute-start(bf16[128,1152]{1,0:T(8,128)(2,1)S(1)} %collective-permute-done.4), channel_id=1, source_target_pairs={{0,1},{1,2},{2,3},{3,4},{4,5},{5,6},{6,7},{7,8},{8,9},{9,10},{10,1... | collective-permute-start | bytes 884744 | tf_op jit(solution)/shard_map/ppermute | solution.py:179
  75.4 9.8 %collective-permute-start.6 = (bf16[128,1152]{1,0:T(8,128)(2,1)S(1)}, bf16[128,1152]{1,0:T(8,128)(2,1)S(1)}, u32[]{:S(2)}, u32[]{:S(2)}) collective-permute-start(bf16[128,1152]{1,0:T(8,128)(2,1)S(1)} %collective-permute-done.5), channel_id=1, source_target_pairs={{0,1},{1,2},{2,3},{3,4},{4,5},{5,6},{6,7},{7,8},{8,9},{9,10},{10,1... | collective-permute-start | bytes 884744 | tf_op jit(solution)/shard_map/ppermute | solution.py:179
  85.2 9.8 %collective-permute-start.7 = (bf16[128,1152]{1,0:T(8,128)(2,1)S(1)}, bf16[128,1152]{1,0:T(8,128)(2,1)S(1)}, u32[]{:S(2)}, u32[]{:S(2)}) collective-permute-start(bf16[128,1152]{1,0:T(8,128)(2,1)S(1)} %collective-permute-done.6), channel_id=1, source_target_pairs={{0,1},{1,2},{2,3},{3,4},{4,5},{5,6},{6,7},{7,8},{8,9},{9,10},{10,1... | collective-permute-start | bytes 884744 | tf_op jit(solution)/shard_map/ppermute | solution.py:179
  95.0 9.8 %collective-permute-start.8 = (bf16[128,1152]{1,0:T(8,128)(2,1)S(1)}, bf16[128,1152]{1,0:T(8,128)(2,1)S(1)}, u32[]{:S(2)}, u32[]{:S(2)}) collective-permute-start(bf16[128,1152]{1,0:T(8,128)(2,1)S(1)} %collective-permute-done.7), channel_id=1, source_target_pairs={{0,1},{1,2},{2,3},{3,4},{4,5},{5,6},{6,7},{7,8},{8,9},{9,10},{10,1... | collective-permute-start | bytes 884744 | tf_op jit(solution)/shard_map/ppermute | solution.py:179
  128.1 10.0 %collective-permute-start.36 = (bf16[4,4,128,1152]{3,2,1,0:T(8,128)(2,1)}, bf16[4,4,128,1152]{3,2,1,0:T(8,128)(2,1)S(1)}, u32[]{:S(2)}, u32[]{:S(2)}) collective-permute-start(bf16[4,4,128,1152]{3,2,1,0:T(8,128)(2,1)} %get-tuple-element.16), channel_id=1, source_target_pairs={{0,64},{64,0},{1,65},{65,1},{2,66},{66,2},{3,67},{67,3},{4,68},{68... | collective-permute-start | bytes 14155784 | tf_op jit(solution)/shard_map/ppermute | solution.py:183
  148.0 9.5 %collective-permute-start.18 = (bf16[128,1152]{1,0:T(8,128)(2,1)S(1)}, bf16[128,1152]{1,0:T(8,128)(2,1)S(1)}, u32[]{:S(2)}, u32[]{:S(2)}) collective-permute-start(bf16[128,1152]{1,0:T(8,128)(2,1)S(1)} %broadcast_select_fusion), channel_id=1, source_target_pairs={{0,15},{1,0},{2,1},{3,2},{4,3},{5,4},{6,5},{7,6},{8,7},{9,8},{10,9... | collective-permute-start | bytes 884744 | tf_op jit(solution)/shard_map/ppermute | solution.py:179
  163.7 9.5 %collective-permute-start.29 = (bf16[128,1024]{1,0:T(8,128)(2,1)S(1)}, bf16[128,1024]{1,0:T(8,128)(2,1)S(1)}, u32[]{:S(2)}, u32[]{:S(2)}) collective-permute-start(bf16[128,1024]{1,0:T(8,128)(2,1)S(1)} %add_convert_fusion.15), channel_id=1, source_target_pairs={{0,15},{1,0},{2,1},{3,2},{4,3},{5,4},{6,5},{7,6},{8,7},{9,8},{10,9... | collective-permute-start | bytes 786440 | tf_op jit(solution)/shard_map/ppermute | solution.py:179
  174.2 9.8 %collective-permute-start.30 = (bf16[128,1024]{1,0:T(8,128)(2,1)S(1)}, bf16[128,1024]{1,0:T(8,128)(2,1)S(1)}, u32[]{:S(2)}, u32[]{:S(2)}) collective-permute-start(bf16[128,1024]{1,0:T(8,128)(2,1)S(1)} %add_convert_fusion.14), channel_id=1, source_target_pairs={{0,15},{1,0},{2,1},{3,2},{4,3},{5,4},{6,5},{7,6},{8,7},{9,8},{10,9... | collective-permute-start | bytes 786440 | tf_op jit(solution)/shard_map/ppermute | solution.py:179
  179.6 9.5 %collective-permute-start.21 = (bf16[128,1152]{1,0:T(8,128)(2,1)S(1)}, bf16[128,1152]{1,0:T(8,128)(2,1)S(1)}, u32[]{:S(2)}, u32[]{:S(2)}) collective-permute-start(bf16[128,1152]{1,0:T(8,128)(2,1)S(1)} %add_convert_fusion.6), channel_id=1, source_target_pairs={{0,15},{1,0},{2,1},{3,2},{4,3},{5,4},{6,5},{7,6},{8,7},{9,8},{10,9... | collective-permute-start | bytes 884744 | tf_op jit(solution)/shard_map/ppermute | solution.py:179
  185.0 9.8 %collective-permute-start.31 = (bf16[128,1024]{1,0:T(8,128)(2,1)S(1)}, bf16[128,1024]{1,0:T(8,128)(2,1)S(1)}, u32[]{:S(2)}, u32[]{:S(2)}) collective-permute-start(bf16[128,1024]{1,0:T(8,128)(2,1)S(1)} %add_convert_fusion.13), channel_id=1, source_target_pairs={{0,15},{1,0},{2,1},{3,2},{4,3},{5,4},{6,5},{7,6},{8,7},{9,8},{10,9... | collective-permute-start | bytes 786440 | tf_op jit(solution)/shard_map/ppermute | solution.py:179
  195.9 9.8 %collective-permute-start.32 = (bf16[128,1024]{1,0:T(8,128)(2,1)S(1)}, bf16[128,1024]{1,0:T(8,128)(2,1)S(1)}, u32[]{:S(2)}, u32[]{:S(2)}) collective-permute-start(bf16[128,1024]{1,0:T(8,128)(2,1)S(1)} %add_convert_fusion.12), channel_id=1, source_target_pairs={{0,15},{1,0},{2,1},{3,2},{4,3},{5,4},{6,5},{7,6},{8,7},{9,8},{10,9... | collective-permute-start | bytes 786440 | tf_op jit(solution)/shard_map/ppermute | solution.py:179
  206.8 9.8 %collective-permute-start.33 = (bf16[128,1024]{1,0:T(8,128)(2,1)S(1)}, bf16[128,1024]{1,0:T(8,128)(2,1)S(1)}, u32[]{:S(2)}, u32[]{:S(2)}) collective-permute-start(bf16[128,1024]{1,0:T(8,128)(2,1)S(1)} %add_convert_fusion.11), channel_id=1, source_target_pairs={{0,15},{1,0},{2,1},{3,2},{4,3},{5,4},{6,5},{7,6},{8,7},{9,8},{10,9... | collective-permute-start | bytes 786440 | tf_op jit(solution)/shard_map/ppermute | solution.py:179
  211.1 9.7 %collective-permute-start.24 = (bf16[128,1152]{1,0:T(8,128)(2,1)S(1)}, bf16[128,1152]{1,0:T(8,128)(2,1)S(1)}, u32[]{:S(2)}, u32[]{:S(2)}) collective-permute-start(bf16[128,1152]{1,0:T(8,128)(2,1)S(1)} %add_convert_fusion.3), channel_id=1, source_target_pairs={{0,15},{1,0},{2,1},{3,2},{4,3},{5,4},{6,5},{7,6},{8,7},{9,8},{10,9... | collective-permute-start | bytes 884744 | tf_op jit(solution)/shard_map/ppermute | solution.py:179
  217.6 9.8 %collective-permute-start.34 = (bf16[128,1024]{1,0:T(8,128)(2,1)S(1)}, bf16[128,1024]{1,0:T(8,128)(2,1)S(1)}, u32[]{:S(2)}, u32[]{:S(2)}) collective-permute-start(bf16[128,1024]{1,0:T(8,128)(2,1)S(1)} %add_convert_fusion.10), channel_id=1, source_target_pairs={{0,15},{1,0},{2,1},{3,2},{4,3},{5,4},{6,5},{7,6},{8,7},{9,8},{10,9... | collective-permute-start | bytes 786440 | tf_op jit(solution)/shard_map/ppermute | solution.py:179
  221.8 9.8 %collective-permute-start.25 = (bf16[128,1152]{1,0:T(8,128)(2,1)S(1)}, bf16[128,1152]{1,0:T(8,128)(2,1)S(1)}, u32[]{:S(2)}, u32[]{:S(2)}) collective-permute-start(bf16[128,1152]{1,0:T(8,128)(2,1)S(1)} %add_convert_fusion.2), channel_id=1, source_target_pairs={{0,15},{1,0},{2,1},{3,2},{4,3},{5,4},{6,5},{7,6},{8,7},{9,8},{10,9... | collective-permute-start | bytes 884744 | tf_op jit(solution)/shard_map/ppermute | solution.py:179
  (16 other events, 132.7 us)
Sparse Core Ops, SparseCore 0:
  11.1 74.9 all-gather.1
  144.2 92.5 reduce-scatter.1

commit v3 on v2

v3 whole, which is shorter than its diff:
```python
import jax
import jax.numpy as jnp
from jax import lax
from jax.experimental import pallas as pl
from jax.experimental.pallas import tpu as pltpu
from jax.sharding import Mesh
from jax.sharding import PartitionSpec as P

BF = jnp.bfloat16
F32 = jnp.float32
NX, NY, NZ, NC = 4, 4, 16, 2
NDP = NY * NC
HOPS = NZ // 2
ROOM = 32
AUX = 128
PLANES = 8
BLOCK = 128


def dot(a, b, ca, cb):
    return lax.dot_general(a, b, (((ca,), (cb,)), ((), ())), preferred_element_type=F32)


def flat(v):
    return v.reshape(v.shape[0] * v.shape[1], v.shape[2])


def moe_kernel(
    ids_ref, xa_ref, xb_ref, wt_ref, xe_ref, de_ref, act_ref, wh_ref, pa_ref, pb_ref, pos_s, w_s, sel_s, rows_s
):
    e = pl.program_id(0)
    col = ids_ref[0]
    feat = xb_ref.shape[1]
    hid = wt_ref.shape[3] // 3
    spans = [slice(b * BLOCK, (b + 1) * BLOCK) for b in range(HOPS)]
    slot = lax.broadcasted_iota(jnp.int32, (ROOM, BLOCK), 0)

    @pl.when(e == 0)
    def _():
        row = lax.broadcasted_iota(jnp.int32, (PLANES, AUX), 0)
        lane = lax.broadcasted_iota(jnp.int32, (PLANES, AUX), 1)
        want = (row < NX) & ((lane == col + row) | (lane == col + row + AUX // 2))
        w = dot(jnp.where(want, 1.0, 0.0).astype(BF), xa_ref[:, feat:], 1, 1)
        w_s[...] = w
        live = jnp.where(w > 0.0, 1.0, 0.0)
        r = lax.broadcasted_iota(jnp.int32, (BLOCK, BLOCK), 0)
        c = lax.broadcasted_iota(jnp.int32, (BLOCK, BLOCK), 1)
        upper = jnp.where(r <= c, 1.0, 0.0).astype(BF)
        for b, span in enumerate(spans):
            part = live[:, span]
            rank = dot(part.astype(BF), upper, 1, 0) - 1.0
            pos = jnp.where(part > 0.0, rank, -1.0).astype(jnp.int32)
            pos_s[:, span] = pos
            sel = jnp.concatenate(
                [jnp.where(pos[j : j + 1] == slot, 1.0, 0.0) for j in range(NX)], axis=0
            ).astype(BF)
            sel_s[b] = sel
            xe_ref[b] = dot(sel, xa_ref[span, :feat], 1, 0).astype(BF).reshape(NX, ROOM, feat)
            de_ref[b] = dot(sel, xb_ref[span, :], 1, 0).astype(BF).reshape(NX, ROOM, feat)

    xe = flat(xe_ref[:, e])
    de = flat(de_ref[:, e])
    pos = pos_s[pl.ds(e, 1), :]
    wrow = w_s[pl.ds(e, 1), :]
    w = jnp.concatenate(
        [
            jnp.sum(jnp.where(pos[:, span] == slot, wrow[:, span], 0.0), axis=1, keepdims=True)
            for span in spans
        ],
        axis=0,
    )
    wt = wt_ref[:, 0].reshape(feat, 3 * hid)
    gu = dot(xe, wt[:, : 2 * hid], 1, 0)
    hd = dot(de, wt[:, 2 * hid :], 1, 0)
    g = gu[:, :hid]
    u = gu[:, hid:]
    s = jax.nn.sigmoid(g)
    gs = g * s
    h = gs * u
    rg = jnp.sum(h * hd, axis=1, keepdims=True)
    wh = (w * h).astype(BF)
    hg = w * hd
    gb = (hg * u * s * (1.0 + g * (1.0 - s))).astype(BF)
    ub = (hg * gs).astype(BF)
    act = jnp.concatenate([gb, ub], axis=1)
    act_ref[:, e] = act.reshape(HOPS, ROOM, 2 * hid)
    wh_ref[:, e] = wh.reshape(HOPS, ROOM, hid)
    y = dot(wh, wt[:, 2 * hid :], 1, 1).astype(BF)
    rows_s[:, e, :, :feat] = y.reshape(HOPS, ROOM, feat)
    lane = lax.broadcasted_iota(jnp.int32, (HOPS * ROOM, AUX), 1)
    mine = col + e
    rg_hi = rg.astype(BF).astype(F32)
    aux = jnp.where(lane == mine, rg_hi, 0.0) + jnp.where(lane == mine + AUX // 2, rg - rg_hi, 0.0)
    rows_s[:, e, :, feat : feat + AUX] = aux.astype(BF).reshape(HOPS, ROOM, AUX)
    dx = dot(act, wt[:, : 2 * hid], 1, 1).astype(BF)
    rows_s[:, e, :, feat + AUX :] = dx.reshape(HOPS, ROOM, feat)

    @pl.when(e == NX - 1)
    def _():
        for b, span in enumerate(spans):
            rows = flat(rows_s[b])
            pa_ref[span, :] = dot(sel_s[b], rows[:, : feat + AUX], 0, 0).astype(BF)
            pb_ref[span, :] = dot(sel_s[b], rows[:, feat + AUX :], 0, 0).astype(BF)


def experts(ids, xa, xb, wt):
    tok, feat = xb.shape
    hid3 = wt.shape[3]
    hid = hid3 // 3
    rows = feat // NDP
    width = 2 * feat + AUX
    slots = HOPS * NX * ROOM
    flops = 2 * slots * (BLOCK * width * 2 + 6 * feat * hid)
    whole2 = lambda e, s: (0, 0)
    whole4 = lambda e, s: (0, 0, 0, 0)
    packed = lambda n: (HOPS, NX, ROOM, n)
    return pl.pallas_call(
        moe_kernel,
        grid_spec=pltpu.PrefetchScalarGridSpec(
            num_scalar_prefetch=1,
            grid=(NX,),
            in_specs=[
                pl.BlockSpec((tok, feat + AUX), whole2),
                pl.BlockSpec((tok, feat), whole2),
                pl.BlockSpec((NDP, 1, rows, hid3), lambda e, s: (0, e, 0, 0)),
            ],
            out_specs=[
                pl.BlockSpec(packed(feat), whole4),
                pl.BlockSpec(packed(feat), whole4),
                pl.BlockSpec(packed(2 * hid), whole4),
                pl.BlockSpec(packed(hid), whole4),
                pl.BlockSpec((tok, feat + AUX), whole2),
                pl.BlockSpec((tok, feat), whole2),
            ],
            scratch_shapes=[
                pltpu.VMEM((PLANES, tok), jnp.int32),
                pltpu.VMEM((PLANES, tok), F32),
                pltpu.VMEM((HOPS, NX * ROOM, BLOCK), BF),
                pltpu.VMEM(packed(width), BF),
            ],
        ),
        out_shape=[
            jax.ShapeDtypeStruct(packed(feat), BF),
            jax.ShapeDtypeStruct(packed(feat), BF),
            jax.ShapeDtypeStruct(packed(2 * hid), BF),
            jax.ShapeDtypeStruct(packed(hid), BF),
            jax.ShapeDtypeStruct((tok, feat + AUX), BF),
            jax.ShapeDtypeStruct((tok, feat), BF),
        ],
        cost_estimate=pl.CostEstimate(
            flops=flops, bytes_accessed=26_000_000, transcendentals=slots * hid
        ),
    )(ids, xa, xb, wt)


def grad_kernel(ids_ref, xe_ref, de_ref, act_ref, wh_ref, gu_ref, keep_ref, send_ref):
    core = ids_ref[1]
    xe = flat(xe_ref[:, 0])
    de = flat(de_ref[:, 0])
    act = flat(act_ref[:, 0])
    wh = flat(wh_ref[:, 0])
    step = gu_ref.shape[2]
    gu_ref[:, 0] = dot(xe, act, 0, 0).astype(BF).reshape(NDP, step, act.shape[1])
    even = jnp.concatenate([de[:, i * step : (i + 1) * step] for i in range(0, NDP, 2)], axis=1)
    odd = jnp.concatenate([de[:, i * step : (i + 1) * step] for i in range(1, NDP, 2)], axis=1)
    keep = dot(jnp.where(core == 0, even, odd), wh, 0, 0)
    send = dot(jnp.where(core == 0, odd, even), wh, 0, 0)
    keep_ref[:, 0] = keep.astype(BF).reshape(NY, step, wh.shape[1])
    send_ref[:, 0] = send.astype(BF).reshape(NY, step, wh.shape[1])


def weight_grads(ids, xe, de, act, wh):
    feat, hid = xe.shape[3], wh.shape[3]
    rows = feat // NDP
    one = lambda n: pl.BlockSpec((HOPS, 1, ROOM, n), lambda e, s: (0, e, 0, 0))
    out = lambda n, w: pl.BlockSpec((n, 1, rows, w), lambda e, s: (0, e, 0, 0))
    return pl.pallas_call(
        grad_kernel,
        grid_spec=pltpu.PrefetchScalarGridSpec(
            num_scalar_prefetch=1,
            grid=(NX,),
            in_specs=[one(feat), one(feat), one(2 * hid), one(hid)],
            out_specs=[out(NDP, 2 * hid), out(NY, hid), out(NY, hid)],
        ),
        out_shape=[
            jax.ShapeDtypeStruct((NDP, NX, rows, 2 * hid), BF),
            jax.ShapeDtypeStruct((NY, NX, rows, hid), BF),
            jax.ShapeDtypeStruct((NY, NX, rows, hid), BF),
        ],
        cost_estimate=pl.CostEstimate(
            flops=6 * HOPS * NX * ROOM * feat * hid, bytes_accessed=16_000_000, transcendentals=0
        ),
    )(ids, xe, de, act, wh)


def pack_kernel(g_ref, u_ref, d_ref, o_ref):
    hid = g_ref.shape[2]
    o_ref[:, :hid] = g_ref[0]
    o_ref[:, hid : 2 * hid] = u_ref[0]
    o_ref[:, 2 * hid :] = d_ref[0].astype(F32).T.astype(BF)


def pack(g, u, d):
    return pl.pallas_call(
        pack_kernel, out_shape=jax.ShapeDtypeStruct((g.shape[1], 3 * g.shape[2]), BF)
    )(g, u, d)


def unpack_kernel(s_ref, d_ref, g_out, u_out, d_out):
    hid = g_out.shape[2]
    g_out[0] = s_ref[:, :hid].astype(F32)
    u_out[0] = s_ref[:, hid:].astype(F32)
    d = d_ref[0].astype(F32)
    for i in range(1, NX):
        d = d + d_ref[i].astype(F32)
    d_out[0] = d.T


def unpack(s, d):
    rows, hid = s.shape[0], s.shape[1] // 2
    return pl.pallas_call(
        unpack_kernel,
        out_shape=[
            jax.ShapeDtypeStruct((1, rows, hid), F32),
            jax.ShapeDtypeStruct((1, rows, hid), F32),
            jax.ShapeDtypeStruct((1, hid, rows), F32),
        ],
    )(s, d)


def around(value, sign):
    pairs = [(z, (z + sign) % NZ) for z in range(NZ)]
    pairs += [(NZ + z, NZ + (z - sign) % NZ) for z in range(NZ)]
    return lax.ppermute(value, ("c", "z"), pairs)


def swap(value):
    return lax.ppermute(value, "c", [(0, 1), (1, 0)])


def add(a, b):
    return (a.astype(F32) + b.astype(F32)).astype(BF)


def shards(tokens, expert_ids, route_weight, out_grad, gate_weight, up_weight, down_weight):
    rows, feat = tokens.shape
    hid = gate_weight.shape[2]
    z = lax.axis_index("z").astype(jnp.int32)
    core = lax.axis_index("c").astype(jnp.int32)
    half = AUX // 2
    pair_rows = 2 * rows
    wa = lax.all_gather(pack(gate_weight, up_weight, down_weight), ("y", "c", "x"), axis=0, tiled=True)
    place = (expert_ids % NZ) * NX + expert_ids // NZ
    hot = place[:, :, None] == jnp.arange(half, dtype=jnp.int32)
    dense = jnp.sum(jnp.where(hot, route_weight[:, :, None], 0.0), 1)
    hi = lax.reduce_precision(dense, 8, 7)
    own_a = jnp.concatenate([tokens, hi.astype(BF), (dense - hi).astype(BF)], axis=1)
    chain_a = chip_a = jnp.concatenate([own_a, swap(own_a)], axis=0)
    chain_b = chip_b = jnp.concatenate([out_grad, swap(out_grad)], axis=0)
    got_a, got_b = [], []
    for _ in range(HOPS):
        chain_a = around(chain_a, 1)
        chain_b = around(chain_b, 1)
        got_a.append(chain_a)
        got_b.append(chain_b)
    got_a[-1] = jnp.where(core == 0, got_a[-1], chip_a)
    got_b[-1] = jnp.where(core == 0, got_b[-1], chip_b)
    ids = jnp.stack([z * NX, core])
    *saved, pa, pb = experts(
        ids,
        jnp.concatenate(got_a, axis=0),
        jnp.concatenate(got_b, axis=0),
        wa.reshape(NDP, NX, feat // NDP, 3 * hid),
    )
    gu, keep, send = weight_grads(ids, *saved)
    summed = lax.psum_scatter(
        gu.reshape(-1, 2 * hid), ("y", "c", "x"), scatter_dimension=0, tiled=True
    )
    down = swap(send)
    down = add(keep, down)
    down = lax.all_to_all(down, "y", 0, 0, tiled=True)
    down = jnp.sum(down.astype(F32), 0).astype(BF)
    down = lax.all_to_all(down, "x", 0, 0, tiled=True)

    def block(part, hop):
        return part[(hop - 1) * pair_rows : hop * pair_rows]

    none = jnp.zeros((), BF)
    chain_a = jnp.where(core == 0, block(pa, HOPS), none)
    chain_b = jnp.where(core == 0, block(pb, HOPS), none)
    for hop in range(HOPS, 0, -1):
        chain_a = around(chain_a, -1)
        chain_b = around(chain_b, -1)
        if hop > 1:
            chain_a = add(chain_a, block(pa, hop - 1))
            chain_b = add(chain_b, block(pb, hop - 1))
    chain_a = add(chain_a, jnp.where(core == 0, none, block(pa, HOPS)))
    chain_b = add(chain_b, jnp.where(core == 0, none, block(pb, HOPS)))
    total_a = chain_a[:rows].astype(F32) + swap(chain_a[rows:]).astype(F32)
    total_b = chain_b[:rows].astype(F32) + swap(chain_b[rows:]).astype(F32)
    layer_out = total_a[:, :feat].astype(BF)
    token_grad = total_b.astype(BF)
    pair = total_a[:, feat : feat + half] + total_a[:, feat + half :]
    route_grad = jnp.sum(jnp.where(hot, pair[:, None, :], 0.0), 2)
    return (layer_out, token_grad, route_grad, *unpack(summed, down))


def solution(mesh):
    grid = Mesh(mesh.devices.reshape(NY, NC, NX, NZ), ("y", "c", "x", "z"))
    dp, ex = ("y", "c"), ("x", "z")
    rowwise = P(dp + ex, None)
    weights = (P(ex, dp, None), P(ex, dp, None), P(ex, None, dp))
    return jax.shard_map(
        shards,
        mesh=grid,
        in_specs=(rowwise, rowwise, rowwise, rowwise, *weights),
        out_specs=(rowwise, rowwise, rowwise, *weights),
        check_vma=False,
    )
```

time: 249 us -> 255 us (1.024)
  other arithmetic: 27.9 us -> 11.4 us
  starting transfers between devices: 107 us -> 116 us
  waiting for transfers between devices: 61.1 us -> 69.1 us
  Pallas kernels: 26.1 us -> 30.7 us
    convert_element_type x17, other arithmetic: 22.5 us -> 5.69 us  [add(): return (a.astype(F32) + b.astype(F32)).astype(BF)]
    all_to_all x0 -> x2, waiting for transfers between devices: none -> 13.2 us  [the longest x1 8.86 us: shards(): down = lax.all_to_all(down, 'y', 0, 0, tiled=True)]
    all_to_all x0 -> x2, starting transfers between devices: none -> 8.98 us  [the longest x1 4.5 us: shards(): down = lax.all_to_all(down, 'x', 0, 0, tiled=True)]
    pallas_call x0 -> x1, Pallas kernels: none -> 8.85 us  [weight_grads(): pl.pallas_call(grad_kernel, grid_spec=pltpu.PrefetchScalarGridSpec(num_sc...]
    ppermute x5, waiting for transfers between devices: 8.73 us -> 0.29 us  [swap(): return lax.ppermute(value, 'c', [(0, 1), (1, 0)])]
    pallas_call x1, Pallas kernels: 22.4 us -> 18 us  [experts(): pl.pallas_call(moe_kernel, grid_spec=pltpu.PrefetchScalarGridSpec(num_sca...]
    ppermute x32, waiting for transfers between devices: 52.3 us -> 55.5 us  [around(): return lax.ppermute(value, ('c', 'z'), pairs)]
    unnamed x19 -> x29, local copies, waits for them, and re-layouts: 7.71 us -> 8.48 us
  transfers between devices with their start and end apart: 39 -> 41, of which waited for: 22 -> 24; matrix products, arithmetic and copies ran while one was open for 13% -> 8% of each run, Pallas kernels for 0% -> 0%
where the time goes in v3:
time: 255 us; the launch traced here: 252 us
  starting transfers between devices  116 us (45%)
  waiting for transfers between devices  69.1 us (27%)
  Pallas kernels  30.7 us (12%)
  between operations  14.8 us (6%)
  other arithmetic  11.4 us (4%)
  local copies, waits for them, and re-layouts  10.3 us (4%)
    ppermute x32, starting transfers between devices, around(): return lax.ppermute(value, ('c', 'z'), pairs)  96.4 us
    ppermute x32, waiting for transfers between devices, around(): return lax.ppermute(value, ('c', 'z'), pairs)  55.5 us
    pallas_call x1, Pallas kernels, experts(): pl.pallas_call(moe_kernel, grid_spec=pltpu.PrefetchScalarGridSpec(num_sca...  18 us
    ppermute x5, starting transfers between devices, swap(): return lax.ppermute(value, 'c', [(0, 1), (1, 0)])  10.6 us
    all_to_all x1, waiting for transfers between devices, shards(): down = lax.all_to_all(down, 'y', 0, 0, tiled=True)  8.86 us
    pallas_call x1, Pallas kernels, weight_grads(): pl.pallas_call(grad_kernel, grid_spec=pltpu.PrefetchScalarGridSpec(num_sc...  8.85 us
    unnamed x29, local copies, waits for them, and re-layouts  8.48 us
    convert_element_type x17, other arithmetic, add(): return (a.astype(F32) + b.astype(F32)).astype(BF)  5.69 us
  transfers between devices with their start and end apart: 41, of which 24 were waited for; matrix products, arithmetic and copies ran while one was open for 8% of the time, Pallas kernels for 0%

profile of v3, /device:TPU:6, one launch (start us, length us, event | category | flops | bytes accessed | tf_op | source)
XLA Modules:
  0.0 252.2 jit_solution(16286654881107958503)
XLA Ops:
  17.2 3.8 %collective-permute-start.10 = (bf16[128,1024]{1,0:T(8,128)(2,1)S(1)}, bf16[128,1024]{1,0:T(8,128)(2,1)S(1)}, u32[]{:S(2)}, u32[]{:S(2)}) collective-permute-start(bf16[128,1024]{1,0:T(8,128)(2,1)S(1)} %constant_dynamic-update-slice_fusion.7), channel_id=1, source_target_pairs={{0,1},{1,2},{2,3},{3,4},{4,5},{5,6},{6,7},{7,8},{8,9},{9,10},{10,1... | collective-permute-start | bytes 786440 | tf_op jit(solution)/shard_map/ppermute | solution.py:234
  21.1 3.8 %collective-permute-start.1 = (bf16[128,1152]{1,0:T(8,128)(2,1)S(1)}, bf16[128,1152]{1,0:T(8,128)(2,1)S(1)}, u32[]{:S(2)}, u32[]{:S(2)}) collective-permute-start(bf16[128,1152]{1,0:T(8,128)(2,1)S(1)} %pad_maximum_fusion), channel_id=1, source_target_pairs={{0,1},{1,2},{2,3},{3,4},{4,5},{5,6},{6,7},{7,8},{8,9},{9,10},{10,1... | collective-permute-start | bytes 884744 | tf_op jit(solution)/shard_map/ppermute | solution.py:234
  25.5 7.4 %collective-permute-done.10 = bf16[128,1024]{1,0:T(8,128)(2,1)S(1)} collective-permute-done((bf16[128,1024]{1,0:T(8,128)(2,1)S(1)}, bf16[128,1024]{1,0:T(8,128)(2,1)S(1)}, u32[]{:S(2)}, u32[]{:S(2)}) %collective-permute-start.10) | collective-permute-done | bytes 262176 | tf_op jit(solution)/shard_map/ppermute | solution.py:234
  38.8 3.6 %collective-permute-done.11 = bf16[128,1024]{1,0:T(8,128)(2,1)S(1)} collective-permute-done((bf16[128,1024]{1,0:T(8,128)(2,1)S(1)}, bf16[128,1024]{1,0:T(8,128)(2,1)S(1)}, u32[]{:S(2)}, u32[]{:S(2)}) %collective-permute-start.11) | collective-permute-done | bytes 262176 | tf_op jit(solution)/shard_map/ppermute | solution.py:234
  91.7 3.3 %collective-permute-done.7 = bf16[128,1152]{1,0:T(8,128)(2,1)S(1)} collective-permute-done((bf16[128,1152]{1,0:T(8,128)(2,1)S(1)}, bf16[128,1152]{1,0:T(8,128)(2,1)S(1)}, u32[]{:S(2)}, u32[]{:S(2)}) %collective-permute-start.7) | collective-permute-done | bytes 294944 | tf_op jit(solution)/shard_map/ppermute | solution.py:234
  99.3 5.5 %collective-permute-done.8 = bf16[128,1152]{1,0:T(8,128)(2,1)S(1)} collective-permute-done((bf16[128,1152]{1,0:T(8,128)(2,1)S(1)}, bf16[128,1152]{1,0:T(8,128)(2,1)S(1)}, u32[]{:S(2)}, u32[]{:S(2)}) %collective-permute-start.8) | collective-permute-done | bytes 294944 | tf_op jit(solution)/shard_map/ppermute | solution.py:234
  105.6 18.0 %shard_map.119 = (bf16[8,4,32,1024]{3,2,1,0:T(8,128)(2,1)}, bf16[8,4,32,1024]{3,2,1,0:T(8,128)(2,1)}, bf16[8,4,32,768]{3,2,1,0:T(8,128)(2,1)}, bf16[8,4,32,384]{...) custom-call(s32[2]{0:T(128)} %pad_add_fusion.ids_ref, ...), custom_call_target="tpu_custom_call" | custom-call | flops 5972688896 | bytes 26000000 | tf_op jit(solution)/shard_map/pallas_call | solution.py:117
  123.7 8.9 %shard_map.120 = (bf16[8,4,128,768]{3,2,1,0:T(8,128)(2,1)}, bf16[4,4,128,384]{3,2,1,0:T(8,128)(2,1)}, bf16[4,4,128,384]{3,2,1,0:T(8,128)(2,1)}) custom-call(s32[2]{0:T(128)} %pad_add_fusion.ids_ref, bf16[8,4,32,1024]{3,2,1,0:T(8,128)(2,1)} %get-tuple-element.20.xe_ref, bf16[8,4,32,1024]{3,2,1,0:T(8,128)(2,1)} %get-tuple-element.21.de_ref, ...), custom_call_target="tpu_custom_call" | custom-call | flops 2415919104 | bytes 16000000 | tf_op jit(solution)/shard_map/pallas_call | solution.py:177
  137.7 4.4 %collective-permute-done.27 = bf16[128,1024]{1,0:T(8,128)(2,1)S(1)} collective-permute-done((bf16[128,1024]{1,0:T(8,128)(2,1)S(1)}, bf16[128,1024]{1,0:T(8,128)(2,1)S(1)}, u32[]{:S(2)}, u32[]{:S(2)}) %collective-permute-start.27) | collective-permute-done | bytes 262176 | tf_op jit(solution)/shard_map/ppermute | solution.py:234
  151.4 4.5 %collective-permute-start.29 = (bf16[128,1024]{1,0:T(8,128)(2,1)S(1)}, bf16[128,1024]{1,0:T(8,128)(2,1)S(1)}, u32[]{:S(2)}, u32[]{:S(2)}) collective-permute-start(bf16[128,1024]{1,0:T(8,128)(2,1)S(1)} %add_convert_fusion.15), channel_id=1, source_target_pairs={{0,15},{1,0},{2,1},{3,2},{4,3},{5,4},{6,5},{7,6},{8,7},{9,8},{10,9... | collective-permute-start | bytes 786440 | tf_op jit(solution)/shard_map/ppermute | solution.py:234
  159.9 5.6 %collective-permute-start.30 = (bf16[128,1024]{1,0:T(8,128)(2,1)S(1)}, bf16[128,1024]{1,0:T(8,128)(2,1)S(1)}, u32[]{:S(2)}, u32[]{:S(2)}) collective-permute-start(bf16[128,1024]{1,0:T(8,128)(2,1)S(1)} %add_convert_fusion.14), channel_id=1, source_target_pairs={{0,15},{1,0},{2,1},{3,2},{4,3},{5,4},{6,5},{7,6},{8,7},{9,8},{10,9... | collective-permute-start | bytes 786440 | tf_op jit(solution)/shard_map/ppermute | solution.py:234
  165.6 3.3 %collective-permute-start.21 = (bf16[128,1152]{1,0:T(8,128)(2,1)S(1)}, bf16[128,1152]{1,0:T(8,128)(2,1)S(1)}, u32[]{:S(2)}, u32[]{:S(2)}) collective-permute-start(bf16[128,1152]{1,0:T(8,128)(2,1)S(1)} %add_convert_fusion.6), channel_id=1, source_target_pairs={{0,15},{1,0},{2,1},{3,2},{4,3},{5,4},{6,5},{7,6},{8,7},{9,8},{10,9... | collective-permute-start | bytes 884744 | tf_op jit(solution)/shard_map/ppermute | solution.py:234
  169.4 5.6 %collective-permute-start.31 = (bf16[128,1024]{1,0:T(8,128)(2,1)S(1)}, bf16[128,1024]{1,0:T(8,128)(2,1)S(1)}, u32[]{:S(2)}, u32[]{:S(2)}) collective-permute-start(bf16[128,1024]{1,0:T(8,128)(2,1)S(1)} %add_convert_fusion.13), channel_id=1, source_target_pairs={{0,15},{1,0},{2,1},{3,2},{4,3},{5,4},{6,5},{7,6},{8,7},{9,8},{10,9... | collective-permute-start | bytes 786440 | tf_op jit(solution)/shard_map/ppermute | solution.py:234
  175.1 3.6 %collective-permute-start.22 = (bf16[128,1152]{1,0:T(8,128)(2,1)S(1)}, bf16[128,1152]{1,0:T(8,128)(2,1)S(1)}, u32[]{:S(2)}, u32[]{:S(2)}) collective-permute-start(bf16[128,1152]{1,0:T(8,128)(2,1)S(1)} %add_convert_fusion.5), channel_id=1, source_target_pairs={{0,15},{1,0},{2,1},{3,2},{4,3},{5,4},{6,5},{7,6},{8,7},{9,8},{10,9... | collective-permute-start | bytes 884744 | tf_op jit(solution)/shard_map/ppermute | solution.py:234
  180.8 3.9 %collective-permute-start.32 = (bf16[128,1024]{1,0:T(8,128)(2,1)S(1)}, bf16[128,1024]{1,0:T(8,128)(2,1)S(1)}, u32[]{:S(2)}, u32[]{:S(2)}) collective-permute-start(bf16[128,1024]{1,0:T(8,128)(2,1)S(1)} %add_convert_fusion.12), channel_id=1, source_target_pairs={{0,15},{1,0},{2,1},{3,2},{4,3},{5,4},{6,5},{7,6},{8,7},{9,8},{10,9... | collective-permute-start | bytes 786440 | tf_op jit(solution)/shard_map/ppermute | solution.py:234
  184.8 3.9 %collective-permute-start.23 = (bf16[128,1152]{1,0:T(8,128)(2,1)S(1)}, bf16[128,1152]{1,0:T(8,128)(2,1)S(1)}, u32[]{:S(2)}, u32[]{:S(2)}) collective-permute-start(bf16[128,1152]{1,0:T(8,128)(2,1)S(1)} %add_convert_fusion.4), channel_id=1, source_target_pairs={{0,15},{1,0},{2,1},{3,2},{4,3},{5,4},{6,5},{7,6},{8,7},{9,8},{10,9... | collective-permute-start | bytes 884744 | tf_op jit(solution)/shard_map/ppermute | solution.py:234
  189.3 5.0 %collective-permute-start.33 = (bf16[128,1024]{1,0:T(8,128)(2,1)S(1)}, bf16[128,1024]{1,0:T(8,128)(2,1)S(1)}, u32[]{:S(2)}, u32[]{:S(2)}) collective-permute-start(bf16[128,1024]{1,0:T(8,128)(2,1)S(1)} %add_convert_fusion.11), channel_id=1, source_target_pairs={{0,15},{1,0},{2,1},{3,2},{4,3},{5,4},{6,5},{7,6},{8,7},{9,8},{10,9... | collective-permute-start | bytes 786440 | tf_op jit(solution)/shard_map/ppermute | solution.py:234
  194.4 4.2 %collective-permute-start.24 = (bf16[128,1152]{1,0:T(8,128)(2,1)S(1)}, bf16[128,1152]{1,0:T(8,128)(2,1)S(1)}, u32[]{:S(2)}, u32[]{:S(2)}) collective-permute-start(bf16[128,1152]{1,0:T(8,128)(2,1)S(1)} %add_convert_fusion.3), channel_id=1, source_target_pairs={{0,15},{1,0},{2,1},{3,2},{4,3},{5,4},{6,5},{7,6},{8,7},{9,8},{10,9... | collective-permute-start | bytes 884744 | tf_op jit(solution)/shard_map/ppermute | solution.py:234
  198.7 5.1 %collective-permute-start.34 = (bf16[128,1024]{1,0:T(8,128)(2,1)S(1)}, bf16[128,1024]{1,0:T(8,128)(2,1)S(1)}, u32[]{:S(2)}, u32[]{:S(2)}) collective-permute-start(bf16[128,1024]{1,0:T(8,128)(2,1)S(1)} %add_convert_fusion.10), channel_id=1, source_target_pairs={{0,15},{1,0},{2,1},{3,2},{4,3},{5,4},{6,5},{7,6},{8,7},{9,8},{10,9... | collective-permute-start | bytes 786440 | tf_op jit(solution)/shard_map/ppermute | solution.py:234
  203.9 4.6 %collective-permute-start.25 = (bf16[128,1152]{1,0:T(8,128)(2,1)S(1)}, bf16[128,1152]{1,0:T(8,128)(2,1)S(1)}, u32[]{:S(2)}, u32[]{:S(2)}) collective-permute-start(bf16[128,1152]{1,0:T(8,128)(2,1)S(1)} %add_convert_fusion.2), channel_id=1, source_target_pairs={{0,15},{1,0},{2,1},{3,2},{4,3},{5,4},{6,5},{7,6},{8,7},{9,8},{10,9... | collective-permute-start | bytes 884744 | tf_op jit(solution)/shard_map/ppermute | solution.py:234
  210.2 4.5 %all-to-all-start = ((bf16[4,4,128,384]{3,2,1,0:T(8,128)(2,1)}), bf16[4,4,128,384]{3,2,1,0:T(8,128)(2,1)S(1)}, u32[]{:S(2)}, u32[]{:S(2)}) async-start(bf16[4,4,128,384]{3,2,1,0:T(8,128)(2,1)} %add_convert_fusion), calls=%async_computation.1 | async-start | bytes 3145728 | tf_op jit(solution)/shard_map/all_to_all | solution.py:281
  222.8 8.9 %all-to-all-done = bf16[4,4,128,384]{3,2,1,0:T(8,128)(2,1)S(1)} async-done(((bf16[4,4,128,384]{3,2,1,0:T(8,128)(2,1)}), bf16[4,4,128,384]{3,2,1,0:T(8,128)(2,1)S(1)}, u32[]{:S(2)}, u32[]{:S(2)}) %all-to-all-start) | async-done | bytes 1572896 | tf_op jit(solution)/shard_map/all_to_all | solution.py:281
  232.8 4.5 %all-to-all-start.1 = ((bf16[4,128,384]{2,1,0:T(8,128)(2,1)}), bf16[4,128,384]{2,1,0:T(8,128)(2,1)S(1)}, u32[]{:S(2)}, u32[]{:S(2)}) async-start(bf16[4,128,384]{2,1,0:T(8,128)(2,1)} %reduce_sum.32), calls=%async_computation.2 | async-start | bytes 786432 | tf_op jit(solution)/shard_map/all_to_all | solution.py:283
  238.3 4.3 %all-to-all-done.1.d_ref = bf16[4,128,384]{2,1,0:T(8,128)(2,1)S(1)} async-done(((bf16[4,128,384]{2,1,0:T(8,128)(2,1)}), bf16[4,128,384]{2,1,0:T(8,128)(2,1)S(1)}, u32[]{:S(2)}, u32[]{:S(2)}) %all-to-all-start.1) | async-done | bytes 393248 | tf_op jit(solution)/shard_map/all_to_all | solution.py:283
  (130 shorter events, 107.2 us)
Async XLA Ops:
  7.2 98.5 %all-gather.2.cloned.1.call-start = ((), (), s32[]{:S(2)}) async-start(), calls=%async_computation.3 | async-start | bytes 9732096 | tf_op jit(solution)/shard_map/all_gather | solution.py:252
  9.1 233.6 %reduce-scatter.2.cloned.1.call-start = ((), (), s32[]{:S(2)}) async-start(), calls=%async_computation.4 | async-start | bytes 6488064 | tf_op jit(solution)/shard_map/reduce_scatter | solution.py:276
  17.2 15.7 %collective-permute-start.10 = (bf16[128,1024]{1,0:T(8,128)(2,1)S(1)}, bf16[128,1024]{1,0:T(8,128)(2,1)S(1)}, u32[]{:S(2)}, u32[]{:S(2)}) collective-permute-start(bf16[128,1024]{1,0:T(8,128)(2,1)S(1)} %constant_dynamic-update-slice_fusion.7), channel_id=1, source_target_pairs={{0,1},{1,2},{2,3},{3,4},{4,5},{5,6},{6,7},{7,8},{8,9},{9,10},{10,1... | collective-permute-start | bytes 786440 | tf_op jit(solution)/shard_map/ppermute | solution.py:234
  21.1 15.0 %collective-permute-start.1 = (bf16[128,1152]{1,0:T(8,128)(2,1)S(1)}, bf16[128,1152]{1,0:T(8,128)(2,1)S(1)}, u32[]{:S(2)}, u32[]{:S(2)}) collective-permute-start(bf16[128,1152]{1,0:T(8,128)(2,1)S(1)} %pad_maximum_fusion), channel_id=1, source_target_pairs={{0,1},{1,2},{2,3},{3,4},{4,5},{5,6},{6,7},{7,8},{8,9},{9,10},{10,1... | collective-permute-start | bytes 884744 | tf_op jit(solution)/shard_map/ppermute | solution.py:234
  32.9 9.5 %collective-permute-start.11 = (bf16[128,1024]{1,0:T(8,128)(2,1)S(1)}, bf16[128,1024]{1,0:T(8,128)(2,1)S(1)}, u32[]{:S(2)}, u32[]{:S(2)}) collective-permute-start(bf16[128,1024]{1,0:T(8,128)(2,1)S(1)} %collective-permute-done.10), channel_id=1, source_target_pairs={{0,1},{1,2},{2,3},{3,4},{4,5},{5,6},{6,7},{7,8},{8,9},{9,10},{10,1... | collective-permute-start | bytes 786440 | tf_op jit(solution)/shard_map/ppermute | solution.py:234
  36.1 9.8 %collective-permute-start.2 = (bf16[128,1152]{1,0:T(8,128)(2,1)S(1)}, bf16[128,1152]{1,0:T(8,128)(2,1)S(1)}, u32[]{:S(2)}, u32[]{:S(2)}) collective-permute-start(bf16[128,1152]{1,0:T(8,128)(2,1)S(1)} %collective-permute-done.1), channel_id=1, source_target_pairs={{0,1},{1,2},{2,3},{3,4},{4,5},{5,6},{6,7},{7,8},{8,9},{9,10},{10,1... | collective-permute-start | bytes 884744 | tf_op jit(solution)/shard_map/ppermute | solution.py:234
  42.4 9.5 %collective-permute-start.12 = (bf16[128,1024]{1,0:T(8,128)(2,1)S(1)}, bf16[128,1024]{1,0:T(8,128)(2,1)S(1)}, u32[]{:S(2)}, u32[]{:S(2)}) collective-permute-start(bf16[128,1024]{1,0:T(8,128)(2,1)S(1)} %collective-permute-done.11), channel_id=1, source_target_pairs={{0,1},{1,2},{2,3},{3,4},{4,5},{5,6},{6,7},{7,8},{8,9},{9,10},{10,1... | collective-permute-start | bytes 786440 | tf_op jit(solution)/shard_map/ppermute | solution.py:234
  45.9 9.8 %collective-permute-start.3 = (bf16[128,1152]{1,0:T(8,128)(2,1)S(1)}, bf16[128,1152]{1,0:T(8,128)(2,1)S(1)}, u32[]{:S(2)}, u32[]{:S(2)}) collective-permute-start(bf16[128,1152]{1,0:T(8,128)(2,1)S(1)} %collective-permute-done.2), channel_id=1, source_target_pairs={{0,1},{1,2},{2,3},{3,4},{4,5},{5,6},{6,7},{7,8},{8,9},{9,10},{10,1... | collective-permute-start | bytes 884744 | tf_op jit(solution)/shard_map/ppermute | solution.py:234
  51.9 9.5 %collective-permute-start.13 = (bf16[128,1024]{1,0:T(8,128)(2,1)S(1)}, bf16[128,1024]{1,0:T(8,128)(2,1)S(1)}, u32[]{:S(2)}, u32[]{:S(2)}) collective-permute-start(bf16[128,1024]{1,0:T(8,128)(2,1)S(1)} %collective-permute-done.12), channel_id=1, source_target_pairs={{0,1},{1,2},{2,3},{3,4},{4,5},{5,6},{6,7},{7,8},{8,9},{9,10},{10,1... | collective-permute-start | bytes 786440 | tf_op jit(solution)/shard_map/ppermute | solution.py:234
  55.7 9.8 %collective-permute-start.4 = (bf16[128,1152]{1,0:T(8,128)(2,1)S(1)}, bf16[128,1152]{1,0:T(8,128)(2,1)S(1)}, u32[]{:S(2)}, u32[]{:S(2)}) collective-permute-start(bf16[128,1152]{1,0:T(8,128)(2,1)S(1)} %collective-permute-done.3), channel_id=1, source_target_pairs={{0,1},{1,2},{2,3},{3,4},{4,5},{5,6},{6,7},{7,8},{8,9},{9,10},{10,1... | collective-permute-start | bytes 884744 | tf_op jit(solution)/shard_map/ppermute | solution.py:234
  61.3 9.5 %collective-permute-start.14 = (bf16[128,1024]{1,0:T(8,128)(2,1)S(1)}, bf16[128,1024]{1,0:T(8,128)(2,1)S(1)}, u32[]{:S(2)}, u32[]{:S(2)}) collective-permute-start(bf16[128,1024]{1,0:T(8,128)(2,1)S(1)} %collective-permute-done.13), channel_id=1, source_target_pairs={{0,1},{1,2},{2,3},{3,4},{4,5},{5,6},{6,7},{7,8},{8,9},{9,10},{10,1... | collective-permute-start | bytes 786440 | tf_op jit(solution)/shard_map/ppermute | solution.py:234
  65.5 9.8 %collective-permute-start.5 = (bf16[128,1152]{1,0:T(8,128)(2,1)S(1)}, bf16[128,1152]{1,0:T(8,128)(2,1)S(1)}, u32[]{:S(2)}, u32[]{:S(2)}) collective-permute-start(bf16[128,1152]{1,0:T(8,128)(2,1)S(1)} %collective-permute-done.4), channel_id=1, source_target_pairs={{0,1},{1,2},{2,3},{3,4},{4,5},{5,6},{6,7},{7,8},{8,9},{9,10},{10,1... | collective-permute-start | bytes 884744 | tf_op jit(solution)/shard_map/ppermute | solution.py:234
  75.4 9.8 %collective-permute-start.6 = (bf16[128,1152]{1,0:T(8,128)(2,1)S(1)}, bf16[128,1152]{1,0:T(8,128)(2,1)S(1)}, u32[]{:S(2)}, u32[]{:S(2)}) collective-permute-start(bf16[128,1152]{1,0:T(8,128)(2,1)S(1)} %collective-permute-done.5), channel_id=1, source_target_pairs={{0,1},{1,2},{2,3},{3,4},{4,5},{5,6},{6,7},{7,8},{8,9},{9,10},{10,1... | collective-permute-start | bytes 884744 | tf_op jit(solution)/shard_map/ppermute | solution.py:234
  85.2 9.8 %collective-permute-start.7 = (bf16[128,1152]{1,0:T(8,128)(2,1)S(1)}, bf16[128,1152]{1,0:T(8,128)(2,1)S(1)}, u32[]{:S(2)}, u32[]{:S(2)}) collective-permute-start(bf16[128,1152]{1,0:T(8,128)(2,1)S(1)} %collective-permute-done.6), channel_id=1, source_target_pairs={{0,1},{1,2},{2,3},{3,4},{4,5},{5,6},{6,7},{7,8},{8,9},{9,10},{10,1... | collective-permute-start | bytes 884744 | tf_op jit(solution)/shard_map/ppermute | solution.py:234
  95.0 9.8 %collective-permute-start.8 = (bf16[128,1152]{1,0:T(8,128)(2,1)S(1)}, bf16[128,1152]{1,0:T(8,128)(2,1)S(1)}, u32[]{:S(2)}, u32[]{:S(2)}) collective-permute-start(bf16[128,1152]{1,0:T(8,128)(2,1)S(1)} %collective-permute-done.7), channel_id=1, source_target_pairs={{0,1},{1,2},{2,3},{3,4},{4,5},{5,6},{6,7},{7,8},{8,9},{9,10},{10,1... | collective-permute-start | bytes 884744 | tf_op jit(solution)/shard_map/ppermute | solution.py:234
  135.8 10.4 %collective-permute-start.18 = (bf16[128,1152]{1,0:T(8,128)(2,1)S(1)}, bf16[128,1152]{1,0:T(8,128)(2,1)S(1)}, u32[]{:S(2)}, u32[]{:S(2)}) collective-permute-start(bf16[128,1152]{1,0:T(8,128)(2,1)S(1)} %broadcast_select_fusion), channel_id=1, source_target_pairs={{0,15},{1,0},{2,1},{3,2},{4,3},{5,4},{6,5},{7,6},{8,7},{9,8},{10,9... | collective-permute-start | bytes 884744 | tf_op jit(solution)/shard_map/ppermute | solution.py:234
  146.3 9.6 %collective-permute-start.19 = (bf16[128,1152]{1,0:T(8,128)(2,1)S(1)}, bf16[128,1152]{1,0:T(8,128)(2,1)S(1)}, u32[]{:S(2)}, u32[]{:S(2)}) collective-permute-start(bf16[128,1152]{1,0:T(8,128)(2,1)S(1)} %add_convert_fusion.8), channel_id=1, source_target_pairs={{0,15},{1,0},{2,1},{3,2},{4,3},{5,4},{6,5},{7,6},{8,7},{9,8},{10,9... | collective-permute-start | bytes 884744 | tf_op jit(solution)/shard_map/ppermute | solution.py:234
  169.4 11.3 %collective-permute-start.31 = (bf16[128,1024]{1,0:T(8,128)(2,1)S(1)}, bf16[128,1024]{1,0:T(8,128)(2,1)S(1)}, u32[]{:S(2)}, u32[]{:S(2)}) collective-permute-start(bf16[128,1024]{1,0:T(8,128)(2,1)S(1)} %add_convert_fusion.13), channel_id=1, source_target_pairs={{0,15},{1,0},{2,1},{3,2},{4,3},{5,4},{6,5},{7,6},{8,7},{9,8},{10,9... | collective-permute-start | bytes 786440 | tf_op jit(solution)/shard_map/ppermute | solution.py:234
  175.1 9.6 %collective-permute-start.22 = (bf16[128,1152]{1,0:T(8,128)(2,1)S(1)}, bf16[128,1152]{1,0:T(8,128)(2,1)S(1)}, u32[]{:S(2)}, u32[]{:S(2)}) collective-permute-start(bf16[128,1152]{1,0:T(8,128)(2,1)S(1)} %add_convert_fusion.5), channel_id=1, source_target_pairs={{0,15},{1,0},{2,1},{3,2},{4,3},{5,4},{6,5},{7,6},{8,7},{9,8},{10,9... | collective-permute-start | bytes 884744 | tf_op jit(solution)/shard_map/ppermute | solution.py:234
  178.8 29.7 %collective-permute-start.36 = (bf16[4,4,128,384]{3,2,1,0:T(8,128)(2,1)S(1)}, bf16[4,4,128,384]{3,2,1,0:T(8,128)(2,1)S(1)}, u32[]{:S(2)}, u32[]{:S(2)}) collective-permute-start(bf16[4,4,128,384]{3,2,1,0:T(8,128)(2,1)S(1)} %copy-done.5), channel_id=1, source_target_pairs={{0,64},{64,0},{1,65},{65,1},{2,66},{66,2},{3,67},{67,3},{4,68},{68... | collective-permute-start | bytes 4718600 | tf_op jit(solution)/shard_map/ppermute | solution.py:238
  198.7 16.0 %collective-permute-start.34 = (bf16[128,1024]{1,0:T(8,128)(2,1)S(1)}, bf16[128,1024]{1,0:T(8,128)(2,1)S(1)}, u32[]{:S(2)}, u32[]{:S(2)}) collective-permute-start(bf16[128,1024]{1,0:T(8,128)(2,1)S(1)} %add_convert_fusion.10), channel_id=1, source_target_pairs={{0,15},{1,0},{2,1},{3,2},{4,3},{5,4},{6,5},{7,6},{8,7},{9,8},{10,9... | collective-permute-start | bytes 786440 | tf_op jit(solution)/shard_map/ppermute | solution.py:234
  203.9 13.7 %collective-permute-start.25 = (bf16[128,1152]{1,0:T(8,128)(2,1)S(1)}, bf16[128,1152]{1,0:T(8,128)(2,1)S(1)}, u32[]{:S(2)}, u32[]{:S(2)}) collective-permute-start(bf16[128,1152]{1,0:T(8,128)(2,1)S(1)} %add_convert_fusion.2), channel_id=1, source_target_pairs={{0,15},{1,0},{2,1},{3,2},{4,3},{5,4},{6,5},{7,6},{8,7},{9,8},{10,9... | collective-permute-start | bytes 884744 | tf_op jit(solution)/shard_map/ppermute | solution.py:234
  210.2 21.5 %all-to-all-start = ((bf16[4,4,128,384]{3,2,1,0:T(8,128)(2,1)}), bf16[4,4,128,384]{3,2,1,0:T(8,128)(2,1)S(1)}, u32[]{:S(2)}, u32[]{:S(2)}) async-start(bf16[4,4,128,384]{3,2,1,0:T(8,128)(2,1)} %add_convert_fusion), calls=%async_computation.1 | async-start | bytes 3145728 | tf_op jit(solution)/shard_map/all_to_all | solution.py:281
  232.8 9.8 %all-to-all-start.1 = ((bf16[4,128,384]{2,1,0:T(8,128)(2,1)}), bf16[4,128,384]{2,1,0:T(8,128)(2,1)S(1)}, u32[]{:S(2)}, u32[]{:S(2)}) async-start(bf16[4,128,384]{2,1,0:T(8,128)(2,1)} %reduce_sum.32), calls=%async_computation.2 | async-start | bytes 786432 | tf_op jit(solution)/shard_map/all_to_all | solution.py:283
  (23 other events, 225.9 us)
Sparse Core Ops, SparseCore 0:
  11.1 74.9 all-gather.1
  132.7 108.2 reduce-scatter.1

commit v4 on v2

--- a/solution.py
+++ b/solution.py
@@ -21,13 +21,16 @@
     return lax.dot_general(a, b, (((ca,), (cb,)), ((), ())), preferred_element_type=F32)
 
 
-def moe_kernel(ids_ref, xa_ref, xb_ref, wt_ref, keep_ref, send_ref, pa_ref, pb_ref, pos_s, w_s, sel_s, rows_s):
+def grad_kernel(
+    ids_ref, xa_ref, xb_ref, wt_ref, keep_ref, send_ref, act_ref, wh_ref, aux_ref, sel_ref, w_s, pos_s, xe_s, de_s
+):
     e = pl.program_id(0)
     col = ids_ref[0]
     core = ids_ref[1]
     tok = xa_ref.shape[0]
     feat = xb_ref.shape[1]
     hid = wt_ref.shape[3] // 3
+    slot = lax.broadcasted_iota(jnp.int32, (SLOTS, tok), 0)
 
     @pl.when(e == 0)
     def _():
@@ -46,12 +49,19 @@
             rank = dot(part.astype(BF), upper, 1, 0) + before
             pos_s[:, lo : lo + 128] = jnp.where(part > 0.0, rank, -1.0).astype(jnp.int32)
             before = before + jnp.sum(part, axis=1, keepdims=True)
-
-    picked = pos_s[pl.ds(e, 1), :] == lax.broadcasted_iota(jnp.int32, (SLOTS, tok), 0)
-    sel = jnp.where(picked, 1.0, 0.0).astype(BF)
+        for j in range(NX):
+            hit = pos_s[j : j + 1, :] == slot
+            sel_ref[j * SLOTS : (j + 1) * SLOTS, :] = jnp.where(hit, 1.0, 0.0).astype(BF)
+        for lo in range(0, feat, 512):
+            span = slice(lo, lo + 512)
+            xe_s[:, span] = dot(sel_ref[...], xa_ref[:, span], 1, 0).astype(BF)
+            de_s[:, span] = dot(sel_ref[...], xb_ref[:, span], 1, 0).astype(BF)
+
+    here = pl.ds(pl.multiple_of(e * SLOTS, SLOTS), SLOTS)
+    xe = xe_s[here, :]
+    de = de_s[here, :]
+    picked = pos_s[pl.ds(e, 1), :] == slot
     w = jnp.sum(jnp.where(picked, w_s[pl.ds(e, 1), :], 0.0), axis=1, keepdims=True)
-    xe = dot(sel, xa_ref[:, :feat], 1, 0).astype(BF)
-    de = dot(sel, xb_ref[...], 1, 0).astype(BF)
     wt = wt_ref[:, 0].reshape(feat, 3 * hid)
     gu = dot(xe, wt[:, : 2 * hid], 1, 0)
     hd = dot(de, wt[:, 2 * hid :], 1, 0)
@@ -66,15 +76,13 @@
     gb = (hg * u * s * (1.0 + g * (1.0 - s))).astype(BF)
     ub = (hg * gs).astype(BF)
     act = jnp.concatenate([gb, ub], axis=1)
-    here = pl.ds(pl.multiple_of(e * SLOTS, SLOTS), SLOTS)
-    sel_s[here, :] = sel
-    rows_s[here, :feat] = dot(wh, wt[:, 2 * hid :], 1, 1).astype(BF)
+    act_ref[...] = act
+    wh_ref[...] = wh
     lane = lax.broadcasted_iota(jnp.int32, (SLOTS, AUX), 1)
     mine = col + e
     rg_hi = rg.astype(BF).astype(F32)
     aux = jnp.where(lane == mine, rg_hi, 0.0) + jnp.where(lane == mine + AUX // 2, rg - rg_hi, 0.0)
-    rows_s[here, feat : feat + AUX] = aux.astype(BF)
-    rows_s[here, feat + AUX :] = dot(act, wt[:, : 2 * hid], 1, 1).astype(BF)
+    aux_ref[...] = aux.astype(BF)
     step = feat // NDP
 
     def halves(v):
@@ -89,56 +97,106 @@
     send_ref[:, 0, :, : 2 * hid] = dot(xs, act, 0, 0).astype(BF).reshape(NY, step, 2 * hid)
     send_ref[:, 0, :, 2 * hid :] = dot(ds, wh, 0, 0).astype(BF).reshape(NY, step, hid)
 
-    @pl.when(e == NX - 1)
-    def _():
-        for lo in range(0, feat + AUX, 384):
-            pa_ref[:, lo : lo + 384] = dot(sel_s[...], rows_s[:, lo : lo + 384], 0, 0).astype(BF)
-        for lo in range(0, feat, 512):
-            off = feat + AUX + lo
-            pb_ref[:, lo : lo + 512] = dot(sel_s[...], rows_s[:, off : off + 512], 0, 0).astype(BF)
-
-
-def experts(ids, xa, xb, wt):
+
+def expert_grads(ids, xa, xb, wt):
     tok, feat = xb.shape
     hid3 = wt.shape[3]
+    hid = hid3 // 3
     rows = feat // NDP
     slots = NX * SLOTS
-    width = 2 * feat + AUX
-    flops = 2 * slots * (tok * width * 2 + 9 * feat * hid3 // 3)
     whole = lambda e, s: (0, 0)
+    expert = lambda e, s: (0, e, 0, 0)
+    slotted = lambda e, s: (e, 0)
     return pl.pallas_call(
-        moe_kernel,
+        grad_kernel,
         grid_spec=pltpu.PrefetchScalarGridSpec(
             num_scalar_prefetch=1,
             grid=(NX,),
             in_specs=[
                 pl.BlockSpec((tok, feat + AUX), whole),
                 pl.BlockSpec((tok, feat), whole),
-                pl.BlockSpec((NDP, 1, rows, hid3), lambda e, s: (0, e, 0, 0)),
+                pl.BlockSpec((NDP, 1, rows, hid3), expert),
             ],
             out_specs=[
-                pl.BlockSpec((NY, 1, rows, hid3), lambda e, s: (0, e, 0, 0)),
-                pl.BlockSpec((NY, 1, rows, hid3), lambda e, s: (0, e, 0, 0)),
-                pl.BlockSpec((tok, feat + AUX), whole),
-                pl.BlockSpec((tok, feat), whole),
+                pl.BlockSpec((NY, 1, rows, hid3), expert),
+                pl.BlockSpec((NY, 1, rows, hid3), expert),
+                pl.BlockSpec((SLOTS, 2 * hid), slotted),
+                pl.BlockSpec((SLOTS, hid), slotted),
+                pl.BlockSpec((SLOTS, AUX), slotted),
+                pl.BlockSpec((slots, tok), whole),
             ],
             scratch_shapes=[
+                pltpu.VMEM((PLANES, tok), F32),
                 pltpu.VMEM((PLANES, tok), jnp.int32),
-                pltpu.VMEM((PLANES, tok), F32),
-                pltpu.VMEM((slots, tok), BF),
-                pltpu.VMEM((slots, width), BF),
+                pltpu.VMEM((slots, feat), BF),
+                pltpu.VMEM((slots, feat), BF),
             ],
         ),
         out_shape=[
             jax.ShapeDtypeStruct((NY, NX, rows, hid3), BF),
             jax.ShapeDtypeStruct((NY, NX, rows, hid3), BF),
+            jax.ShapeDtypeStruct((slots, 2 * hid), BF),
+            jax.ShapeDtypeStruct((slots, hid), BF),
+            jax.ShapeDtypeStruct((slots, AUX), BF),
+            jax.ShapeDtypeStruct((slots, tok), BF),
+        ],
+        cost_estimate=pl.CostEstimate(
+            flops=2 * slots * feat * (2 * tok + 6 * hid),
+            bytes_accessed=26_000_000,
+            transcendentals=slots * hid,
+        ),
+    )(ids, xa, xb, wt)
+
+
+def merge_kernel(act_ref, wh_ref, aux_ref, sel_ref, wt_ref, pa_ref, pb_ref, rows_s):
+    e = pl.program_id(0)
+    feat = pb_ref.shape[1]
+    hid = wh_ref.shape[1]
+    here = pl.ds(pl.multiple_of(e * SLOTS, SLOTS), SLOTS)
+    wt = wt_ref[:, 0].reshape(feat, 3 * hid)
+    rows_s[here, :feat] = dot(wh_ref[...], wt[:, 2 * hid :], 1, 1).astype(BF)
+    rows_s[here, feat : feat + AUX] = aux_ref[...]
+    rows_s[here, feat + AUX :] = dot(act_ref[...], wt[:, : 2 * hid], 1, 1).astype(BF)
+
+    @pl.when(e == NX - 1)
+    def _():
+        for lo in range(0, feat + AUX, 384):
+            pa_ref[:, lo : lo + 384] = dot(sel_ref[...], rows_s[:, lo : lo + 384], 0, 0).astype(BF)
+        for lo in range(0, feat, 512):
+            off = feat + AUX + lo
+            pb_ref[:, lo : lo + 512] = dot(sel_ref[...], rows_s[:, off : off + 512], 0, 0).astype(BF)
+
+
+def merge(act, wh, aux, sel, wt):
+    slots, tok = sel.shape
+    hid = wh.shape[1]
+    rows = wt.shape[2]
+    feat = rows * NDP
+    whole = lambda e: (0, 0)
+    slotted = lambda e: (e, 0)
+    return pl.pallas_call(
+        merge_kernel,
+        grid=(NX,),
+        in_specs=[
+            pl.BlockSpec((SLOTS, 2 * hid), slotted),
+            pl.BlockSpec((SLOTS, hid), slotted),
+            pl.BlockSpec((SLOTS, AUX), slotted),
+            pl.BlockSpec((slots, tok), whole),
+            pl.BlockSpec((NDP, 1, rows, 3 * hid), lambda e: (0, e, 0, 0)),
+        ],
+        out_specs=[
+            pl.BlockSpec((tok, feat + AUX), whole),
+            pl.BlockSpec((tok, feat), whole),
+        ],
+        scratch_shapes=[pltpu.VMEM((slots, 2 * feat + AUX), BF)],
+        out_shape=[
             jax.ShapeDtypeStruct((tok, feat + AUX), BF),
             jax.ShapeDtypeStruct((tok, feat), BF),
         ],
         cost_estimate=pl.CostEstimate(
-            flops=flops, bytes_accessed=30_000_000, transcendentals=slots * hid3 // 3
+            flops=2 * slots * feat * (2 * tok + 3 * hid), bytes_accessed=16_000_000, transcendentals=0
         ),
-    )(ids, xa, xb, wt)
+    )(act, wh, aux, sel, wt)
 
 
 def pack_kernel(g_ref, u_ref, d_ref, o_ref):
@@ -210,15 +268,14 @@
         got_b.append(chain_b)
     got_a[-1] = jnp.where(core == 0, got_a[-1], chip_a)
     got_b[-1] = jnp.where(core == 0, got_b[-1], chip_b)
-    keep, send, pa, pb = experts(
-        jnp.stack([z * NX, core]),
-        jnp.concatenate(got_a, axis=0),
-        jnp.concatenate(got_b, axis=0),
-        wa.reshape(NDP, NX, feat // NDP, 3 * hid),
+    wt = wa.reshape(NDP, NX, feat // NDP, 3 * hid)
+    keep, send, *saved = expert_grads(
+        jnp.stack([z * NX, core]), jnp.concatenate(got_a, axis=0), jnp.concatenate(got_b, axis=0), wt
     )
-    grads = add(keep, swap(send))
+    send = swap(send)
+    pa, pb = merge(*saved, wt)
     summed = lax.psum_scatter(
-        grads.reshape(-1, 3 * hid), ("y", "x"), scatter_dimension=0, tiled=True
+        add(keep, send).reshape(-1, 3 * hid), ("y", "x"), scatter_dimension=0, tiled=True
     )
 
     def block(part, hop):

time: 249 us -> 257 us (1.032)
  Pallas kernels: 26.1 us -> 33.5 us
    pallas_call x1 -> x2, Pallas kernels: 22.4 us -> 29.9 us  [the longest x1 16.7 us: expert_grads(): pl.pallas_call(grad_kernel, grid_spec=pltpu.PrefetchScalarGridSpec(num_sc...]
  transfers between devices with their start and end apart: 39 -> 39, of which waited for: 22 -> 22; matrix products, arithmetic and copies ran while one was open for 13% -> 12% of each run, Pallas kernels for 0% -> 5%
where the time goes in v4:
time: 257 us; the launch traced here: 254 us
  starting transfers between devices  107 us (42%)
  waiting for transfers between devices  61 us (24%)
  Pallas kernels  33.5 us (13%)
  other arithmetic  27.9 us (11%)
  between operations  14.7 us (6%)
  local copies, waits for them, and re-layouts  9.45 us (4%)
    ppermute x32, starting transfers between devices, around(): return lax.ppermute(value, ('c', 'z'), pairs)  97 us
    ppermute x32, waiting for transfers between devices, around(): return lax.ppermute(value, ('c', 'z'), pairs)  52.4 us
    convert_element_type x17, other arithmetic, add(): return (a.astype(F32) + b.astype(F32)).astype(BF)  22.5 us
    pallas_call x1, Pallas kernels, expert_grads(): pl.pallas_call(grad_kernel, grid_spec=pltpu.PrefetchScalarGridSpec(num_sc...  16.7 us
    pallas_call x1, Pallas kernels, merge(): pl.pallas_call(merge_kernel, grid=(NX,), in_specs=[pl.BlockSpec((SLOTS, 2...  13.2 us
    ppermute x5, starting transfers between devices, swap(): return lax.ppermute(value, 'c', [(0, 1), (1, 0)])  10.3 us
    ppermute x5, waiting for transfers between devices, swap(): return lax.ppermute(value, 'c', [(0, 1), (1, 0)])  8.55 us
    unnamed x19, local copies, waits for them, and re-layouts  7.66 us
  transfers between devices with their start and end apart: 39, of which 22 were waited for; matrix products, arithmetic and copies ran while one was open for 12% of the time, Pallas kernels for 5%

profile of v4, /device:TPU:6, one launch (start us, length us, event | category | flops | bytes accessed | tf_op | source)
XLA Modules:
  0.0 253.9 jit_solution(13168377431618270462)
XLA Ops:
  17.2 3.8 %collective-permute-start.10 = (bf16[128,1024]{1,0:T(8,128)(2,1)S(1)}, bf16[128,1024]{1,0:T(8,128)(2,1)S(1)}, u32[]{:S(2)}, u32[]{:S(2)}) collective-permute-start(bf16[128,1024]{1,0:T(8,128)(2,1)S(1)} %constant_dynamic-update-slice_fusion.7), channel_id=1, source_target_pairs={{0,1},{1,2},{2,3},{3,4},{4,5},{5,6},{6,7},{7,8},{8,9},{9,10},{10,1... | collective-permute-start | bytes 786440 | tf_op jit(solution)/shard_map/ppermute | solution.py:237
  21.1 3.8 %collective-permute-start.1 = (bf16[128,1152]{1,0:T(8,128)(2,1)S(1)}, bf16[128,1152]{1,0:T(8,128)(2,1)S(1)}, u32[]{:S(2)}, u32[]{:S(2)}) collective-permute-start(bf16[128,1152]{1,0:T(8,128)(2,1)S(1)} %pad_maximum_fusion), channel_id=1, source_target_pairs={{0,1},{1,2},{2,3},{3,4},{4,5},{5,6},{6,7},{7,8},{8,9},{9,10},{10,1... | collective-permute-start | bytes 884744 | tf_op jit(solution)/shard_map/ppermute | solution.py:237
  25.5 7.4 %collective-permute-done.10 = bf16[128,1024]{1,0:T(8,128)(2,1)S(1)} collective-permute-done((bf16[128,1024]{1,0:T(8,128)(2,1)S(1)}, bf16[128,1024]{1,0:T(8,128)(2,1)S(1)}, u32[]{:S(2)}, u32[]{:S(2)}) %collective-permute-start.10) | collective-permute-done | bytes 262176 | tf_op jit(solution)/shard_map/ppermute | solution.py:237
  38.7 3.6 %collective-permute-done.11 = bf16[128,1024]{1,0:T(8,128)(2,1)S(1)} collective-permute-done((bf16[128,1024]{1,0:T(8,128)(2,1)S(1)}, bf16[128,1024]{1,0:T(8,128)(2,1)S(1)}, u32[]{:S(2)}, u32[]{:S(2)}) %collective-permute-start.11) | collective-permute-done | bytes 262176 | tf_op jit(solution)/shard_map/ppermute | solution.py:237
  48.6 3.3 %collective-permute-done.12 = bf16[128,1024]{1,0:T(8,128)(2,1)S(1)} collective-permute-done((bf16[128,1024]{1,0:T(8,128)(2,1)S(1)}, bf16[128,1024]{1,0:T(8,128)(2,1)S(1)}, u32[]{:S(2)}, u32[]{:S(2)}) %collective-permute-start.12) | collective-permute-done | bytes 262176 | tf_op jit(solution)/shard_map/ppermute | solution.py:237
  91.7 3.3 %collective-permute-done.7 = bf16[128,1152]{1,0:T(8,128)(2,1)S(1)} collective-permute-done((bf16[128,1152]{1,0:T(8,128)(2,1)S(1)}, bf16[128,1152]{1,0:T(8,128)(2,1)S(1)}, u32[]{:S(2)}, u32[]{:S(2)}) %collective-permute-start.7) | collective-permute-done | bytes 294944 | tf_op jit(solution)/shard_map/ppermute | solution.py:237
  99.3 5.5 %collective-permute-done.8 = bf16[128,1152]{1,0:T(8,128)(2,1)S(1)} collective-permute-done((bf16[128,1152]{1,0:T(8,128)(2,1)S(1)}, bf16[128,1152]{1,0:T(8,128)(2,1)S(1)}, u32[]{:S(2)}, u32[]{:S(2)}) %collective-permute-start.8) | collective-permute-done | bytes 294944 | tf_op jit(solution)/shard_map/ppermute | solution.py:237
  105.6 16.7 %shard_map.119 = (bf16[4,4,128,1152]{3,2,1,0:T(8,128)(2,1)}, bf16[4,4,128,1152]{3,2,1,0:T(8,128)(2,1)}, bf16[640,768]{1,0:T(8,128)(2,1)}, bf16[640,384]{1,0:T(8,...) custom-call(s32[2]{0:T(128)} %pad_add_fusion.ids_ref, ...), custom_call_target="tpu_custom_call" | custom-call | flops 5704253440 | bytes 26000000 | tf_op jit(solution)/shard_map/pallas_call | solution.py:110
  124.5 7.9 %collective-permute-done.36 = bf16[4,4,128,1152]{3,2,1,0:T(8,128)(2,1)S(1)} collective-permute-done((bf16[4,4,128,1152]{3,2,1,0:T(8,128)(2,1)}, bf16[4,4,128,1152]{3,2,1,0:T(8,128)(2,1)S(1)}, u32[]{:S(2)}, u32[]{:S(2)}) %collective-permute-start.36) | collective-permute-done | bytes 4718624 | tf_op jit(solution)/shard_map/ppermute | solution.py:241
  132.4 6.1 %add_convert_fusion = bf16[4,4,128,1152]{3,2,1,0:T(8,128)(2,1)} fusion(bf16[4,4,128,1152]{3,2,1,0:T(8,128)(2,1)S(1)} %collective-permute-done.36, bf16[4,4,128,1152]{3,2,1,0:T(8,128)(2,1)} %get-tuple-element.23), kind=kLoop, calls=%fused_computation | loop fusion | flops 9437184 | bytes 14155776 | tf_op jit(solution)/shard_map/convert_element_type | solution.py:245
  138.5 13.2 %shard_map.120 = (bf16[1024,1152]{1,0:T(8,128)(2,1)}, bf16[1024,1024]{1,0:T(8,128)(2,1)}) custom-call(bf16[640,768]{1,0:T(8,128)(2,1)} %get-tuple-element.17.act_ref, bf16[640,384]{1,0:T(8,128)(2,1)} %get-tuple-element.18.wh_ref, bf16[640,128]{1,0:T(8,128)(2,1)} %get-tuple-element.19.aux_ref, bf16[640,1024]{1,0:T(8,128)(2,1)} %get-tuple-element.20.sel_ref, ...), custom_call_target="tpu_custom_call" | custom-call | flops 4194304000 | bytes 16000000 | tf_op jit(solution)/shard_map/pallas_call | solution.py:177
  157.5 3.4 %collective-permute-done.27 = bf16[128,1024]{1,0:T(8,128)(2,1)S(1)} collective-permute-done((bf16[128,1024]{1,0:T(8,128)(2,1)S(1)}, bf16[128,1024]{1,0:T(8,128)(2,1)S(1)}, u32[]{:S(2)}, u32[]{:S(2)}) %collective-permute-start.27) | collective-permute-done | bytes 262176 | tf_op jit(solution)/shard_map/ppermute | solution.py:237
  166.1 3.7 %collective-permute-start.19 = (bf16[128,1152]{1,0:T(8,128)(2,1)S(1)}, bf16[128,1152]{1,0:T(8,128)(2,1)S(1)}, u32[]{:S(2)}, u32[]{:S(2)}) collective-permute-start(bf16[128,1152]{1,0:T(8,128)(2,1)S(1)} %add_convert_fusion.8), channel_id=1, source_target_pairs={{0,15},{1,0},{2,1},{3,2},{4,3},{5,4},{6,5},{7,6},{8,7},{9,8},{10,9... | collective-permute-start | bytes 884744 | tf_op jit(solution)/shard_map/ppermute | solution.py:237
  171.2 4.3 %collective-permute-start.29 = (bf16[128,1024]{1,0:T(8,128)(2,1)S(1)}, bf16[128,1024]{1,0:T(8,128)(2,1)S(1)}, u32[]{:S(2)}, u32[]{:S(2)}) collective-permute-start(bf16[128,1024]{1,0:T(8,128)(2,1)S(1)} %add_convert_fusion.15), channel_id=1, source_target_pairs={{0,15},{1,0},{2,1},{3,2},{4,3},{5,4},{6,5},{7,6},{8,7},{9,8},{10,9... | collective-permute-start | bytes 786440 | tf_op jit(solution)/shard_map/ppermute | solution.py:237
  176.6 4.1 %collective-permute-start.20 = (bf16[128,1152]{1,0:T(8,128)(2,1)S(1)}, bf16[128,1152]{1,0:T(8,128)(2,1)S(1)}, u32[]{:S(2)}, u32[]{:S(2)}) collective-permute-start(bf16[128,1152]{1,0:T(8,128)(2,1)S(1)} %add_convert_fusion.7), channel_id=1, source_target_pairs={{0,15},{1,0},{2,1},{3,2},{4,3},{5,4},{6,5},{7,6},{8,7},{9,8},{10,9... | collective-permute-start | bytes 884744 | tf_op jit(solution)/shard_map/ppermute | solution.py:237
  181.7 4.3 %collective-permute-start.30 = (bf16[128,1024]{1,0:T(8,128)(2,1)S(1)}, bf16[128,1024]{1,0:T(8,128)(2,1)S(1)}, u32[]{:S(2)}, u32[]{:S(2)}) collective-permute-start(bf16[128,1024]{1,0:T(8,128)(2,1)S(1)} %add_convert_fusion.14), channel_id=1, source_target_pairs={{0,15},{1,0},{2,1},{3,2},{4,3},{5,4},{6,5},{7,6},{8,7},{9,8},{10,9... | collective-permute-start | bytes 786440 | tf_op jit(solution)/shard_map/ppermute | solution.py:237
  187.1 4.4 %collective-permute-start.21 = (bf16[128,1152]{1,0:T(8,128)(2,1)S(1)}, bf16[128,1152]{1,0:T(8,128)(2,1)S(1)}, u32[]{:S(2)}, u32[]{:S(2)}) collective-permute-start(bf16[128,1152]{1,0:T(8,128)(2,1)S(1)} %add_convert_fusion.6), channel_id=1, source_target_pairs={{0,15},{1,0},{2,1},{3,2},{4,3},{5,4},{6,5},{7,6},{8,7},{9,8},{10,9... | collective-permute-start | bytes 884744 | tf_op jit(solution)/shard_map/ppermute | solution.py:237
  192.6 4.0 %collective-permute-start.31 = (bf16[128,1024]{1,0:T(8,128)(2,1)S(1)}, bf16[128,1024]{1,0:T(8,128)(2,1)S(1)}, u32[]{:S(2)}, u32[]{:S(2)}) collective-permute-start(bf16[128,1024]{1,0:T(8,128)(2,1)S(1)} %add_convert_fusion.13), channel_id=1, source_target_pairs={{0,15},{1,0},{2,1},{3,2},{4,3},{5,4},{6,5},{7,6},{8,7},{9,8},{10,9... | collective-permute-start | bytes 786440 | tf_op jit(solution)/shard_map/ppermute | solution.py:237
  197.6 4.8 %collective-permute-start.22 = (bf16[128,1152]{1,0:T(8,128)(2,1)S(1)}, bf16[128,1152]{1,0:T(8,128)(2,1)S(1)}, u32[]{:S(2)}, u32[]{:S(2)}) collective-permute-start(bf16[128,1152]{1,0:T(8,128)(2,1)S(1)} %add_convert_fusion.5), channel_id=1, source_target_pairs={{0,15},{1,0},{2,1},{3,2},{4,3},{5,4},{6,5},{7,6},{8,7},{9,8},{10,9... | collective-permute-start | bytes 884744 | tf_op jit(solution)/shard_map/ppermute | solution.py:237
  203.4 3.6 %collective-permute-start.32 = (bf16[128,1024]{1,0:T(8,128)(2,1)S(1)}, bf16[128,1024]{1,0:T(8,128)(2,1)S(1)}, u32[]{:S(2)}, u32[]{:S(2)}) collective-permute-start(bf16[128,1024]{1,0:T(8,128)(2,1)S(1)} %add_convert_fusion.12), channel_id=1, source_target_pairs={{0,15},{1,0},{2,1},{3,2},{4,3},{5,4},{6,5},{7,6},{8,7},{9,8},{10,9... | collective-permute-start | bytes 786440 | tf_op jit(solution)/shard_map/ppermute | solution.py:237
  208.1 5.1 %collective-permute-start.23 = (bf16[128,1152]{1,0:T(8,128)(2,1)S(1)}, bf16[128,1152]{1,0:T(8,128)(2,1)S(1)}, u32[]{:S(2)}, u32[]{:S(2)}) collective-permute-start(bf16[128,1152]{1,0:T(8,128)(2,1)S(1)} %add_convert_fusion.4), channel_id=1, source_target_pairs={{0,15},{1,0},{2,1},{3,2},{4,3},{5,4},{6,5},{7,6},{8,7},{9,8},{10,9... | collective-permute-start | bytes 884744 | tf_op jit(solution)/shard_map/ppermute | solution.py:237
  214.3 3.3 %collective-permute-start.33 = (bf16[128,1024]{1,0:T(8,128)(2,1)S(1)}, bf16[128,1024]{1,0:T(8,128)(2,1)S(1)}, u32[]{:S(2)}, u32[]{:S(2)}) collective-permute-start(bf16[128,1024]{1,0:T(8,128)(2,1)S(1)} %add_convert_fusion.11), channel_id=1, source_target_pairs={{0,15},{1,0},{2,1},{3,2},{4,3},{5,4},{6,5},{7,6},{8,7},{9,8},{10,9... | collective-permute-start | bytes 786440 | tf_op jit(solution)/shard_map/ppermute | solution.py:237
  218.6 5.5 %collective-permute-start.24 = (bf16[128,1152]{1,0:T(8,128)(2,1)S(1)}, bf16[128,1152]{1,0:T(8,128)(2,1)S(1)}, u32[]{:S(2)}, u32[]{:S(2)}) collective-permute-start(bf16[128,1152]{1,0:T(8,128)(2,1)S(1)} %add_convert_fusion.3), channel_id=1, source_target_pairs={{0,15},{1,0},{2,1},{3,2},{4,3},{5,4},{6,5},{7,6},{8,7},{9,8},{10,9... | collective-permute-start | bytes 884744 | tf_op jit(solution)/shard_map/ppermute | solution.py:237
  229.4 5.6 %collective-permute-start.25 = (bf16[128,1152]{1,0:T(8,128)(2,1)S(1)}, bf16[128,1152]{1,0:T(8,128)(2,1)S(1)}, u32[]{:S(2)}, u32[]{:S(2)}) collective-permute-start(bf16[128,1152]{1,0:T(8,128)(2,1)S(1)} %add_convert_fusion.2), channel_id=1, source_target_pairs={{0,15},{1,0},{2,1},{3,2},{4,3},{5,4},{6,5},{7,6},{8,7},{9,8},{10,9... | collective-permute-start | bytes 884744 | tf_op jit(solution)/shard_map/ppermute | solution.py:237
  (115 shorter events, 108.3 us)
Async XLA Ops:
  7.2 98.5 %all-gather.2.cloned.1.call-start = ((), (), s32[]{:S(2)}) async-start(), calls=%async_computation.1 | async-start | bytes 9732096 | tf_op jit(solution)/shard_map/all_gather | solution.py:255
  9.0 236.2 %reduce-scatter.2.cloned.1.call-start = ((), (), s32[]{:S(2)}) async-start(), calls=%async_computation.2 | async-start | bytes 5013504 | tf_op jit(solution)/shard_map/reduce_scatter | solution.py:277
  17.2 15.7 %collective-permute-start.10 = (bf16[128,1024]{1,0:T(8,128)(2,1)S(1)}, bf16[128,1024]{1,0:T(8,128)(2,1)S(1)}, u32[]{:S(2)}, u32[]{:S(2)}) collective-permute-start(bf16[128,1024]{1,0:T(8,128)(2,1)S(1)} %constant_dynamic-update-slice_fusion.7), channel_id=1, source_target_pairs={{0,1},{1,2},{2,3},{3,4},{4,5},{5,6},{6,7},{7,8},{8,9},{9,10},{10,1... | collective-permute-start | bytes 786440 | tf_op jit(solution)/shard_map/ppermute | solution.py:237
  21.1 15.0 %collective-permute-start.1 = (bf16[128,1152]{1,0:T(8,128)(2,1)S(1)}, bf16[128,1152]{1,0:T(8,128)(2,1)S(1)}, u32[]{:S(2)}, u32[]{:S(2)}) collective-permute-start(bf16[128,1152]{1,0:T(8,128)(2,1)S(1)} %pad_maximum_fusion), channel_id=1, source_target_pairs={{0,1},{1,2},{2,3},{3,4},{4,5},{5,6},{6,7},{7,8},{8,9},{9,10},{10,1... | collective-permute-start | bytes 884744 | tf_op jit(solution)/shard_map/ppermute | solution.py:237
  36.1 9.8 %collective-permute-start.2 = (bf16[128,1152]{1,0:T(8,128)(2,1)S(1)}, bf16[128,1152]{1,0:T(8,128)(2,1)S(1)}, u32[]{:S(2)}, u32[]{:S(2)}) collective-permute-start(bf16[128,1152]{1,0:T(8,128)(2,1)S(1)} %collective-permute-done.1), channel_id=1, source_target_pairs={{0,1},{1,2},{2,3},{3,4},{4,5},{5,6},{6,7},{7,8},{8,9},{9,10},{10,1... | collective-permute-start | bytes 884744 | tf_op jit(solution)/shard_map/ppermute | solution.py:237
  42.4 9.5 %collective-permute-start.12 = (bf16[128,1024]{1,0:T(8,128)(2,1)S(1)}, bf16[128,1024]{1,0:T(8,128)(2,1)S(1)}, u32[]{:S(2)}, u32[]{:S(2)}) collective-permute-start(bf16[128,1024]{1,0:T(8,128)(2,1)S(1)} %collective-permute-done.11), channel_id=1, source_target_pairs={{0,1},{1,2},{2,3},{3,4},{4,5},{5,6},{6,7},{7,8},{8,9},{9,10},{10,1... | collective-permute-start | bytes 786440 | tf_op jit(solution)/shard_map/ppermute | solution.py:237
  45.9 9.8 %collective-permute-start.3 = (bf16[128,1152]{1,0:T(8,128)(2,1)S(1)}, bf16[128,1152]{1,0:T(8,128)(2,1)S(1)}, u32[]{:S(2)}, u32[]{:S(2)}) collective-permute-start(bf16[128,1152]{1,0:T(8,128)(2,1)S(1)} %collective-permute-done.2), channel_id=1, source_target_pairs={{0,1},{1,2},{2,3},{3,4},{4,5},{5,6},{6,7},{7,8},{8,9},{9,10},{10,1... | collective-permute-start | bytes 884744 | tf_op jit(solution)/shard_map/ppermute | solution.py:237
  51.9 9.5 %collective-permute-start.13 = (bf16[128,1024]{1,0:T(8,128)(2,1)S(1)}, bf16[128,1024]{1,0:T(8,128)(2,1)S(1)}, u32[]{:S(2)}, u32[]{:S(2)}) collective-permute-start(bf16[128,1024]{1,0:T(8,128)(2,1)S(1)} %collective-permute-done.12), channel_id=1, source_target_pairs={{0,1},{1,2},{2,3},{3,4},{4,5},{5,6},{6,7},{7,8},{8,9},{9,10},{10,1... | collective-permute-start | bytes 786440 | tf_op jit(solution)/shard_map/ppermute | solution.py:237
  55.7 9.8 %collective-permute-start.4 = (bf16[128,1152]{1,0:T(8,128)(2,1)S(1)}, bf16[128,1152]{1,0:T(8,128)(2,1)S(1)}, u32[]{:S(2)}, u32[]{:S(2)}) collective-permute-start(bf16[128,1152]{1,0:T(8,128)(2,1)S(1)} %collective-permute-done.3), channel_id=1, source_target_pairs={{0,1},{1,2},{2,3},{3,4},{4,5},{5,6},{6,7},{7,8},{8,9},{9,10},{10,1... | collective-permute-start | bytes 884744 | tf_op jit(solution)/shard_map/ppermute | solution.py:237
  61.3 9.5 %collective-permute-start.14 = (bf16[128,1024]{1,0:T(8,128)(2,1)S(1)}, bf16[128,1024]{1,0:T(8,128)(2,1)S(1)}, u32[]{:S(2)}, u32[]{:S(2)}) collective-permute-start(bf16[128,1024]{1,0:T(8,128)(2,1)S(1)} %collective-permute-done.13), channel_id=1, source_target_pairs={{0,1},{1,2},{2,3},{3,4},{4,5},{5,6},{6,7},{7,8},{8,9},{9,10},{10,1... | collective-permute-start | bytes 786440 | tf_op jit(solution)/shard_map/ppermute | solution.py:237
  65.5 9.8 %collective-permute-start.5 = (bf16[128,1152]{1,0:T(8,128)(2,1)S(1)}, bf16[128,1152]{1,0:T(8,128)(2,1)S(1)}, u32[]{:S(2)}, u32[]{:S(2)}) collective-permute-start(bf16[128,1152]{1,0:T(8,128)(2,1)S(1)} %collective-permute-done.4), channel_id=1, source_target_pairs={{0,1},{1,2},{2,3},{3,4},{4,5},{5,6},{6,7},{7,8},{8,9},{9,10},{10,1... | collective-permute-start | bytes 884744 | tf_op jit(solution)/shard_map/ppermute | solution.py:237
  70.8 9.5 %collective-permute-start.15 = (bf16[128,1024]{1,0:T(8,128)(2,1)S(1)}, bf16[128,1024]{1,0:T(8,128)(2,1)S(1)}, u32[]{:S(2)}, u32[]{:S(2)}) collective-permute-start(bf16[128,1024]{1,0:T(8,128)(2,1)S(1)} %collective-permute-done.14), channel_id=1, source_target_pairs={{0,1},{1,2},{2,3},{3,4},{4,5},{5,6},{6,7},{7,8},{8,9},{9,10},{10,1... | collective-permute-start | bytes 786440 | tf_op jit(solution)/shard_map/ppermute | solution.py:237
  75.3 9.8 %collective-permute-start.6 = (bf16[128,1152]{1,0:T(8,128)(2,1)S(1)}, bf16[128,1152]{1,0:T(8,128)(2,1)S(1)}, u32[]{:S(2)}, u32[]{:S(2)}) collective-permute-start(bf16[128,1152]{1,0:T(8,128)(2,1)S(1)} %collective-permute-done.5), channel_id=1, source_target_pairs={{0,1},{1,2},{2,3},{3,4},{4,5},{5,6},{6,7},{7,8},{8,9},{9,10},{10,1... | collective-permute-start | bytes 884744 | tf_op jit(solution)/shard_map/ppermute | solution.py:237
  85.2 9.8 %collective-permute-start.7 = (bf16[128,1152]{1,0:T(8,128)(2,1)S(1)}, bf16[128,1152]{1,0:T(8,128)(2,1)S(1)}, u32[]{:S(2)}, u32[]{:S(2)}) collective-permute-start(bf16[128,1152]{1,0:T(8,128)(2,1)S(1)} %collective-permute-done.6), channel_id=1, source_target_pairs={{0,1},{1,2},{2,3},{3,4},{4,5},{5,6},{6,7},{7,8},{8,9},{9,10},{10,1... | collective-permute-start | bytes 884744 | tf_op jit(solution)/shard_map/ppermute | solution.py:237
  95.0 9.8 %collective-permute-start.8 = (bf16[128,1152]{1,0:T(8,128)(2,1)S(1)}, bf16[128,1152]{1,0:T(8,128)(2,1)S(1)}, u32[]{:S(2)}, u32[]{:S(2)}) collective-permute-start(bf16[128,1152]{1,0:T(8,128)(2,1)S(1)} %collective-permute-done.7), channel_id=1, source_target_pairs={{0,1},{1,2},{2,3},{3,4},{4,5},{5,6},{6,7},{7,8},{8,9},{9,10},{10,1... | collective-permute-start | bytes 884744 | tf_op jit(solution)/shard_map/ppermute | solution.py:237
  122.4 10.0 %collective-permute-start.36 = (bf16[4,4,128,1152]{3,2,1,0:T(8,128)(2,1)}, bf16[4,4,128,1152]{3,2,1,0:T(8,128)(2,1)S(1)}, u32[]{:S(2)}, u32[]{:S(2)}) collective-permute-start(bf16[4,4,128,1152]{3,2,1,0:T(8,128)(2,1)} %get-tuple-element.24), channel_id=1, source_target_pairs={{0,64},{64,0},{1,65},{65,1},{2,66},{66,2},{3,67},{67,3},{4,68},{68... | collective-permute-start | bytes 14155784 | tf_op jit(solution)/shard_map/ppermute | solution.py:241
  155.6 9.5 %collective-permute-start.18 = (bf16[128,1152]{1,0:T(8,128)(2,1)S(1)}, bf16[128,1152]{1,0:T(8,128)(2,1)S(1)}, u32[]{:S(2)}, u32[]{:S(2)}) collective-permute-start(bf16[128,1152]{1,0:T(8,128)(2,1)S(1)} %broadcast_select_fusion), channel_id=1, source_target_pairs={{0,15},{1,0},{2,1},{3,2},{4,3},{5,4},{6,5},{7,6},{8,7},{9,8},{10,9... | collective-permute-start | bytes 884744 | tf_op jit(solution)/shard_map/ppermute | solution.py:237
  181.7 9.8 %collective-permute-start.30 = (bf16[128,1024]{1,0:T(8,128)(2,1)S(1)}, bf16[128,1024]{1,0:T(8,128)(2,1)S(1)}, u32[]{:S(2)}, u32[]{:S(2)}) collective-permute-start(bf16[128,1024]{1,0:T(8,128)(2,1)S(1)} %add_convert_fusion.14), channel_id=1, source_target_pairs={{0,15},{1,0},{2,1},{3,2},{4,3},{5,4},{6,5},{7,6},{8,7},{9,8},{10,9... | collective-permute-start | bytes 786440 | tf_op jit(solution)/shard_map/ppermute | solution.py:237
  192.6 9.8 %collective-permute-start.31 = (bf16[128,1024]{1,0:T(8,128)(2,1)S(1)}, bf16[128,1024]{1,0:T(8,128)(2,1)S(1)}, u32[]{:S(2)}, u32[]{:S(2)}) collective-permute-start(bf16[128,1024]{1,0:T(8,128)(2,1)S(1)} %add_convert_fusion.13), channel_id=1, source_target_pairs={{0,15},{1,0},{2,1},{3,2},{4,3},{5,4},{6,5},{7,6},{8,7},{9,8},{10,9... | collective-permute-start | bytes 786440 | tf_op jit(solution)/shard_map/ppermute | solution.py:237
  203.4 9.8 %collective-permute-start.32 = (bf16[128,1024]{1,0:T(8,128)(2,1)S(1)}, bf16[128,1024]{1,0:T(8,128)(2,1)S(1)}, u32[]{:S(2)}, u32[]{:S(2)}) collective-permute-start(bf16[128,1024]{1,0:T(8,128)(2,1)S(1)} %add_convert_fusion.12), channel_id=1, source_target_pairs={{0,15},{1,0},{2,1},{3,2},{4,3},{5,4},{6,5},{7,6},{8,7},{9,8},{10,9... | collective-permute-start | bytes 786440 | tf_op jit(solution)/shard_map/ppermute | solution.py:237
  214.3 9.8 %collective-permute-start.33 = (bf16[128,1024]{1,0:T(8,128)(2,1)S(1)}, bf16[128,1024]{1,0:T(8,128)(2,1)S(1)}, u32[]{:S(2)}, u32[]{:S(2)}) collective-permute-start(bf16[128,1024]{1,0:T(8,128)(2,1)S(1)} %add_convert_fusion.11), channel_id=1, source_target_pairs={{0,15},{1,0},{2,1},{3,2},{4,3},{5,4},{6,5},{7,6},{8,7},{9,8},{10,9... | collective-permute-start | bytes 786440 | tf_op jit(solution)/shard_map/ppermute | solution.py:237
  218.6 9.7 %collective-permute-start.24 = (bf16[128,1152]{1,0:T(8,128)(2,1)S(1)}, bf16[128,1152]{1,0:T(8,128)(2,1)S(1)}, u32[]{:S(2)}, u32[]{:S(2)}) collective-permute-start(bf16[128,1152]{1,0:T(8,128)(2,1)S(1)} %add_convert_fusion.3), channel_id=1, source_target_pairs={{0,15},{1,0},{2,1},{3,2},{4,3},{5,4},{6,5},{7,6},{8,7},{9,8},{10,9... | collective-permute-start | bytes 884744 | tf_op jit(solution)/shard_map/ppermute | solution.py:237
  225.2 9.8 %collective-permute-start.34 = (bf16[128,1024]{1,0:T(8,128)(2,1)S(1)}, bf16[128,1024]{1,0:T(8,128)(2,1)S(1)}, u32[]{:S(2)}, u32[]{:S(2)}) collective-permute-start(bf16[128,1024]{1,0:T(8,128)(2,1)S(1)} %add_convert_fusion.10), channel_id=1, source_target_pairs={{0,15},{1,0},{2,1},{3,2},{4,3},{5,4},{6,5},{7,6},{8,7},{9,8},{10,9... | collective-permute-start | bytes 786440 | tf_op jit(solution)/shard_map/ppermute | solution.py:237
  229.4 9.8 %collective-permute-start.25 = (bf16[128,1152]{1,0:T(8,128)(2,1)S(1)}, bf16[128,1152]{1,0:T(8,128)(2,1)S(1)}, u32[]{:S(2)}, u32[]{:S(2)}) collective-permute-start(bf16[128,1152]{1,0:T(8,128)(2,1)S(1)} %add_convert_fusion.2), channel_id=1, source_target_pairs={{0,15},{1,0},{2,1},{3,2},{4,3},{5,4},{6,5},{7,6},{8,7},{9,8},{10,9... | collective-permute-start | bytes 884744 | tf_op jit(solution)/shard_map/ppermute | solution.py:237
  (16 other events, 132.7 us)
Sparse Core Ops, SparseCore 0:
  11.1 74.9 all-gather.1
  138.6 92.4 reduce-scatter.1

commit v5 on v2

--- a/solution.py
+++ b/solution.py
@@ -15,19 +15,22 @@
 SLOTS = NZ * CAP
 AUX = 128
 PLANES = 8
+MERGE = 256
 
 
 def dot(a, b, ca, cb):
     return lax.dot_general(a, b, (((ca,), (cb,)), ((), ())), preferred_element_type=F32)
 
 
-def moe_kernel(ids_ref, xa_ref, xb_ref, wt_ref, keep_ref, send_ref, pa_ref, pb_ref, pos_s, w_s, sel_s, rows_s):
+def moe_kernel(ids_ref, xa_ref, xb_ref, wt_ref, keep_ref, send_ref, pa_ref, pb_ref, pos_s, post_s, w_s, sel_s, xe_s, de_s, rows_s):
     e = pl.program_id(0)
     col = ids_ref[0]
     core = ids_ref[1]
     tok = xa_ref.shape[0]
     feat = xb_ref.shape[1]
     hid = wt_ref.shape[3] // 3
+    slots = NX * SLOTS
+    slot = lax.broadcasted_iota(jnp.int32, (SLOTS, tok), 0)
 
     @pl.when(e == 0)
     def _():
@@ -44,14 +47,23 @@
         for lo in range(0, tok, 128):
             part = live[:, lo : lo + 128]
             rank = dot(part.astype(BF), upper, 1, 0) + before
-            pos_s[:, lo : lo + 128] = jnp.where(part > 0.0, rank, -1.0).astype(jnp.int32)
+            pos = jnp.where(part > 0.0, rank, -float(slots))
+            pos_s[:, lo : lo + 128] = pos.astype(jnp.int32)
+            post_s[lo : lo + 128, :] = pos.T
             before = before + jnp.sum(part, axis=1, keepdims=True)
-
-    picked = pos_s[pl.ds(e, 1), :] == lax.broadcasted_iota(jnp.int32, (SLOTS, tok), 0)
-    sel = jnp.where(picked, 1.0, 0.0).astype(BF)
+        for j in range(NX):
+            hit = pos_s[j : j + 1, :] == slot
+            sel_s[j * SLOTS : (j + 1) * SLOTS, :] = jnp.where(hit, 1.0, 0.0).astype(BF)
+        for lo in range(0, feat, 512):
+            span = slice(lo, lo + 512)
+            xe_s[:, span] = dot(sel_s[...], xa_ref[:, span], 1, 0).astype(BF)
+            de_s[:, span] = dot(sel_s[...], xb_ref[:, span], 1, 0).astype(BF)
+
+    here = pl.ds(pl.multiple_of(e * SLOTS, SLOTS), SLOTS)
+    xe = xe_s[here, :]
+    de = de_s[here, :]
+    picked = pos_s[pl.ds(e, 1), :] == slot
     w = jnp.sum(jnp.where(picked, w_s[pl.ds(e, 1), :], 0.0), axis=1, keepdims=True)
-    xe = dot(sel, xa_ref[:, :feat], 1, 0).astype(BF)
-    de = dot(sel, xb_ref[...], 1, 0).astype(BF)
     wt = wt_ref[:, 0].reshape(feat, 3 * hid)
     gu = dot(xe, wt[:, : 2 * hid], 1, 0)
     hd = dot(de, wt[:, 2 * hid :], 1, 0)
@@ -66,8 +78,6 @@
     gb = (hg * u * s * (1.0 + g * (1.0 - s))).astype(BF)
     ub = (hg * gs).astype(BF)
     act = jnp.concatenate([gb, ub], axis=1)
-    here = pl.ds(pl.multiple_of(e * SLOTS, SLOTS), SLOTS)
-    sel_s[here, :] = sel
     rows_s[here, :feat] = dot(wh, wt[:, 2 * hid :], 1, 1).astype(BF)
     lane = lax.broadcasted_iota(jnp.int32, (SLOTS, AUX), 1)
     mine = col + e
@@ -91,11 +101,19 @@
 
     @pl.when(e == NX - 1)
     def _():
-        for lo in range(0, feat + AUX, 384):
-            pa_ref[:, lo : lo + 384] = dot(sel_s[...], rows_s[:, lo : lo + 384], 0, 0).astype(BF)
-        for lo in range(0, feat, 512):
-            off = feat + AUX + lo
-            pb_ref[:, lo : lo + 512] = dot(sel_s[...], rows_s[:, off : off + 512], 0, 0).astype(BF)
+        @pl.loop(0, tok // MERGE)
+        def _(i):
+            span = pl.ds(pl.multiple_of(i * MERGE, MERGE), MERGE)
+            lane = lax.broadcasted_iota(jnp.int32, (MERGE, slots), 1).astype(F32)
+            sel = jnp.zeros((MERGE, slots), F32)
+            for j in range(NX):
+                sel = jnp.where(post_s[span, j : j + 1] + float(j * SLOTS) == lane, 1.0, sel)
+            sel = sel.astype(BF)
+            for lo in range(0, feat + AUX, 384):
+                pa_ref[span, lo : lo + 384] = dot(sel, rows_s[:, lo : lo + 384], 1, 0).astype(BF)
+            for lo in range(0, feat, 512):
+                off = feat + AUX + lo
+                pb_ref[span, lo : lo + 512] = dot(sel, rows_s[:, off : off + 512], 1, 0).astype(BF)
 
 
 def experts(ids, xa, xb, wt):
@@ -124,8 +142,11 @@
             ],
             scratch_shapes=[
                 pltpu.VMEM((PLANES, tok), jnp.int32),
+                pltpu.VMEM((tok, PLANES), F32),
                 pltpu.VMEM((PLANES, tok), F32),
                 pltpu.VMEM((slots, tok), BF),
+                pltpu.VMEM((slots, feat), BF),
+                pltpu.VMEM((slots, feat), BF),
                 pltpu.VMEM((slots, width), BF),
             ],
         ),
@@ -173,9 +194,10 @@
     )(s)
 
 
-def around(value, sign):
-    pairs = [(z, (z + sign) % NZ) for z in range(NZ)]
-    pairs += [(NZ + z, NZ + (z - sign) % NZ) for z in range(NZ)]
+def around(value, sign, far=False):
+    pairs = [(NZ + z, NZ + (z - sign) % NZ) for z in range(NZ)]
+    if not far:
+        pairs += [(z, (z + sign) % NZ) for z in range(NZ)]
     return lax.ppermute(value, ("c", "z"), pairs)
 
 
@@ -203,13 +225,13 @@
     chain_a = chip_a = jnp.concatenate([own_a, swap(own_a)], axis=0)
     chain_b = chip_b = jnp.concatenate([out_grad, swap(out_grad)], axis=0)
     got_a, got_b = [], []
-    for _ in range(HOPS):
-        chain_a = around(chain_a, 1)
-        chain_b = around(chain_b, 1)
+    for hop in range(1, HOPS + 1):
+        chain_a = around(chain_a, 1, hop == HOPS)
+        chain_b = around(chain_b, 1, hop == HOPS)
         got_a.append(chain_a)
         got_b.append(chain_b)
-    got_a[-1] = jnp.where(core == 0, got_a[-1], chip_a)
-    got_b[-1] = jnp.where(core == 0, got_b[-1], chip_b)
+    got_a[-1] = jnp.where(core == 0, chip_a, got_a[-1])
+    got_b[-1] = jnp.where(core == 0, chip_b, got_b[-1])
     keep, send, pa, pb = experts(
         jnp.stack([z * NX, core]),
         jnp.concatenate(got_a, axis=0),
@@ -225,16 +247,16 @@
         return part[(hop - 1) * pair_rows : hop * pair_rows]
 
     none = jnp.zeros((), BF)
-    chain_a = jnp.where(core == 0, block(pa, HOPS), none)
-    chain_b = jnp.where(core == 0, block(pb, HOPS), none)
+    chain_a = block(pa, HOPS)
+    chain_b = block(pb, HOPS)
     for hop in range(HOPS, 0, -1):
-        chain_a = around(chain_a, -1)
-        chain_b = around(chain_b, -1)
+        chain_a = around(chain_a, -1, hop == HOPS)
+        chain_b = around(chain_b, -1, hop == HOPS)
         if hop > 1:
             chain_a = add(chain_a, block(pa, hop - 1))
             chain_b = add(chain_b, block(pb, hop - 1))
-    chain_a = add(chain_a, jnp.where(core == 0, none, block(pa, HOPS)))
-    chain_b = add(chain_b, jnp.where(core == 0, none, block(pb, HOPS)))
+    chain_a = add(chain_a, jnp.where(core == 0, block(pa, HOPS), none))
+    chain_b = add(chain_b, jnp.where(core == 0, block(pb, HOPS), none))
     total_a = chain_a[:rows].astype(F32) + swap(chain_a[rows:]).astype(F32)
     total_b = chain_b[:rows].astype(F32) + swap(chain_b[rows:]).astype(F32)
     layer_out = total_a[:, :feat].astype(BF)

time: 249 us -> 242 us (0.972)
  starting transfers between devices: 107 us -> 101 us
  waiting for transfers between devices: 61.1 us -> 58.3 us
  local copies, waits for them, and re-layouts: 9.5 us -> 12 us
    ppermute x32, waiting for transfers between devices: 52.3 us -> 44.6 us  [around(): return lax.ppermute(value, ('c', 'z'), pairs)]
    ppermute x32, starting transfers between devices: 97 us -> 89.9 us  [around(): return lax.ppermute(value, ('c', 'z'), pairs)]
    reduce_scatter x1, waiting for transfers between devices: 0.01 us -> 5.27 us  [shards(): lax.psum_scatter(grads.reshape(-1, 3 * hid), ('y', 'x'), scatter_dimensio...]
  transfers between devices with their start and end apart: 39 -> 39, of which waited for: 22 -> 21; matrix products, arithmetic and copies ran while one was open for 13% -> 13% of each run, Pallas kernels for 0% -> 0%
where the time goes in v5:
time: 242 us; the launch traced here: 240 us
  starting transfers between devices  101 us (42%)
  waiting for transfers between devices  58.3 us (24%)
  Pallas kernels  27.9 us (12%)
  other arithmetic  26 us (11%)
  between operations  14.7 us (6%)
  local copies, waits for them, and re-layouts  12 us (5%)
    ppermute x32, starting transfers between devices, around(): return lax.ppermute(value, ('c', 'z'), pairs)  89.9 us
    ppermute x32, waiting for transfers between devices, around(): return lax.ppermute(value, ('c', 'z'), pairs)  44.6 us
    pallas_call x1, Pallas kernels, experts(): pl.pallas_call(moe_kernel, grid_spec=pltpu.PrefetchScalarGridSpec(num_sca...  24.3 us
    convert_element_type x17, other arithmetic, add(): return (a.astype(F32) + b.astype(F32)).astype(BF)  22.5 us
    ppermute x5, starting transfers between devices, swap(): return lax.ppermute(value, 'c', [(0, 1), (1, 0)])  10.8 us
    ppermute x5, waiting for transfers between devices, swap(): return lax.ppermute(value, 'c', [(0, 1), (1, 0)])  8.38 us
    unnamed x19, local copies, waits for them, and re-layouts  8.24 us
    reduce_scatter x1, waiting for transfers between devices, shards(): lax.psum_scatter(grads.reshape(-1, 3 * hid), ('y', 'x'), scatter_dimensio...  5.27 us
  transfers between devices with their start and end apart: 39, of which 21 were waited for; matrix products, arithmetic and copies ran while one was open for 13% of the time, Pallas kernels for 0%

profile of v5, /device:TPU:6, one launch (start us, length us, event | category | flops | bytes accessed | tf_op | source)
XLA Modules:
  0.0 239.6 jit_solution(16274758310673711916)
XLA Ops:
  17.2 3.8 %collective-permute-start.10 = (bf16[128,1024]{1,0:T(8,128)(2,1)S(1)}, bf16[128,1024]{1,0:T(8,128)(2,1)S(1)}, u32[]{:S(2)}, u32[]{:S(2)}) collective-permute-start(bf16[128,1024]{1,0:T(8,128)(2,1)S(1)} %constant_dynamic-update-slice_fusion.7), channel_id=1, source_target_pairs={{64,79},{65,64},{66,65},{67,66},{68,67},{69,68},{70,69},{71,70},{7... | collective-permute-start | bytes 786440 | tf_op jit(solution)/shard_map/ppermute | solution.py:201
  21.1 3.8 %collective-permute-start.1 = (bf16[128,1152]{1,0:T(8,128)(2,1)S(1)}, bf16[128,1152]{1,0:T(8,128)(2,1)S(1)}, u32[]{:S(2)}, u32[]{:S(2)}) collective-permute-start(bf16[128,1152]{1,0:T(8,128)(2,1)S(1)} %pad_maximum_fusion), channel_id=1, source_target_pairs={{64,79},{65,64},{66,65},{67,66},{68,67},{69,68},{70,69},{71,70},{7... | collective-permute-start | bytes 884744 | tf_op jit(solution)/shard_map/ppermute | solution.py:201
  25.5 7.4 %collective-permute-done.10 = bf16[128,1024]{1,0:T(8,128)(2,1)S(1)} collective-permute-done((bf16[128,1024]{1,0:T(8,128)(2,1)S(1)}, bf16[128,1024]{1,0:T(8,128)(2,1)S(1)}, u32[]{:S(2)}, u32[]{:S(2)}) %collective-permute-start.10) | collective-permute-done | bytes 262176 | tf_op jit(solution)/shard_map/ppermute | solution.py:201
  38.7 3.7 %collective-permute-done.11 = bf16[128,1024]{1,0:T(8,128)(2,1)S(1)} collective-permute-done((bf16[128,1024]{1,0:T(8,128)(2,1)S(1)}, bf16[128,1024]{1,0:T(8,128)(2,1)S(1)}, u32[]{:S(2)}, u32[]{:S(2)}) %collective-permute-start.11) | collective-permute-done | bytes 262176 | tf_op jit(solution)/shard_map/ppermute | solution.py:201
  48.6 3.3 %collective-permute-done.12 = bf16[128,1024]{1,0:T(8,128)(2,1)S(1)} collective-permute-done((bf16[128,1024]{1,0:T(8,128)(2,1)S(1)}, bf16[128,1024]{1,0:T(8,128)(2,1)S(1)}, u32[]{:S(2)}, u32[]{:S(2)}) %collective-permute-start.12) | collective-permute-done | bytes 262176 | tf_op jit(solution)/shard_map/ppermute | solution.py:201
  58.4 2.9 %collective-permute-done.13 = bf16[128,1024]{1,0:T(8,128)(2,1)S(1)} collective-permute-done((bf16[128,1024]{1,0:T(8,128)(2,1)S(1)}, bf16[128,1024]{1,0:T(8,128)(2,1)S(1)}, u32[]{:S(2)}, u32[]{:S(2)}) %collective-permute-start.13) | collective-permute-done | bytes 262176 | tf_op jit(solution)/shard_map/ppermute | solution.py:201
  82.2 3.0 %collective-permute-done.6 = bf16[128,1152]{1,0:T(8,128)(2,1)S(1)} collective-permute-done((bf16[128,1152]{1,0:T(8,128)(2,1)S(1)}, bf16[128,1152]{1,0:T(8,128)(2,1)S(1)}, u32[]{:S(2)}, u32[]{:S(2)}) %collective-permute-start.6) | collective-permute-done | bytes 294944 | tf_op jit(solution)/shard_map/ppermute | solution.py:201
  90.4 4.6 %collective-permute-done.7 = bf16[128,1152]{1,0:T(8,128)(2,1)S(1)} collective-permute-done((bf16[128,1152]{1,0:T(8,128)(2,1)S(1)}, bf16[128,1152]{1,0:T(8,128)(2,1)S(1)}, u32[]{:S(2)}, u32[]{:S(2)}) %collective-permute-start.7) | collective-permute-done | bytes 294944 | tf_op jit(solution)/shard_map/ppermute | solution.py:201
  98.0 24.3 %shard_map.119 = (bf16[4,4,128,1152]{3,2,1,0:T(8,128)(2,1)}, bf16[4,4,128,1152]{3,2,1,0:T(8,128)(2,1)}, bf16[1024,1152]{1,0:T(8,128)(2,1)}, bf16[1024,1024]{1,0:T(8,128)(2,1)}) custom-call(s32[2]{0:T(128)} %pad_add_fusion.ids_ref, bf16[1024,1152]{1,0:T(8,128)(2,1)} %select_dynamic-update-slice_fusion.xa_ref, bf16[1024,1024]{1,0:T(8,128)(2,1)} %copy-done, ...), custom_call_target="tpu_custom_call" | custom-call | flops 10234101760 | bytes 30000000 | tf_op jit(solution)/shard_map/pallas_call | solution.py:127
  124.2 8.1 %collective-permute-done.36 = bf16[4,4,128,1152]{3,2,1,0:T(8,128)(2,1)S(1)} collective-permute-done((bf16[4,4,128,1152]{3,2,1,0:T(8,128)(2,1)}, bf16[4,4,128,1152]{3,2,1,0:T(8,128)(2,1)S(1)}, u32[]{:S(2)}, u32[]{:S(2)}) %collective-permute-start.36) | collective-permute-done | bytes 4718624 | tf_op jit(solution)/shard_map/ppermute | solution.py:205
  132.3 6.0 %add_convert_fusion = bf16[4,4,128,1152]{3,2,1,0:T(8,128)(2,1)} fusion(bf16[4,4,128,1152]{3,2,1,0:T(8,128)(2,1)S(1)} %collective-permute-done.36, bf16[4,4,128,1152]{3,2,1,0:T(8,128)(2,1)} %get-tuple-element.15), kind=kLoop, calls=%fused_computation | loop fusion | flops 9437184 | bytes 14155776 | tf_op jit(solution)/shard_map/convert_element_type | solution.py:209
  142.7 4.0 %collective-permute-start.28 = (bf16[128,1024]{1,0:T(8,128)(2,1)S(1)}, bf16[128,1024]{1,0:T(8,128)(2,1)S(1)}, u32[]{:S(2)}, u32[]{:S(2)}) collective-permute-start(bf16[128,1024]{1,0:T(8,128)(2,1)S(1)} %add_convert_fusion.16), channel_id=1, source_target_pairs={{64,65},{65,66},{66,67},{67,68},{68,69},{69,70},{70,71},{71,72},{7... | collective-permute-start | bytes 786440 | tf_op jit(solution)/shard_map/ppermute | solution.py:201
  151.9 5.2 %collective-permute-start.29 = (bf16[128,1024]{1,0:T(8,128)(2,1)S(1)}, bf16[128,1024]{1,0:T(8,128)(2,1)S(1)}, u32[]{:S(2)}, u32[]{:S(2)}) collective-permute-start(bf16[128,1024]{1,0:T(8,128)(2,1)S(1)} %add_convert_fusion.15), channel_id=1, source_target_pairs={{64,65},{65,66},{66,67},{67,68},{68,69},{69,70},{70,71},{71,72},{7... | collective-permute-start | bytes 786440 | tf_op jit(solution)/shard_map/ppermute | solution.py:201
  162.1 5.6 %collective-permute-start.30 = (bf16[128,1024]{1,0:T(8,128)(2,1)S(1)}, bf16[128,1024]{1,0:T(8,128)(2,1)S(1)}, u32[]{:S(2)}, u32[]{:S(2)}) collective-permute-start(bf16[128,1024]{1,0:T(8,128)(2,1)S(1)} %add_convert_fusion.14), channel_id=1, source_target_pairs={{64,65},{65,66},{66,67},{67,68},{68,69},{69,70},{70,71},{71,72},{7... | collective-permute-start | bytes 786440 | tf_op jit(solution)/shard_map/ppermute | solution.py:201
  168.7 2.7 %collective-permute-start.21 = (bf16[128,1152]{1,0:T(8,128)(2,1)S(1)}, bf16[128,1152]{1,0:T(8,128)(2,1)S(1)}, u32[]{:S(2)}, u32[]{:S(2)}) collective-permute-start(bf16[128,1152]{1,0:T(8,128)(2,1)S(1)} %add_convert_fusion.6), channel_id=1, source_target_pairs={{64,65},{65,66},{66,67},{67,68},{68,69},{69,70},{70,71},{71,72},{7... | collective-permute-start | bytes 884744 | tf_op jit(solution)/shard_map/ppermute | solution.py:201
  172.6 5.6 %collective-permute-start.31 = (bf16[128,1024]{1,0:T(8,128)(2,1)S(1)}, bf16[128,1024]{1,0:T(8,128)(2,1)S(1)}, u32[]{:S(2)}, u32[]{:S(2)}) collective-permute-start(bf16[128,1024]{1,0:T(8,128)(2,1)S(1)} %add_convert_fusion.13), channel_id=1, source_target_pairs={{64,65},{65,66},{66,67},{67,68},{68,69},{69,70},{70,71},{71,72},{7... | collective-permute-start | bytes 786440 | tf_op jit(solution)/shard_map/ppermute | solution.py:201
  179.2 3.0 %collective-permute-start.22 = (bf16[128,1152]{1,0:T(8,128)(2,1)S(1)}, bf16[128,1152]{1,0:T(8,128)(2,1)S(1)}, u32[]{:S(2)}, u32[]{:S(2)}) collective-permute-start(bf16[128,1152]{1,0:T(8,128)(2,1)S(1)} %add_convert_fusion.5), channel_id=1, source_target_pairs={{64,65},{65,66},{66,67},{67,68},{68,69},{69,70},{70,71},{71,72},{7... | collective-permute-start | bytes 884744 | tf_op jit(solution)/shard_map/ppermute | solution.py:201
  183.3 5.4 %collective-permute-start.32 = (bf16[128,1024]{1,0:T(8,128)(2,1)S(1)}, bf16[128,1024]{1,0:T(8,128)(2,1)S(1)}, u32[]{:S(2)}, u32[]{:S(2)}) collective-permute-start(bf16[128,1024]{1,0:T(8,128)(2,1)S(1)} %add_convert_fusion.12), channel_id=1, source_target_pairs={{64,65},{65,66},{66,67},{67,68},{68,69},{69,70},{70,71},{71,72},{7... | collective-permute-start | bytes 786440 | tf_op jit(solution)/shard_map/ppermute | solution.py:201
  189.7 3.4 %collective-permute-start.23 = (bf16[128,1152]{1,0:T(8,128)(2,1)S(1)}, bf16[128,1152]{1,0:T(8,128)(2,1)S(1)}, u32[]{:S(2)}, u32[]{:S(2)}) collective-permute-start(bf16[128,1152]{1,0:T(8,128)(2,1)S(1)} %add_convert_fusion.4), channel_id=1, source_target_pairs={{64,65},{65,66},{66,67},{67,68},{68,69},{69,70},{70,71},{71,72},{7... | collective-permute-start | bytes 884744 | tf_op jit(solution)/shard_map/ppermute | solution.py:201
  194.2 5.0 %collective-permute-start.33 = (bf16[128,1024]{1,0:T(8,128)(2,1)S(1)}, bf16[128,1024]{1,0:T(8,128)(2,1)S(1)}, u32[]{:S(2)}, u32[]{:S(2)}) collective-permute-start(bf16[128,1024]{1,0:T(8,128)(2,1)S(1)} %add_convert_fusion.11), channel_id=1, source_target_pairs={{64,65},{65,66},{66,67},{67,68},{68,69},{69,70},{70,71},{71,72},{7... | collective-permute-start | bytes 786440 | tf_op jit(solution)/shard_map/ppermute | solution.py:201
  200.2 3.8 %collective-permute-start.24 = (bf16[128,1152]{1,0:T(8,128)(2,1)S(1)}, bf16[128,1152]{1,0:T(8,128)(2,1)S(1)}, u32[]{:S(2)}, u32[]{:S(2)}) collective-permute-start(bf16[128,1152]{1,0:T(8,128)(2,1)S(1)} %add_convert_fusion.3), channel_id=1, source_target_pairs={{64,65},{65,66},{66,67},{67,68},{68,69},{69,70},{70,71},{71,72},{7... | collective-permute-start | bytes 884744 | tf_op jit(solution)/shard_map/ppermute | solution.py:201
  205.0 4.6 %collective-permute-start.34 = (bf16[128,1024]{1,0:T(8,128)(2,1)S(1)}, bf16[128,1024]{1,0:T(8,128)(2,1)S(1)}, u32[]{:S(2)}, u32[]{:S(2)}) collective-permute-start(bf16[128,1024]{1,0:T(8,128)(2,1)S(1)} %add_convert_fusion.10), channel_id=1, source_target_pairs={{64,65},{65,66},{66,67},{67,68},{68,69},{69,70},{70,71},{71,72},{7... | collective-permute-start | bytes 786440 | tf_op jit(solution)/shard_map/ppermute | solution.py:201
  210.7 4.1 %collective-permute-start.25 = (bf16[128,1152]{1,0:T(8,128)(2,1)S(1)}, bf16[128,1152]{1,0:T(8,128)(2,1)S(1)}, u32[]{:S(2)}, u32[]{:S(2)}) collective-permute-start(bf16[128,1152]{1,0:T(8,128)(2,1)S(1)} %add_convert_fusion.2), channel_id=1, source_target_pairs={{64,65},{65,66},{66,67},{67,68},{68,69},{69,70},{70,71},{71,72},{7... | collective-permute-start | bytes 884744 | tf_op jit(solution)/shard_map/ppermute | solution.py:201
  225.7 5.3 %reduce-scatter.2.cloned.1.call-done.s_ref = bf16[128,1152]{1,0:T(8,128)(2,1)} async-done(((bf16[2048,1152]{1,0:T(8,128)(2,1)}), bf16[128,1152]{1,0:T(8,128)(2,1)}) %reduce-scatter.2.cloned.1.call-update) | async-done | bytes 294928 | tf_op jit(solution)/shard_map/reduce_scatter | solution.py:242
  (114 shorter events, 96.4 us)
Async XLA Ops:
  7.2 90.3 %all-gather.2.cloned.1.call-start = ((), (), s32[]{:S(2)}) async-start(), calls=%async_computation.1 | async-start | bytes 9732096 | tf_op jit(solution)/shard_map/all_gather | solution.py:219
  9.0 221.9 %reduce-scatter.2.cloned.1.call-start = ((), (), s32[]{:S(2)}) async-start(), calls=%async_computation.2 | async-start | bytes 5013504 | tf_op jit(solution)/shard_map/reduce_scatter | solution.py:242
  17.2 15.7 %collective-permute-start.10 = (bf16[128,1024]{1,0:T(8,128)(2,1)S(1)}, bf16[128,1024]{1,0:T(8,128)(2,1)S(1)}, u32[]{:S(2)}, u32[]{:S(2)}) collective-permute-start(bf16[128,1024]{1,0:T(8,128)(2,1)S(1)} %constant_dynamic-update-slice_fusion.7), channel_id=1, source_target_pairs={{64,79},{65,64},{66,65},{67,66},{68,67},{69,68},{70,69},{71,70},{7... | collective-permute-start | bytes 786440 | tf_op jit(solution)/shard_map/ppermute | solution.py:201
  21.1 15.0 %collective-permute-start.1 = (bf16[128,1152]{1,0:T(8,128)(2,1)S(1)}, bf16[128,1152]{1,0:T(8,128)(2,1)S(1)}, u32[]{:S(2)}, u32[]{:S(2)}) collective-permute-start(bf16[128,1152]{1,0:T(8,128)(2,1)S(1)} %pad_maximum_fusion), channel_id=1, source_target_pairs={{64,79},{65,64},{66,65},{67,66},{68,67},{69,68},{70,69},{71,70},{7... | collective-permute-start | bytes 884744 | tf_op jit(solution)/shard_map/ppermute | solution.py:201
  32.9 9.5 %collective-permute-start.11 = (bf16[128,1024]{1,0:T(8,128)(2,1)S(1)}, bf16[128,1024]{1,0:T(8,128)(2,1)S(1)}, u32[]{:S(2)}, u32[]{:S(2)}) collective-permute-start(bf16[128,1024]{1,0:T(8,128)(2,1)S(1)} %collective-permute-done.10), channel_id=1, source_target_pairs={{64,79},{65,64},{66,65},{67,66},{68,67},{69,68},{70,69},{71,70},{7... | collective-permute-start | bytes 786440 | tf_op jit(solution)/shard_map/ppermute | solution.py:201
  36.1 9.8 %collective-permute-start.2 = (bf16[128,1152]{1,0:T(8,128)(2,1)S(1)}, bf16[128,1152]{1,0:T(8,128)(2,1)S(1)}, u32[]{:S(2)}, u32[]{:S(2)}) collective-permute-start(bf16[128,1152]{1,0:T(8,128)(2,1)S(1)} %collective-permute-done.1), channel_id=1, source_target_pairs={{64,79},{65,64},{66,65},{67,66},{68,67},{69,68},{70,69},{71,70},{7... | collective-permute-start | bytes 884744 | tf_op jit(solution)/shard_map/ppermute | solution.py:201
  42.4 9.5 %collective-permute-start.12 = (bf16[128,1024]{1,0:T(8,128)(2,1)S(1)}, bf16[128,1024]{1,0:T(8,128)(2,1)S(1)}, u32[]{:S(2)}, u32[]{:S(2)}) collective-permute-start(bf16[128,1024]{1,0:T(8,128)(2,1)S(1)} %collective-permute-done.11), channel_id=1, source_target_pairs={{64,79},{65,64},{66,65},{67,66},{68,67},{69,68},{70,69},{71,70},{7... | collective-permute-start | bytes 786440 | tf_op jit(solution)/shard_map/ppermute | solution.py:201
  45.9 9.8 %collective-permute-start.3 = (bf16[128,1152]{1,0:T(8,128)(2,1)S(1)}, bf16[128,1152]{1,0:T(8,128)(2,1)S(1)}, u32[]{:S(2)}, u32[]{:S(2)}) collective-permute-start(bf16[128,1152]{1,0:T(8,128)(2,1)S(1)} %collective-permute-done.2), channel_id=1, source_target_pairs={{64,79},{65,64},{66,65},{67,66},{68,67},{69,68},{70,69},{71,70},{7... | collective-permute-start | bytes 884744 | tf_op jit(solution)/shard_map/ppermute | solution.py:201
  51.9 9.5 %collective-permute-start.13 = (bf16[128,1024]{1,0:T(8,128)(2,1)S(1)}, bf16[128,1024]{1,0:T(8,128)(2,1)S(1)}, u32[]{:S(2)}, u32[]{:S(2)}) collective-permute-start(bf16[128,1024]{1,0:T(8,128)(2,1)S(1)} %collective-permute-done.12), channel_id=1, source_target_pairs={{64,79},{65,64},{66,65},{67,66},{68,67},{69,68},{70,69},{71,70},{7... | collective-permute-start | bytes 786440 | tf_op jit(solution)/shard_map/ppermute | solution.py:201
  55.7 9.8 %collective-permute-start.4 = (bf16[128,1152]{1,0:T(8,128)(2,1)S(1)}, bf16[128,1152]{1,0:T(8,128)(2,1)S(1)}, u32[]{:S(2)}, u32[]{:S(2)}) collective-permute-start(bf16[128,1152]{1,0:T(8,128)(2,1)S(1)} %collective-permute-done.3), channel_id=1, source_target_pairs={{64,79},{65,64},{66,65},{67,66},{68,67},{69,68},{70,69},{71,70},{7... | collective-permute-start | bytes 884744 | tf_op jit(solution)/shard_map/ppermute | solution.py:201
  61.3 9.5 %collective-permute-start.14 = (bf16[128,1024]{1,0:T(8,128)(2,1)S(1)}, bf16[128,1024]{1,0:T(8,128)(2,1)S(1)}, u32[]{:S(2)}, u32[]{:S(2)}) collective-permute-start(bf16[128,1024]{1,0:T(8,128)(2,1)S(1)} %collective-permute-done.13), channel_id=1, source_target_pairs={{64,79},{65,64},{66,65},{67,66},{68,67},{69,68},{70,69},{71,70},{7... | collective-permute-start | bytes 786440 | tf_op jit(solution)/shard_map/ppermute | solution.py:201
  65.5 9.8 %collective-permute-start.5 = (bf16[128,1152]{1,0:T(8,128)(2,1)S(1)}, bf16[128,1152]{1,0:T(8,128)(2,1)S(1)}, u32[]{:S(2)}, u32[]{:S(2)}) collective-permute-start(bf16[128,1152]{1,0:T(8,128)(2,1)S(1)} %collective-permute-done.4), channel_id=1, source_target_pairs={{64,79},{65,64},{66,65},{67,66},{68,67},{69,68},{70,69},{71,70},{7... | collective-permute-start | bytes 884744 | tf_op jit(solution)/shard_map/ppermute | solution.py:201
  70.8 9.5 %collective-permute-start.15 = (bf16[128,1024]{1,0:T(8,128)(2,1)S(1)}, bf16[128,1024]{1,0:T(8,128)(2,1)S(1)}, u32[]{:S(2)}, u32[]{:S(2)}) collective-permute-start(bf16[128,1024]{1,0:T(8,128)(2,1)S(1)} %collective-permute-done.14), channel_id=1, source_target_pairs={{64,79},{65,64},{66,65},{67,66},{68,67},{69,68},{70,69},{71,70},{7... | collective-permute-start | bytes 786440 | tf_op jit(solution)/shard_map/ppermute | solution.py:201
  75.4 9.8 %collective-permute-start.6 = (bf16[128,1152]{1,0:T(8,128)(2,1)S(1)}, bf16[128,1152]{1,0:T(8,128)(2,1)S(1)}, u32[]{:S(2)}, u32[]{:S(2)}) collective-permute-start(bf16[128,1152]{1,0:T(8,128)(2,1)S(1)} %collective-permute-done.5), channel_id=1, source_target_pairs={{64,79},{65,64},{66,65},{67,66},{68,67},{69,68},{70,69},{71,70},{7... | collective-permute-start | bytes 884744 | tf_op jit(solution)/shard_map/ppermute | solution.py:201
  80.3 9.5 %collective-permute-start.16 = (bf16[128,1024]{1,0:T(8,128)(2,1)S(1)}, bf16[128,1024]{1,0:T(8,128)(2,1)S(1)}, u32[]{:S(2)}, u32[]{:S(2)}) collective-permute-start(bf16[128,1024]{1,0:T(8,128)(2,1)S(1)} %collective-permute-done.15), channel_id=1, source_target_pairs={{64,79},{65,64},{66,65},{67,66},{68,67},{69,68},{70,69},{71,70},{7... | collective-permute-start | bytes 786440 | tf_op jit(solution)/shard_map/ppermute | solution.py:201
  85.2 9.8 %collective-permute-start.7 = (bf16[128,1152]{1,0:T(8,128)(2,1)S(1)}, bf16[128,1152]{1,0:T(8,128)(2,1)S(1)}, u32[]{:S(2)}, u32[]{:S(2)}) collective-permute-start(bf16[128,1152]{1,0:T(8,128)(2,1)S(1)} %collective-permute-done.6), channel_id=1, source_target_pairs={{64,79},{65,64},{66,65},{67,66},{68,67},{69,68},{70,69},{71,70},{7... | collective-permute-start | bytes 884744 | tf_op jit(solution)/shard_map/ppermute | solution.py:201
  122.3 10.0 %collective-permute-start.36 = (bf16[4,4,128,1152]{3,2,1,0:T(8,128)(2,1)}, bf16[4,4,128,1152]{3,2,1,0:T(8,128)(2,1)S(1)}, u32[]{:S(2)}, u32[]{:S(2)}) collective-permute-start(bf16[4,4,128,1152]{3,2,1,0:T(8,128)(2,1)} %get-tuple-element.16), channel_id=1, source_target_pairs={{0,64},{64,0},{1,65},{65,1},{2,66},{66,2},{3,67},{67,3},{4,68},{68... | collective-permute-start | bytes 14155784 | tf_op jit(solution)/shard_map/ppermute | solution.py:205
  147.7 9.5 %collective-permute-start.19 = (bf16[128,1152]{1,0:T(8,128)(2,1)S(1)}, bf16[128,1152]{1,0:T(8,128)(2,1)S(1)}, u32[]{:S(2)}, u32[]{:S(2)}) collective-permute-start(bf16[128,1152]{1,0:T(8,128)(2,1)S(1)} %add_convert_fusion.8), channel_id=1, source_target_pairs={{64,65},{65,66},{66,67},{67,68},{68,69},{69,70},{70,71},{71,72},{7... | collective-permute-start | bytes 884744 | tf_op jit(solution)/shard_map/ppermute | solution.py:201
  162.1 9.5 %collective-permute-start.30 = (bf16[128,1024]{1,0:T(8,128)(2,1)S(1)}, bf16[128,1024]{1,0:T(8,128)(2,1)S(1)}, u32[]{:S(2)}, u32[]{:S(2)}) collective-permute-start(bf16[128,1024]{1,0:T(8,128)(2,1)S(1)} %add_convert_fusion.14), channel_id=1, source_target_pairs={{64,65},{65,66},{66,67},{67,68},{68,69},{69,70},{70,71},{71,72},{7... | collective-permute-start | bytes 786440 | tf_op jit(solution)/shard_map/ppermute | solution.py:201
  172.6 9.7 %collective-permute-start.31 = (bf16[128,1024]{1,0:T(8,128)(2,1)S(1)}, bf16[128,1024]{1,0:T(8,128)(2,1)S(1)}, u32[]{:S(2)}, u32[]{:S(2)}) collective-permute-start(bf16[128,1024]{1,0:T(8,128)(2,1)S(1)} %add_convert_fusion.13), channel_id=1, source_target_pairs={{64,65},{65,66},{66,67},{67,68},{68,69},{69,70},{70,71},{71,72},{7... | collective-permute-start | bytes 786440 | tf_op jit(solution)/shard_map/ppermute | solution.py:201
  183.3 9.8 %collective-permute-start.32 = (bf16[128,1024]{1,0:T(8,128)(2,1)S(1)}, bf16[128,1024]{1,0:T(8,128)(2,1)S(1)}, u32[]{:S(2)}, u32[]{:S(2)}) collective-permute-start(bf16[128,1024]{1,0:T(8,128)(2,1)S(1)} %add_convert_fusion.12), channel_id=1, source_target_pairs={{64,65},{65,66},{66,67},{67,68},{68,69},{69,70},{70,71},{71,72},{7... | collective-permute-start | bytes 786440 | tf_op jit(solution)/shard_map/ppermute | solution.py:201
  189.7 9.5 %collective-permute-start.23 = (bf16[128,1152]{1,0:T(8,128)(2,1)S(1)}, bf16[128,1152]{1,0:T(8,128)(2,1)S(1)}, u32[]{:S(2)}, u32[]{:S(2)}) collective-permute-start(bf16[128,1152]{1,0:T(8,128)(2,1)S(1)} %add_convert_fusion.4), channel_id=1, source_target_pairs={{64,65},{65,66},{66,67},{67,68},{68,69},{69,70},{70,71},{71,72},{7... | collective-permute-start | bytes 884744 | tf_op jit(solution)/shard_map/ppermute | solution.py:201
  194.2 9.8 %collective-permute-start.33 = (bf16[128,1024]{1,0:T(8,128)(2,1)S(1)}, bf16[128,1024]{1,0:T(8,128)(2,1)S(1)}, u32[]{:S(2)}, u32[]{:S(2)}) collective-permute-start(bf16[128,1024]{1,0:T(8,128)(2,1)S(1)} %add_convert_fusion.11), channel_id=1, source_target_pairs={{64,65},{65,66},{66,67},{67,68},{68,69},{69,70},{70,71},{71,72},{7... | collective-permute-start | bytes 786440 | tf_op jit(solution)/shard_map/ppermute | solution.py:201
  205.0 9.8 %collective-permute-start.34 = (bf16[128,1024]{1,0:T(8,128)(2,1)S(1)}, bf16[128,1024]{1,0:T(8,128)(2,1)S(1)}, u32[]{:S(2)}, u32[]{:S(2)}) collective-permute-start(bf16[128,1024]{1,0:T(8,128)(2,1)S(1)} %add_convert_fusion.10), channel_id=1, source_target_pairs={{64,65},{65,66},{66,67},{67,68},{68,69},{69,70},{70,71},{71,72},{7... | collective-permute-start | bytes 786440 | tf_op jit(solution)/shard_map/ppermute | solution.py:201
  (16 other events, 107.6 us)
Sparse Core Ops, SparseCore 0:
  11.1 74.9 all-gather.1
  138.4 92.5 reduce-scatter.1

commit v6 on v5

--- a/solution.py
+++ b/solution.py
@@ -15,14 +15,14 @@
 SLOTS = NZ * CAP
 AUX = 128
 PLANES = 8
-MERGE = 256
+MERGE = 64
 
 
 def dot(a, b, ca, cb):
     return lax.dot_general(a, b, (((ca,), (cb,)), ((), ())), preferred_element_type=F32)
 
 
-def moe_kernel(ids_ref, xa_ref, xb_ref, wt_ref, keep_ref, send_ref, pa_ref, pb_ref, pos_s, post_s, w_s, sel_s, xe_s, de_s, rows_s):
+def moe_kernel(ids_ref, xa_ref, xb_ref, wt_ref, keep_ref, send_ref, pa_ref, pb_ref, pos_s, post_s, w_s, sel_s, selt_s, xe_s, de_s, rows_s):
     e = pl.program_id(0)
     col = ids_ref[0]
     core = ids_ref[1]
@@ -99,21 +99,23 @@
     send_ref[:, 0, :, : 2 * hid] = dot(xs, act, 0, 0).astype(BF).reshape(NY, step, 2 * hid)
     send_ref[:, 0, :, 2 * hid :] = dot(ds, wh, 0, 0).astype(BF).reshape(NY, step, hid)
 
+    quarter = tok // NX
+    for part in range(0, quarter, MERGE):
+        span = pl.ds(pl.multiple_of(e * quarter + part, MERGE), MERGE)
+        lane = lax.broadcasted_iota(jnp.int32, (MERGE, slots), 1).astype(F32)
+        sel = jnp.zeros((MERGE, slots), F32)
+        for j in range(NX):
+            sel = jnp.where(post_s[span, j : j + 1] + float(j * SLOTS) == lane, 1.0, sel)
+        selt_s[span, :] = sel.astype(BF)
+
     @pl.when(e == NX - 1)
     def _():
-        @pl.loop(0, tok // MERGE)
-        def _(i):
-            span = pl.ds(pl.multiple_of(i * MERGE, MERGE), MERGE)
-            lane = lax.broadcasted_iota(jnp.int32, (MERGE, slots), 1).astype(F32)
-            sel = jnp.zeros((MERGE, slots), F32)
-            for j in range(NX):
-                sel = jnp.where(post_s[span, j : j + 1] + float(j * SLOTS) == lane, 1.0, sel)
-            sel = sel.astype(BF)
-            for lo in range(0, feat + AUX, 384):
-                pa_ref[span, lo : lo + 384] = dot(sel, rows_s[:, lo : lo + 384], 1, 0).astype(BF)
-            for lo in range(0, feat, 512):
-                off = feat + AUX + lo
-                pb_ref[span, lo : lo + 512] = dot(sel, rows_s[:, off : off + 512], 1, 0).astype(BF)
+        for lo, hi in ((0, feat // 2), (feat // 2, feat), (feat, feat + AUX)):
+            pa_ref[:, lo:hi] = dot(selt_s[...], rows_s[:, lo:hi], 1, 0).astype(BF)
+        for lo in range(0, feat, feat // 2):
+            off = feat + AUX + lo
+            rows = rows_s[:, off : off + feat // 2]
+            pb_ref[:, lo : lo + feat // 2] = dot(selt_s[...], rows, 1, 0).astype(BF)
 
 
 def experts(ids, xa, xb, wt):
@@ -145,6 +147,7 @@
                 pltpu.VMEM((tok, PLANES), F32),
                 pltpu.VMEM((PLANES, tok), F32),
                 pltpu.VMEM((slots, tok), BF),
+                pltpu.VMEM((tok, slots), BF),
                 pltpu.VMEM((slots, feat), BF),
                 pltpu.VMEM((slots, feat), BF),
                 pltpu.VMEM((slots, width), BF),

time: 242 us -> 240 us (level)
  transfers between devices with their start and end apart: 39 -> 39, of which waited for: 21 -> 20; matrix products, arithmetic and copies ran while one was open for 13% -> 13% of each run, Pallas kernels for 0% -> 0%
where the time goes in v6:
time: 240 us; the launch traced here: 238 us
  starting transfers between devices  101 us (42%)
  waiting for transfers between devices  57.6 us (24%)
  Pallas kernels  26.5 us (11%)
  other arithmetic  26 us (11%)
  between operations  14.7 us (6%)
  local copies, waits for them, and re-layouts  12 us (5%)
    ppermute x32, starting transfers between devices, around(): return lax.ppermute(value, ('c', 'z'), pairs)  90.6 us
    ppermute x32, waiting for transfers between devices, around(): return lax.ppermute(value, ('c', 'z'), pairs)  43.9 us
    pallas_call x1, Pallas kernels, experts(): pl.pallas_call(moe_kernel, grid_spec=pltpu.PrefetchScalarGridSpec(num_sca...  22.9 us
    convert_element_type x17, other arithmetic, add(): return (a.astype(F32) + b.astype(F32)).astype(BF)  22.5 us
    ppermute x5, starting transfers between devices, swap(): return lax.ppermute(value, 'c', [(0, 1), (1, 0)])  10.7 us
    ppermute x5, waiting for transfers between devices, swap(): return lax.ppermute(value, 'c', [(0, 1), (1, 0)])  8.38 us
    unnamed x19, local copies, waits for them, and re-layouts  8.24 us
    reduce_scatter x1, waiting for transfers between devices, shards(): lax.psum_scatter(grads.reshape(-1, 3 * hid), ('y', 'x'), scatter_dimensio...  5.25 us
  transfers between devices with their start and end apart: 39, of which 20 were waited for; matrix products, arithmetic and copies ran while one was open for 13% of the time, Pallas kernels for 0%

profile of v6, /device:TPU:6, one launch (start us, length us, event | category | flops | bytes accessed | tf_op | source)
XLA Modules:
  0.0 238.2 jit_solution(6237307378455845513)
XLA Ops:
  17.2 3.8 %collective-permute-start.10 = (bf16[128,1024]{1,0:T(8,128)(2,1)S(1)}, bf16[128,1024]{1,0:T(8,128)(2,1)S(1)}, u32[]{:S(2)}, u32[]{:S(2)}) collective-permute-start(bf16[128,1024]{1,0:T(8,128)(2,1)S(1)} %constant_dynamic-update-slice_fusion.7), channel_id=1, source_target_pairs={{64,79},{65,64},{66,65},{67,66},{68,67},{69,68},{70,69},{71,70},{7... | collective-permute-start | bytes 786440 | tf_op jit(solution)/shard_map/ppermute | solution.py:204
  21.1 3.8 %collective-permute-start.1 = (bf16[128,1152]{1,0:T(8,128)(2,1)S(1)}, bf16[128,1152]{1,0:T(8,128)(2,1)S(1)}, u32[]{:S(2)}, u32[]{:S(2)}) collective-permute-start(bf16[128,1152]{1,0:T(8,128)(2,1)S(1)} %pad_maximum_fusion), channel_id=1, source_target_pairs={{64,79},{65,64},{66,65},{67,66},{68,67},{69,68},{70,69},{71,70},{7... | collective-permute-start | bytes 884744 | tf_op jit(solution)/shard_map/ppermute | solution.py:204
  25.5 7.4 %collective-permute-done.10 = bf16[128,1024]{1,0:T(8,128)(2,1)S(1)} collective-permute-done((bf16[128,1024]{1,0:T(8,128)(2,1)S(1)}, bf16[128,1024]{1,0:T(8,128)(2,1)S(1)}, u32[]{:S(2)}, u32[]{:S(2)}) %collective-permute-start.10) | collective-permute-done | bytes 262176 | tf_op jit(solution)/shard_map/ppermute | solution.py:204
  38.7 3.7 %collective-permute-done.11 = bf16[128,1024]{1,0:T(8,128)(2,1)S(1)} collective-permute-done((bf16[128,1024]{1,0:T(8,128)(2,1)S(1)}, bf16[128,1024]{1,0:T(8,128)(2,1)S(1)}, u32[]{:S(2)}, u32[]{:S(2)}) %collective-permute-start.11) | collective-permute-done | bytes 262176 | tf_op jit(solution)/shard_map/ppermute | solution.py:204
  48.6 3.3 %collective-permute-done.12 = bf16[128,1024]{1,0:T(8,128)(2,1)S(1)} collective-permute-done((bf16[128,1024]{1,0:T(8,128)(2,1)S(1)}, bf16[128,1024]{1,0:T(8,128)(2,1)S(1)}, u32[]{:S(2)}, u32[]{:S(2)}) %collective-permute-start.12) | collective-permute-done | bytes 262176 | tf_op jit(solution)/shard_map/ppermute | solution.py:204
  58.4 2.9 %collective-permute-done.13 = bf16[128,1024]{1,0:T(8,128)(2,1)S(1)} collective-permute-done((bf16[128,1024]{1,0:T(8,128)(2,1)S(1)}, bf16[128,1024]{1,0:T(8,128)(2,1)S(1)}, u32[]{:S(2)}, u32[]{:S(2)}) %collective-permute-start.13) | collective-permute-done | bytes 262176 | tf_op jit(solution)/shard_map/ppermute | solution.py:204
  82.2 3.0 %collective-permute-done.6 = bf16[128,1152]{1,0:T(8,128)(2,1)S(1)} collective-permute-done((bf16[128,1152]{1,0:T(8,128)(2,1)S(1)}, bf16[128,1152]{1,0:T(8,128)(2,1)S(1)}, u32[]{:S(2)}, u32[]{:S(2)}) %collective-permute-start.6) | collective-permute-done | bytes 294944 | tf_op jit(solution)/shard_map/ppermute | solution.py:204
  90.4 4.6 %collective-permute-done.7 = bf16[128,1152]{1,0:T(8,128)(2,1)S(1)} collective-permute-done((bf16[128,1152]{1,0:T(8,128)(2,1)S(1)}, bf16[128,1152]{1,0:T(8,128)(2,1)S(1)}, u32[]{:S(2)}, u32[]{:S(2)}) %collective-permute-start.7) | collective-permute-done | bytes 294944 | tf_op jit(solution)/shard_map/ppermute | solution.py:204
  98.0 22.9 %shard_map.119 = (bf16[4,4,128,1152]{3,2,1,0:T(8,128)(2,1)}, bf16[4,4,128,1152]{3,2,1,0:T(8,128)(2,1)}, bf16[1024,1152]{1,0:T(8,128)(2,1)}, bf16[1024,1024]{1,0:T(8,128)(2,1)}) custom-call(s32[2]{0:T(128)} %pad_add_fusion.ids_ref, bf16[1024,1152]{1,0:T(8,128)(2,1)} %select_dynamic-update-slice_fusion.xa_ref, bf16[1024,1024]{1,0:T(8,128)(2,1)} %copy-done, ...), custom_call_target="tpu_custom_call" | custom-call | flops 10234101760 | bytes 30000000 | tf_op jit(solution)/shard_map/pallas_call | solution.py:129
  122.8 8.1 %collective-permute-done.36 = bf16[4,4,128,1152]{3,2,1,0:T(8,128)(2,1)S(1)} collective-permute-done((bf16[4,4,128,1152]{3,2,1,0:T(8,128)(2,1)}, bf16[4,4,128,1152]{3,2,1,0:T(8,128)(2,1)S(1)}, u32[]{:S(2)}, u32[]{:S(2)}) %collective-permute-start.36) | collective-permute-done | bytes 4718624 | tf_op jit(solution)/shard_map/ppermute | solution.py:208
  130.9 6.0 %add_convert_fusion = bf16[4,4,128,1152]{3,2,1,0:T(8,128)(2,1)} fusion(bf16[4,4,128,1152]{3,2,1,0:T(8,128)(2,1)S(1)} %collective-permute-done.36, bf16[4,4,128,1152]{3,2,1,0:T(8,128)(2,1)} %get-tuple-element.15), kind=kLoop, calls=%fused_computation | loop fusion | flops 9437184 | bytes 14155776 | tf_op jit(solution)/shard_map/convert_element_type | solution.py:212
  141.2 4.2 %collective-permute-start.28 = (bf16[128,1024]{1,0:T(8,128)(2,1)S(1)}, bf16[128,1024]{1,0:T(8,128)(2,1)S(1)}, u32[]{:S(2)}, u32[]{:S(2)}) collective-permute-start(bf16[128,1024]{1,0:T(8,128)(2,1)S(1)} %add_convert_fusion.16), channel_id=1, source_target_pairs={{64,65},{65,66},{66,67},{67,68},{68,69},{69,70},{70,71},{71,72},{7... | collective-permute-start | bytes 786440 | tf_op jit(solution)/shard_map/ppermute | solution.py:204
  150.5 5.3 %collective-permute-start.29 = (bf16[128,1024]{1,0:T(8,128)(2,1)S(1)}, bf16[128,1024]{1,0:T(8,128)(2,1)S(1)}, u32[]{:S(2)}, u32[]{:S(2)}) collective-permute-start(bf16[128,1024]{1,0:T(8,128)(2,1)S(1)} %add_convert_fusion.15), channel_id=1, source_target_pairs={{64,65},{65,66},{66,67},{67,68},{68,69},{69,70},{70,71},{71,72},{7... | collective-permute-start | bytes 786440 | tf_op jit(solution)/shard_map/ppermute | solution.py:204
  160.7 5.6 %collective-permute-start.30 = (bf16[128,1024]{1,0:T(8,128)(2,1)S(1)}, bf16[128,1024]{1,0:T(8,128)(2,1)S(1)}, u32[]{:S(2)}, u32[]{:S(2)}) collective-permute-start(bf16[128,1024]{1,0:T(8,128)(2,1)S(1)} %add_convert_fusion.14), channel_id=1, source_target_pairs={{64,65},{65,66},{66,67},{67,68},{68,69},{69,70},{70,71},{71,72},{7... | collective-permute-start | bytes 786440 | tf_op jit(solution)/shard_map/ppermute | solution.py:204
  167.4 2.8 %collective-permute-start.21 = (bf16[128,1152]{1,0:T(8,128)(2,1)S(1)}, bf16[128,1152]{1,0:T(8,128)(2,1)S(1)}, u32[]{:S(2)}, u32[]{:S(2)}) collective-permute-start(bf16[128,1152]{1,0:T(8,128)(2,1)S(1)} %add_convert_fusion.6), channel_id=1, source_target_pairs={{64,65},{65,66},{66,67},{67,68},{68,69},{69,70},{70,71},{71,72},{7... | collective-permute-start | bytes 884744 | tf_op jit(solution)/shard_map/ppermute | solution.py:204
  171.2 5.6 %collective-permute-start.31 = (bf16[128,1024]{1,0:T(8,128)(2,1)S(1)}, bf16[128,1024]{1,0:T(8,128)(2,1)S(1)}, u32[]{:S(2)}, u32[]{:S(2)}) collective-permute-start(bf16[128,1024]{1,0:T(8,128)(2,1)S(1)} %add_convert_fusion.13), channel_id=1, source_target_pairs={{64,65},{65,66},{66,67},{67,68},{68,69},{69,70},{70,71},{71,72},{7... | collective-permute-start | bytes 786440 | tf_op jit(solution)/shard_map/ppermute | solution.py:204
  177.8 3.2 %collective-permute-start.22 = (bf16[128,1152]{1,0:T(8,128)(2,1)S(1)}, bf16[128,1152]{1,0:T(8,128)(2,1)S(1)}, u32[]{:S(2)}, u32[]{:S(2)}) collective-permute-start(bf16[128,1152]{1,0:T(8,128)(2,1)S(1)} %add_convert_fusion.5), channel_id=1, source_target_pairs={{64,65},{65,66},{66,67},{67,68},{68,69},{69,70},{70,71},{71,72},{7... | collective-permute-start | bytes 884744 | tf_op jit(solution)/shard_map/ppermute | solution.py:204
  182.1 5.2 %collective-permute-start.32 = (bf16[128,1024]{1,0:T(8,128)(2,1)S(1)}, bf16[128,1024]{1,0:T(8,128)(2,1)S(1)}, u32[]{:S(2)}, u32[]{:S(2)}) collective-permute-start(bf16[128,1024]{1,0:T(8,128)(2,1)S(1)} %add_convert_fusion.12), channel_id=1, source_target_pairs={{64,65},{65,66},{66,67},{67,68},{68,69},{69,70},{70,71},{71,72},{7... | collective-permute-start | bytes 786440 | tf_op jit(solution)/shard_map/ppermute | solution.py:204
  188.3 3.6 %collective-permute-start.23 = (bf16[128,1152]{1,0:T(8,128)(2,1)S(1)}, bf16[128,1152]{1,0:T(8,128)(2,1)S(1)}, u32[]{:S(2)}, u32[]{:S(2)}) collective-permute-start(bf16[128,1152]{1,0:T(8,128)(2,1)S(1)} %add_convert_fusion.4), channel_id=1, source_target_pairs={{64,65},{65,66},{66,67},{67,68},{68,69},{69,70},{70,71},{71,72},{7... | collective-permute-start | bytes 884744 | tf_op jit(solution)/shard_map/ppermute | solution.py:204
  193.0 4.8 %collective-permute-start.33 = (bf16[128,1024]{1,0:T(8,128)(2,1)S(1)}, bf16[128,1024]{1,0:T(8,128)(2,1)S(1)}, u32[]{:S(2)}, u32[]{:S(2)}) collective-permute-start(bf16[128,1024]{1,0:T(8,128)(2,1)S(1)} %add_convert_fusion.11), channel_id=1, source_target_pairs={{64,65},{65,66},{66,67},{67,68},{68,69},{69,70},{70,71},{71,72},{7... | collective-permute-start | bytes 786440 | tf_op jit(solution)/shard_map/ppermute | solution.py:204
  198.9 3.9 %collective-permute-start.24 = (bf16[128,1152]{1,0:T(8,128)(2,1)S(1)}, bf16[128,1152]{1,0:T(8,128)(2,1)S(1)}, u32[]{:S(2)}, u32[]{:S(2)}) collective-permute-start(bf16[128,1152]{1,0:T(8,128)(2,1)S(1)} %add_convert_fusion.3), channel_id=1, source_target_pairs={{64,65},{65,66},{66,67},{67,68},{68,69},{69,70},{70,71},{71,72},{7... | collective-permute-start | bytes 884744 | tf_op jit(solution)/shard_map/ppermute | solution.py:204
  203.8 4.5 %collective-permute-start.34 = (bf16[128,1024]{1,0:T(8,128)(2,1)S(1)}, bf16[128,1024]{1,0:T(8,128)(2,1)S(1)}, u32[]{:S(2)}, u32[]{:S(2)}) collective-permute-start(bf16[128,1024]{1,0:T(8,128)(2,1)S(1)} %add_convert_fusion.10), channel_id=1, source_target_pairs={{64,65},{65,66},{66,67},{67,68},{68,69},{69,70},{70,71},{71,72},{7... | collective-permute-start | bytes 786440 | tf_op jit(solution)/shard_map/ppermute | solution.py:204
  209.3 4.3 %collective-permute-start.25 = (bf16[128,1152]{1,0:T(8,128)(2,1)S(1)}, bf16[128,1152]{1,0:T(8,128)(2,1)S(1)}, u32[]{:S(2)}, u32[]{:S(2)}) collective-permute-start(bf16[128,1152]{1,0:T(8,128)(2,1)S(1)} %add_convert_fusion.2), channel_id=1, source_target_pairs={{64,65},{65,66},{66,67},{67,68},{68,69},{69,70},{70,71},{71,72},{7... | collective-permute-start | bytes 884744 | tf_op jit(solution)/shard_map/ppermute | solution.py:204
  224.3 5.3 %reduce-scatter.2.cloned.1.call-done.s_ref = bf16[128,1152]{1,0:T(8,128)(2,1)} async-done(((bf16[2048,1152]{1,0:T(8,128)(2,1)}), bf16[128,1152]{1,0:T(8,128)(2,1)}) %reduce-scatter.2.cloned.1.call-update) | async-done | bytes 294928 | tf_op jit(solution)/shard_map/reduce_scatter | solution.py:245
  (114 shorter events, 95.8 us)
Async XLA Ops:
  7.2 90.3 %all-gather.2.cloned.1.call-start = ((), (), s32[]{:S(2)}) async-start(), calls=%async_computation.1 | async-start | bytes 9732096 | tf_op jit(solution)/shard_map/all_gather | solution.py:222
  9.0 220.5 %reduce-scatter.2.cloned.1.call-start = ((), (), s32[]{:S(2)}) async-start(), calls=%async_computation.2 | async-start | bytes 5013504 | tf_op jit(solution)/shard_map/reduce_scatter | solution.py:245
  17.2 15.7 %collective-permute-start.10 = (bf16[128,1024]{1,0:T(8,128)(2,1)S(1)}, bf16[128,1024]{1,0:T(8,128)(2,1)S(1)}, u32[]{:S(2)}, u32[]{:S(2)}) collective-permute-start(bf16[128,1024]{1,0:T(8,128)(2,1)S(1)} %constant_dynamic-update-slice_fusion.7), channel_id=1, source_target_pairs={{64,79},{65,64},{66,65},{67,66},{68,67},{69,68},{70,69},{71,70},{7... | collective-permute-start | bytes 786440 | tf_op jit(solution)/shard_map/ppermute | solution.py:204
  21.1 15.0 %collective-permute-start.1 = (bf16[128,1152]{1,0:T(8,128)(2,1)S(1)}, bf16[128,1152]{1,0:T(8,128)(2,1)S(1)}, u32[]{:S(2)}, u32[]{:S(2)}) collective-permute-start(bf16[128,1152]{1,0:T(8,128)(2,1)S(1)} %pad_maximum_fusion), channel_id=1, source_target_pairs={{64,79},{65,64},{66,65},{67,66},{68,67},{69,68},{70,69},{71,70},{7... | collective-permute-start | bytes 884744 | tf_op jit(solution)/shard_map/ppermute | solution.py:204
  32.9 9.5 %collective-permute-start.11 = (bf16[128,1024]{1,0:T(8,128)(2,1)S(1)}, bf16[128,1024]{1,0:T(8,128)(2,1)S(1)}, u32[]{:S(2)}, u32[]{:S(2)}) collective-permute-start(bf16[128,1024]{1,0:T(8,128)(2,1)S(1)} %collective-permute-done.10), channel_id=1, source_target_pairs={{64,79},{65,64},{66,65},{67,66},{68,67},{69,68},{70,69},{71,70},{7... | collective-permute-start | bytes 786440 | tf_op jit(solution)/shard_map/ppermute | solution.py:204
  36.1 9.8 %collective-permute-start.2 = (bf16[128,1152]{1,0:T(8,128)(2,1)S(1)}, bf16[128,1152]{1,0:T(8,128)(2,1)S(1)}, u32[]{:S(2)}, u32[]{:S(2)}) collective-permute-start(bf16[128,1152]{1,0:T(8,128)(2,1)S(1)} %collective-permute-done.1), channel_id=1, source_target_pairs={{64,79},{65,64},{66,65},{67,66},{68,67},{69,68},{70,69},{71,70},{7... | collective-permute-start | bytes 884744 | tf_op jit(solution)/shard_map/ppermute | solution.py:204
  42.4 9.5 %collective-permute-start.12 = (bf16[128,1024]{1,0:T(8,128)(2,1)S(1)}, bf16[128,1024]{1,0:T(8,128)(2,1)S(1)}, u32[]{:S(2)}, u32[]{:S(2)}) collective-permute-start(bf16[128,1024]{1,0:T(8,128)(2,1)S(1)} %collective-permute-done.11), channel_id=1, source_target_pairs={{64,79},{65,64},{66,65},{67,66},{68,67},{69,68},{70,69},{71,70},{7... | collective-permute-start | bytes 786440 | tf_op jit(solution)/shard_map/ppermute | solution.py:204
  45.9 9.8 %collective-permute-start.3 = (bf16[128,1152]{1,0:T(8,128)(2,1)S(1)}, bf16[128,1152]{1,0:T(8,128)(2,1)S(1)}, u32[]{:S(2)}, u32[]{:S(2)}) collective-permute-start(bf16[128,1152]{1,0:T(8,128)(2,1)S(1)} %collective-permute-done.2), channel_id=1, source_target_pairs={{64,79},{65,64},{66,65},{67,66},{68,67},{69,68},{70,69},{71,70},{7... | collective-permute-start | bytes 884744 | tf_op jit(solution)/shard_map/ppermute | solution.py:204
  51.9 9.5 %collective-permute-start.13 = (bf16[128,1024]{1,0:T(8,128)(2,1)S(1)}, bf16[128,1024]{1,0:T(8,128)(2,1)S(1)}, u32[]{:S(2)}, u32[]{:S(2)}) collective-permute-start(bf16[128,1024]{1,0:T(8,128)(2,1)S(1)} %collective-permute-done.12), channel_id=1, source_target_pairs={{64,79},{65,64},{66,65},{67,66},{68,67},{69,68},{70,69},{71,70},{7... | collective-permute-start | bytes 786440 | tf_op jit(solution)/shard_map/ppermute | solution.py:204
  55.7 9.8 %collective-permute-start.4 = (bf16[128,1152]{1,0:T(8,128)(2,1)S(1)}, bf16[128,1152]{1,0:T(8,128)(2,1)S(1)}, u32[]{:S(2)}, u32[]{:S(2)}) collective-permute-start(bf16[128,1152]{1,0:T(8,128)(2,1)S(1)} %collective-permute-done.3), channel_id=1, source_target_pairs={{64,79},{65,64},{66,65},{67,66},{68,67},{69,68},{70,69},{71,70},{7... | collective-permute-start | bytes 884744 | tf_op jit(solution)/shard_map/ppermute | solution.py:204
  61.3 9.5 %collective-permute-start.14 = (bf16[128,1024]{1,0:T(8,128)(2,1)S(1)}, bf16[128,1024]{1,0:T(8,128)(2,1)S(1)}, u32[]{:S(2)}, u32[]{:S(2)}) collective-permute-start(bf16[128,1024]{1,0:T(8,128)(2,1)S(1)} %collective-permute-done.13), channel_id=1, source_target_pairs={{64,79},{65,64},{66,65},{67,66},{68,67},{69,68},{70,69},{71,70},{7... | collective-permute-start | bytes 786440 | tf_op jit(solution)/shard_map/ppermute | solution.py:204
  65.5 9.8 %collective-permute-start.5 = (bf16[128,1152]{1,0:T(8,128)(2,1)S(1)}, bf16[128,1152]{1,0:T(8,128)(2,1)S(1)}, u32[]{:S(2)}, u32[]{:S(2)}) collective-permute-start(bf16[128,1152]{1,0:T(8,128)(2,1)S(1)} %collective-permute-done.4), channel_id=1, source_target_pairs={{64,79},{65,64},{66,65},{67,66},{68,67},{69,68},{70,69},{71,70},{7... | collective-permute-start | bytes 884744 | tf_op jit(solution)/shard_map/ppermute | solution.py:204
  70.8 9.5 %collective-permute-start.15 = (bf16[128,1024]{1,0:T(8,128)(2,1)S(1)}, bf16[128,1024]{1,0:T(8,128)(2,1)S(1)}, u32[]{:S(2)}, u32[]{:S(2)}) collective-permute-start(bf16[128,1024]{1,0:T(8,128)(2,1)S(1)} %collective-permute-done.14), channel_id=1, source_target_pairs={{64,79},{65,64},{66,65},{67,66},{68,67},{69,68},{70,69},{71,70},{7... | collective-permute-start | bytes 786440 | tf_op jit(solution)/shard_map/ppermute | solution.py:204
  75.4 9.8 %collective-permute-start.6 = (bf16[128,1152]{1,0:T(8,128)(2,1)S(1)}, bf16[128,1152]{1,0:T(8,128)(2,1)S(1)}, u32[]{:S(2)}, u32[]{:S(2)}) collective-permute-start(bf16[128,1152]{1,0:T(8,128)(2,1)S(1)} %collective-permute-done.5), channel_id=1, source_target_pairs={{64,79},{65,64},{66,65},{67,66},{68,67},{69,68},{70,69},{71,70},{7... | collective-permute-start | bytes 884744 | tf_op jit(solution)/shard_map/ppermute | solution.py:204
  80.3 9.5 %collective-permute-start.16 = (bf16[128,1024]{1,0:T(8,128)(2,1)S(1)}, bf16[128,1024]{1,0:T(8,128)(2,1)S(1)}, u32[]{:S(2)}, u32[]{:S(2)}) collective-permute-start(bf16[128,1024]{1,0:T(8,128)(2,1)S(1)} %collective-permute-done.15), channel_id=1, source_target_pairs={{64,79},{65,64},{66,65},{67,66},{68,67},{69,68},{70,69},{71,70},{7... | collective-permute-start | bytes 786440 | tf_op jit(solution)/shard_map/ppermute | solution.py:204
  85.2 9.8 %collective-permute-start.7 = (bf16[128,1152]{1,0:T(8,128)(2,1)S(1)}, bf16[128,1152]{1,0:T(8,128)(2,1)S(1)}, u32[]{:S(2)}, u32[]{:S(2)}) collective-permute-start(bf16[128,1152]{1,0:T(8,128)(2,1)S(1)} %collective-permute-done.6), channel_id=1, source_target_pairs={{64,79},{65,64},{66,65},{67,66},{68,67},{69,68},{70,69},{71,70},{7... | collective-permute-start | bytes 884744 | tf_op jit(solution)/shard_map/ppermute | solution.py:204
  120.9 10.0 %collective-permute-start.36 = (bf16[4,4,128,1152]{3,2,1,0:T(8,128)(2,1)}, bf16[4,4,128,1152]{3,2,1,0:T(8,128)(2,1)S(1)}, u32[]{:S(2)}, u32[]{:S(2)}) collective-permute-start(bf16[4,4,128,1152]{3,2,1,0:T(8,128)(2,1)} %get-tuple-element.16), channel_id=1, source_target_pairs={{0,64},{64,0},{1,65},{65,1},{2,66},{66,2},{3,67},{67,3},{4,68},{68... | collective-permute-start | bytes 14155784 | tf_op jit(solution)/shard_map/ppermute | solution.py:208
  156.8 9.5 %collective-permute-start.20 = (bf16[128,1152]{1,0:T(8,128)(2,1)S(1)}, bf16[128,1152]{1,0:T(8,128)(2,1)S(1)}, u32[]{:S(2)}, u32[]{:S(2)}) collective-permute-start(bf16[128,1152]{1,0:T(8,128)(2,1)S(1)} %add_convert_fusion.7), channel_id=1, source_target_pairs={{64,65},{65,66},{66,67},{67,68},{68,69},{69,70},{70,71},{71,72},{7... | collective-permute-start | bytes 884744 | tf_op jit(solution)/shard_map/ppermute | solution.py:204
  160.7 9.5 %collective-permute-start.30 = (bf16[128,1024]{1,0:T(8,128)(2,1)S(1)}, bf16[128,1024]{1,0:T(8,128)(2,1)S(1)}, u32[]{:S(2)}, u32[]{:S(2)}) collective-permute-start(bf16[128,1024]{1,0:T(8,128)(2,1)S(1)} %add_convert_fusion.14), channel_id=1, source_target_pairs={{64,65},{65,66},{66,67},{67,68},{68,69},{69,70},{70,71},{71,72},{7... | collective-permute-start | bytes 786440 | tf_op jit(solution)/shard_map/ppermute | solution.py:204
  171.2 9.8 %collective-permute-start.31 = (bf16[128,1024]{1,0:T(8,128)(2,1)S(1)}, bf16[128,1024]{1,0:T(8,128)(2,1)S(1)}, u32[]{:S(2)}, u32[]{:S(2)}) collective-permute-start(bf16[128,1024]{1,0:T(8,128)(2,1)S(1)} %add_convert_fusion.13), channel_id=1, source_target_pairs={{64,65},{65,66},{66,67},{67,68},{68,69},{69,70},{70,71},{71,72},{7... | collective-permute-start | bytes 786440 | tf_op jit(solution)/shard_map/ppermute | solution.py:204
  182.1 9.8 %collective-permute-start.32 = (bf16[128,1024]{1,0:T(8,128)(2,1)S(1)}, bf16[128,1024]{1,0:T(8,128)(2,1)S(1)}, u32[]{:S(2)}, u32[]{:S(2)}) collective-permute-start(bf16[128,1024]{1,0:T(8,128)(2,1)S(1)} %add_convert_fusion.12), channel_id=1, source_target_pairs={{64,65},{65,66},{66,67},{67,68},{68,69},{69,70},{70,71},{71,72},{7... | collective-permute-start | bytes 786440 | tf_op jit(solution)/shard_map/ppermute | solution.py:204
  188.3 9.5 %collective-permute-start.23 = (bf16[128,1152]{1,0:T(8,128)(2,1)S(1)}, bf16[128,1152]{1,0:T(8,128)(2,1)S(1)}, u32[]{:S(2)}, u32[]{:S(2)}) collective-permute-start(bf16[128,1152]{1,0:T(8,128)(2,1)S(1)} %add_convert_fusion.4), channel_id=1, source_target_pairs={{64,65},{65,66},{66,67},{67,68},{68,69},{69,70},{70,71},{71,72},{7... | collective-permute-start | bytes 884744 | tf_op jit(solution)/shard_map/ppermute | solution.py:204
  193.0 9.8 %collective-permute-start.33 = (bf16[128,1024]{1,0:T(8,128)(2,1)S(1)}, bf16[128,1024]{1,0:T(8,128)(2,1)S(1)}, u32[]{:S(2)}, u32[]{:S(2)}) collective-permute-start(bf16[128,1024]{1,0:T(8,128)(2,1)S(1)} %add_convert_fusion.11), channel_id=1, source_target_pairs={{64,65},{65,66},{66,67},{67,68},{68,69},{69,70},{70,71},{71,72},{7... | collective-permute-start | bytes 786440 | tf_op jit(solution)/shard_map/ppermute | solution.py:204
  203.8 9.8 %collective-permute-start.34 = (bf16[128,1024]{1,0:T(8,128)(2,1)S(1)}, bf16[128,1024]{1,0:T(8,128)(2,1)S(1)}, u32[]{:S(2)}, u32[]{:S(2)}) collective-permute-start(bf16[128,1024]{1,0:T(8,128)(2,1)S(1)} %add_convert_fusion.10), channel_id=1, source_target_pairs={{64,65},{65,66},{66,67},{67,68},{68,69},{69,70},{70,71},{71,72},{7... | collective-permute-start | bytes 786440 | tf_op jit(solution)/shard_map/ppermute | solution.py:204
  (16 other events, 107.4 us)
Sparse Core Ops, SparseCore 0:
  11.1 74.9 all-gather.1
  137.0 92.4 reduce-scatter.1

commit v7 on v6

--- a/solution.py
+++ b/solution.py
@@ -22,7 +22,7 @@
     return lax.dot_general(a, b, (((ca,), (cb,)), ((), ())), preferred_element_type=F32)
 
 
-def moe_kernel(ids_ref, xa_ref, xb_ref, wt_ref, keep_ref, send_ref, pa_ref, pb_ref, pos_s, post_s, w_s, sel_s, selt_s, xe_s, de_s, rows_s):
+def moe_kernel(ids_ref, xa_ref, xb_ref, wt_ref, keep_ref, send_ref, rows_ref, selt_ref, pos_s, post_s, w_s, sel_s, xe_s, de_s):
     e = pl.program_id(0)
     col = ids_ref[0]
     core = ids_ref[1]
@@ -78,13 +78,13 @@
     gb = (hg * u * s * (1.0 + g * (1.0 - s))).astype(BF)
     ub = (hg * gs).astype(BF)
     act = jnp.concatenate([gb, ub], axis=1)
-    rows_s[here, :feat] = dot(wh, wt[:, 2 * hid :], 1, 1).astype(BF)
+    rows_ref[:, :feat] = dot(wh, wt[:, 2 * hid :], 1, 1).astype(BF)
     lane = lax.broadcasted_iota(jnp.int32, (SLOTS, AUX), 1)
     mine = col + e
     rg_hi = rg.astype(BF).astype(F32)
     aux = jnp.where(lane == mine, rg_hi, 0.0) + jnp.where(lane == mine + AUX // 2, rg - rg_hi, 0.0)
-    rows_s[here, feat : feat + AUX] = aux.astype(BF)
-    rows_s[here, feat + AUX :] = dot(act, wt[:, : 2 * hid], 1, 1).astype(BF)
+    rows_ref[:, feat : feat + AUX] = aux.astype(BF)
+    rows_ref[:, feat + AUX :] = dot(act, wt[:, : 2 * hid], 1, 1).astype(BF)
     step = feat // NDP
 
     def halves(v):
@@ -106,16 +106,33 @@
         sel = jnp.zeros((MERGE, slots), F32)
         for j in range(NX):
             sel = jnp.where(post_s[span, j : j + 1] + float(j * SLOTS) == lane, 1.0, sel)
-        selt_s[span, :] = sel.astype(BF)
-
-    @pl.when(e == NX - 1)
-    def _():
-        for lo, hi in ((0, feat // 2), (feat // 2, feat), (feat, feat + AUX)):
-            pa_ref[:, lo:hi] = dot(selt_s[...], rows_s[:, lo:hi], 1, 0).astype(BF)
-        for lo in range(0, feat, feat // 2):
-            off = feat + AUX + lo
-            rows = rows_s[:, off : off + feat // 2]
-            pb_ref[:, lo : lo + feat // 2] = dot(selt_s[...], rows, 1, 0).astype(BF)
+        selt_ref[part : part + MERGE, :] = sel.astype(BF)
+
+
+def merge_kernel(rows_ref, selt_ref, pa_ref, pb_ref):
+    feat = pb_ref.shape[1]
+    for lo, hi in ((0, feat // 2), (feat // 2, feat), (feat, feat + AUX)):
+        pa_ref[:, lo:hi] = dot(selt_ref[...], rows_ref[:, lo:hi], 1, 0).astype(BF)
+    for lo in range(0, feat, feat // 2):
+        off = feat + AUX + lo
+        rows = rows_ref[:, off : off + feat // 2]
+        pb_ref[:, lo : lo + feat // 2] = dot(selt_ref[...], rows, 1, 0).astype(BF)
+
+
+def merge(rows, selt):
+    slots, width = rows.shape
+    tok = selt.shape[0]
+    feat = (width - AUX) // 2
+    return pl.pallas_call(
+        merge_kernel,
+        out_shape=[
+            jax.ShapeDtypeStruct((tok, feat + AUX), BF),
+            jax.ShapeDtypeStruct((tok, feat), BF),
+        ],
+        cost_estimate=pl.CostEstimate(
+            flops=2 * slots * tok * width, bytes_accessed=9_000_000, transcendentals=0
+        ),
+    )(rows, selt)
 
 
 def experts(ids, xa, xb, wt):
@@ -139,25 +156,23 @@
             out_specs=[
                 pl.BlockSpec((NY, 1, rows, hid3), lambda e, s: (0, e, 0, 0)),
                 pl.BlockSpec((NY, 1, rows, hid3), lambda e, s: (0, e, 0, 0)),
-                pl.BlockSpec((tok, feat + AUX), whole),
-                pl.BlockSpec((tok, feat), whole),
+                pl.BlockSpec((SLOTS, width), lambda e, s: (e, 0)),
+                pl.BlockSpec((tok // NX, slots), lambda e, s: (e, 0)),
             ],
             scratch_shapes=[
                 pltpu.VMEM((PLANES, tok), jnp.int32),
                 pltpu.VMEM((tok, PLANES), F32),
                 pltpu.VMEM((PLANES, tok), F32),
                 pltpu.VMEM((slots, tok), BF),
-                pltpu.VMEM((tok, slots), BF),
                 pltpu.VMEM((slots, feat), BF),
                 pltpu.VMEM((slots, feat), BF),
-                pltpu.VMEM((slots, width), BF),
             ],
         ),
         out_shape=[
             jax.ShapeDtypeStruct((NY, NX, rows, hid3), BF),
             jax.ShapeDtypeStruct((NY, NX, rows, hid3), BF),
-            jax.ShapeDtypeStruct((tok, feat + AUX), BF),
-            jax.ShapeDtypeStruct((tok, feat), BF),
+            jax.ShapeDtypeStruct((slots, width), BF),
+            jax.ShapeDtypeStruct((tok, slots), BF),
         ],
         cost_estimate=pl.CostEstimate(
             flops=flops, bytes_accessed=30_000_000, transcendentals=slots * hid3 // 3
@@ -235,13 +250,15 @@
         got_b.append(chain_b)
     got_a[-1] = jnp.where(core == 0, chip_a, got_a[-1])
     got_b[-1] = jnp.where(core == 0, chip_b, got_b[-1])
-    keep, send, pa, pb = experts(
+    keep, send, *saved = experts(
         jnp.stack([z * NX, core]),
         jnp.concatenate(got_a, axis=0),
         jnp.concatenate(got_b, axis=0),
         wa.reshape(NDP, NX, feat // NDP, 3 * hid),
     )
-    grads = add(keep, swap(send))
+    send = swap(send)
+    pa, pb = merge(*saved)
+    grads = add(keep, send)
     summed = lax.psum_scatter(
         grads.reshape(-1, 3 * hid), ("y", "x"), scatter_dimension=0, tiled=True
     )

time: 240 us -> 239 us (level)
  waiting for transfers between devices: 57.6 us -> 52.4 us
  Pallas kernels: 26.5 us -> 29.4 us
    pallas_call x0 -> x1, Pallas kernels: none -> 7.31 us  [merge(): pl.pallas_call(merge_kernel, out_shape=[jax.ShapeDtypeStruct((tok, feat +...]
    reduce_scatter x1, waiting for transfers between devices: 5.25 us -> 0.01 us  [shards(): lax.psum_scatter(grads.reshape(-1, 3 * hid), ('y', 'x'), scatter_dimensio...]
    pallas_call x1, Pallas kernels: 22.9 us -> 18.5 us  [experts(): pl.pallas_call(moe_kernel, grid_spec=pltpu.PrefetchScalarGridSpec(num_sca...]
  transfers between devices with their start and end apart: 39 -> 39, of which waited for: 20 -> 19; matrix products, arithmetic and copies ran while one was open for 13% -> 13% of each run, Pallas kernels for 0% -> 3%
where the time goes in v7:
time: 239 us; the launch traced here: 236 us
  starting transfers between devices  102 us (43%)
  waiting for transfers between devices  52.4 us (22%)
  Pallas kernels  29.4 us (12%)
  other arithmetic  26.1 us (11%)
  between operations  14.7 us (6%)
  local copies, waits for them, and re-layouts  11.9 us (5%)
    ppermute x32, starting transfers between devices, around(): return lax.ppermute(value, ('c', 'z'), pairs)  90.5 us
    ppermute x32, waiting for transfers between devices, around(): return lax.ppermute(value, ('c', 'z'), pairs)  44 us
    convert_element_type x17, other arithmetic, add(): return (a.astype(F32) + b.astype(F32)).astype(BF)  22.5 us
    pallas_call x1, Pallas kernels, experts(): pl.pallas_call(moe_kernel, grid_spec=pltpu.PrefetchScalarGridSpec(num_sca...  18.5 us
    ppermute x5, starting transfers between devices, swap(): return lax.ppermute(value, 'c', [(0, 1), (1, 0)])  11.1 us
    ppermute x5, waiting for transfers between devices, swap(): return lax.ppermute(value, 'c', [(0, 1), (1, 0)])  8.38 us
    unnamed x19, local copies, waits for them, and re-layouts  8.16 us
    pallas_call x1, Pallas kernels, merge(): pl.pallas_call(merge_kernel, out_shape=[jax.ShapeDtypeStruct((tok, feat +...  7.31 us
  transfers between devices with their start and end apart: 39, of which 19 were waited for; matrix products, arithmetic and copies ran while one was open for 13% of the time, Pallas kernels for 3%

profile of v7, /device:TPU:6, one launch (start us, length us, event | category | flops | bytes accessed | tf_op | source)
XLA Modules:
  0.0 236.2 jit_solution(4019993375340825091)
XLA Ops:
  17.2 3.8 %collective-permute-start.10 = (bf16[128,1024]{1,0:T(8,128)(2,1)S(1)}, bf16[128,1024]{1,0:T(8,128)(2,1)S(1)}, u32[]{:S(2)}, u32[]{:S(2)}) collective-permute-start(bf16[128,1024]{1,0:T(8,128)(2,1)S(1)} %constant_dynamic-update-slice_fusion.7), channel_id=1, source_target_pairs={{64,79},{65,64},{66,65},{67,66},{68,67},{69,68},{70,69},{71,70},{7... | collective-permute-start | bytes 786440 | tf_op jit(solution)/shard_map/ppermute | solution.py:219
  21.1 3.8 %collective-permute-start.1 = (bf16[128,1152]{1,0:T(8,128)(2,1)S(1)}, bf16[128,1152]{1,0:T(8,128)(2,1)S(1)}, u32[]{:S(2)}, u32[]{:S(2)}) collective-permute-start(bf16[128,1152]{1,0:T(8,128)(2,1)S(1)} %pad_maximum_fusion), channel_id=1, source_target_pairs={{64,79},{65,64},{66,65},{67,66},{68,67},{69,68},{70,69},{71,70},{7... | collective-permute-start | bytes 884744 | tf_op jit(solution)/shard_map/ppermute | solution.py:219
  25.5 7.4 %collective-permute-done.10 = bf16[128,1024]{1,0:T(8,128)(2,1)S(1)} collective-permute-done((bf16[128,1024]{1,0:T(8,128)(2,1)S(1)}, bf16[128,1024]{1,0:T(8,128)(2,1)S(1)}, u32[]{:S(2)}, u32[]{:S(2)}) %collective-permute-start.10) | collective-permute-done | bytes 262176 | tf_op jit(solution)/shard_map/ppermute | solution.py:219
  38.8 3.6 %collective-permute-done.11 = bf16[128,1024]{1,0:T(8,128)(2,1)S(1)} collective-permute-done((bf16[128,1024]{1,0:T(8,128)(2,1)S(1)}, bf16[128,1024]{1,0:T(8,128)(2,1)S(1)}, u32[]{:S(2)}, u32[]{:S(2)}) %collective-permute-start.11) | collective-permute-done | bytes 262176 | tf_op jit(solution)/shard_map/ppermute | solution.py:219
  48.5 3.3 %collective-permute-done.12 = bf16[128,1024]{1,0:T(8,128)(2,1)S(1)} collective-permute-done((bf16[128,1024]{1,0:T(8,128)(2,1)S(1)}, bf16[128,1024]{1,0:T(8,128)(2,1)S(1)}, u32[]{:S(2)}, u32[]{:S(2)}) %collective-permute-start.12) | collective-permute-done | bytes 262176 | tf_op jit(solution)/shard_map/ppermute | solution.py:219
  58.4 3.0 %collective-permute-done.13 = bf16[128,1024]{1,0:T(8,128)(2,1)S(1)} collective-permute-done((bf16[128,1024]{1,0:T(8,128)(2,1)S(1)}, bf16[128,1024]{1,0:T(8,128)(2,1)S(1)}, u32[]{:S(2)}, u32[]{:S(2)}) %collective-permute-start.13) | collective-permute-done | bytes 262176 | tf_op jit(solution)/shard_map/ppermute | solution.py:219
  82.2 3.0 %collective-permute-done.6 = bf16[128,1152]{1,0:T(8,128)(2,1)S(1)} collective-permute-done((bf16[128,1152]{1,0:T(8,128)(2,1)S(1)}, bf16[128,1152]{1,0:T(8,128)(2,1)S(1)}, u32[]{:S(2)}, u32[]{:S(2)}) %collective-permute-start.6) | collective-permute-done | bytes 294944 | tf_op jit(solution)/shard_map/ppermute | solution.py:219
  90.4 4.6 %collective-permute-done.7 = bf16[128,1152]{1,0:T(8,128)(2,1)S(1)} collective-permute-done((bf16[128,1152]{1,0:T(8,128)(2,1)S(1)}, bf16[128,1152]{1,0:T(8,128)(2,1)S(1)}, u32[]{:S(2)}, u32[]{:S(2)}) %collective-permute-start.7) | collective-permute-done | bytes 294944 | tf_op jit(solution)/shard_map/ppermute | solution.py:219
  97.9 18.5 %shard_map.119 = (bf16[4,4,128,1152]{3,2,1,0:T(8,128)(2,1)}, bf16[4,4,128,1152]{3,2,1,0:T(8,128)(2,1)}, bf16[640,2176]{1,0:T(8,128)(2,1)}, bf16[1024,640]{1,0:T(8,128)(2,1)}) custom-call(s32[2]{0:T(128)} %pad_add_fusion.ids_ref, bf16[1024,1152]{1,0:T(8,128)(2,1)} %select_dynamic-update-slice_fusion.xa_ref, bf16[1024,1024]{1,0:T(8,128)(2,1)} %copy-done, ...), custom_call_target="tpu_custom_call" | custom-call | flops 10234101760 | bytes 30000000 | tf_op jit(solution)/shard_map/pallas_call | solution.py:146
  118.3 8.1 %collective-permute-done.36 = bf16[4,4,128,1152]{3,2,1,0:T(8,128)(2,1)S(1)} collective-permute-done((bf16[4,4,128,1152]{3,2,1,0:T(8,128)(2,1)}, bf16[4,4,128,1152]{3,2,1,0:T(8,128)(2,1)S(1)}, u32[]{:S(2)}, u32[]{:S(2)}) %collective-permute-start.36) | collective-permute-done | bytes 4718624 | tf_op jit(solution)/shard_map/ppermute | solution.py:223
  126.4 6.0 %add_convert_fusion = bf16[4,4,128,1152]{3,2,1,0:T(8,128)(2,1)} fusion(bf16[4,4,128,1152]{3,2,1,0:T(8,128)(2,1)S(1)} %collective-permute-done.36, bf16[4,4,128,1152]{3,2,1,0:T(8,128)(2,1)} %get-tuple-element.19), kind=kLoop, calls=%fused_computation | loop fusion | flops 9437184 | bytes 14155776 | tf_op jit(solution)/shard_map/convert_element_type | solution.py:227
  132.4 7.3 %shard_map.120 = (bf16[1024,1152]{1,0:T(8,128)(2,1)}, bf16[1024,1024]{1,0:T(8,128)(2,1)}) custom-call(bf16[640,2176]{1,0:T(8,128)(2,1)} %get-tuple-element.15.rows_ref, bf16[1024,640]{1,0:T(8,128)(2,1)} %get-tuple-element.16.selt_ref), custom_call_target="tpu_custom_call" | custom-call | flops 2852126720 | bytes 9000000 | tf_op jit(solution)/shard_map/pallas_call | solution.py:126
  144.1 4.2 %collective-permute-start.28 = (bf16[128,1024]{1,0:T(8,128)(2,1)S(1)}, bf16[128,1024]{1,0:T(8,128)(2,1)S(1)}, u32[]{:S(2)}, u32[]{:S(2)}) collective-permute-start(bf16[128,1024]{1,0:T(8,128)(2,1)S(1)} %add_convert_fusion.16), channel_id=1, source_target_pairs={{64,65},{65,66},{66,67},{67,68},{68,69},{69,70},{70,71},{71,72},{7... | collective-permute-start | bytes 786440 | tf_op jit(solution)/shard_map/ppermute | solution.py:219
  153.4 5.2 %collective-permute-start.29 = (bf16[128,1024]{1,0:T(8,128)(2,1)S(1)}, bf16[128,1024]{1,0:T(8,128)(2,1)S(1)}, u32[]{:S(2)}, u32[]{:S(2)}) collective-permute-start(bf16[128,1024]{1,0:T(8,128)(2,1)S(1)} %add_convert_fusion.15), channel_id=1, source_target_pairs={{64,65},{65,66},{66,67},{67,68},{68,69},{69,70},{70,71},{71,72},{7... | collective-permute-start | bytes 786440 | tf_op jit(solution)/shard_map/ppermute | solution.py:219
  163.5 5.6 %collective-permute-start.30 = (bf16[128,1024]{1,0:T(8,128)(2,1)S(1)}, bf16[128,1024]{1,0:T(8,128)(2,1)S(1)}, u32[]{:S(2)}, u32[]{:S(2)}) collective-permute-start(bf16[128,1024]{1,0:T(8,128)(2,1)S(1)} %add_convert_fusion.14), channel_id=1, source_target_pairs={{64,65},{65,66},{66,67},{67,68},{68,69},{69,70},{70,71},{71,72},{7... | collective-permute-start | bytes 786440 | tf_op jit(solution)/shard_map/ppermute | solution.py:219
  174.0 5.6 %collective-permute-start.31 = (bf16[128,1024]{1,0:T(8,128)(2,1)S(1)}, bf16[128,1024]{1,0:T(8,128)(2,1)S(1)}, u32[]{:S(2)}, u32[]{:S(2)}) collective-permute-start(bf16[128,1024]{1,0:T(8,128)(2,1)S(1)} %add_convert_fusion.13), channel_id=1, source_target_pairs={{64,65},{65,66},{66,67},{67,68},{68,69},{69,70},{70,71},{71,72},{7... | collective-permute-start | bytes 786440 | tf_op jit(solution)/shard_map/ppermute | solution.py:219
  180.7 3.2 %collective-permute-start.22 = (bf16[128,1152]{1,0:T(8,128)(2,1)S(1)}, bf16[128,1152]{1,0:T(8,128)(2,1)S(1)}, u32[]{:S(2)}, u32[]{:S(2)}) collective-permute-start(bf16[128,1152]{1,0:T(8,128)(2,1)S(1)} %add_convert_fusion.5), channel_id=1, source_target_pairs={{64,65},{65,66},{66,67},{67,68},{68,69},{69,70},{70,71},{71,72},{7... | collective-permute-start | bytes 884744 | tf_op jit(solution)/shard_map/ppermute | solution.py:219
  184.9 5.2 %collective-permute-start.32 = (bf16[128,1024]{1,0:T(8,128)(2,1)S(1)}, bf16[128,1024]{1,0:T(8,128)(2,1)S(1)}, u32[]{:S(2)}, u32[]{:S(2)}) collective-permute-start(bf16[128,1024]{1,0:T(8,128)(2,1)S(1)} %add_convert_fusion.12), channel_id=1, source_target_pairs={{64,65},{65,66},{66,67},{67,68},{68,69},{69,70},{70,71},{71,72},{7... | collective-permute-start | bytes 786440 | tf_op jit(solution)/shard_map/ppermute | solution.py:219
  191.2 3.6 %collective-permute-start.23 = (bf16[128,1152]{1,0:T(8,128)(2,1)S(1)}, bf16[128,1152]{1,0:T(8,128)(2,1)S(1)}, u32[]{:S(2)}, u32[]{:S(2)}) collective-permute-start(bf16[128,1152]{1,0:T(8,128)(2,1)S(1)} %add_convert_fusion.4), channel_id=1, source_target_pairs={{64,65},{65,66},{66,67},{67,68},{68,69},{69,70},{70,71},{71,72},{7... | collective-permute-start | bytes 884744 | tf_op jit(solution)/shard_map/ppermute | solution.py:219
  195.8 4.8 %collective-permute-start.33 = (bf16[128,1024]{1,0:T(8,128)(2,1)S(1)}, bf16[128,1024]{1,0:T(8,128)(2,1)S(1)}, u32[]{:S(2)}, u32[]{:S(2)}) collective-permute-start(bf16[128,1024]{1,0:T(8,128)(2,1)S(1)} %add_convert_fusion.11), channel_id=1, source_target_pairs={{64,65},{65,66},{66,67},{67,68},{68,69},{69,70},{70,71},{71,72},{7... | collective-permute-start | bytes 786440 | tf_op jit(solution)/shard_map/ppermute | solution.py:219
  201.7 3.9 %collective-permute-start.24 = (bf16[128,1152]{1,0:T(8,128)(2,1)S(1)}, bf16[128,1152]{1,0:T(8,128)(2,1)S(1)}, u32[]{:S(2)}, u32[]{:S(2)}) collective-permute-start(bf16[128,1152]{1,0:T(8,128)(2,1)S(1)} %add_convert_fusion.3), channel_id=1, source_target_pairs={{64,65},{65,66},{66,67},{67,68},{68,69},{69,70},{70,71},{71,72},{7... | collective-permute-start | bytes 884744 | tf_op jit(solution)/shard_map/ppermute | solution.py:219
  206.6 4.5 %collective-permute-start.34 = (bf16[128,1024]{1,0:T(8,128)(2,1)S(1)}, bf16[128,1024]{1,0:T(8,128)(2,1)S(1)}, u32[]{:S(2)}, u32[]{:S(2)}) collective-permute-start(bf16[128,1024]{1,0:T(8,128)(2,1)S(1)} %add_convert_fusion.10), channel_id=1, source_target_pairs={{64,65},{65,66},{66,67},{67,68},{68,69},{69,70},{70,71},{71,72},{7... | collective-permute-start | bytes 786440 | tf_op jit(solution)/shard_map/ppermute | solution.py:219
  212.2 4.3 %collective-permute-start.25 = (bf16[128,1152]{1,0:T(8,128)(2,1)S(1)}, bf16[128,1152]{1,0:T(8,128)(2,1)S(1)}, u32[]{:S(2)}, u32[]{:S(2)}) collective-permute-start(bf16[128,1152]{1,0:T(8,128)(2,1)S(1)} %add_convert_fusion.2), channel_id=1, source_target_pairs={{64,65},{65,66},{66,67},{67,68},{68,69},{69,70},{70,71},{71,72},{7... | collective-permute-start | bytes 884744 | tf_op jit(solution)/shard_map/ppermute | solution.py:219
  221.9 3.0 %collective-permute-start.26 = (bf16[64,1152]{1,0:T(8,128)(2,1)S(1)}, bf16[64,1152]{1,0:T(8,128)(2,1)S(1)}, u32[]{:S(2)}, u32[]{:S(2)}) collective-permute-start(bf16[64,1152]{1,0:T(8,128)(2,1)S(1)} %slice.96), channel_id=1, source_target_pairs={{0,64},{64,0},{1,65},{65,1},{2,66},{66,2},{3,67},{67,3},{4,68},{68... | collective-permute-start | bytes 442376 | tf_op jit(solution)/shard_map/ppermute | solution.py:223
  (115 shorter events, 96.1 us)
Async XLA Ops:
  7.2 90.3 %all-gather.2.cloned.1.call-start = ((), (), s32[]{:S(2)}) async-start(), calls=%async_computation.1 | async-start | bytes 9732096 | tf_op jit(solution)/shard_map/all_gather | solution.py:237
  9.0 218.5 %reduce-scatter.2.cloned.1.call-start = ((), (), s32[]{:S(2)}) async-start(), calls=%async_computation.2 | async-start | bytes 5013504 | tf_op jit(solution)/shard_map/reduce_scatter | solution.py:262
  17.2 15.7 %collective-permute-start.10 = (bf16[128,1024]{1,0:T(8,128)(2,1)S(1)}, bf16[128,1024]{1,0:T(8,128)(2,1)S(1)}, u32[]{:S(2)}, u32[]{:S(2)}) collective-permute-start(bf16[128,1024]{1,0:T(8,128)(2,1)S(1)} %constant_dynamic-update-slice_fusion.7), channel_id=1, source_target_pairs={{64,79},{65,64},{66,65},{67,66},{68,67},{69,68},{70,69},{71,70},{7... | collective-permute-start | bytes 786440 | tf_op jit(solution)/shard_map/ppermute | solution.py:219
  21.1 15.0 %collective-permute-start.1 = (bf16[128,1152]{1,0:T(8,128)(2,1)S(1)}, bf16[128,1152]{1,0:T(8,128)(2,1)S(1)}, u32[]{:S(2)}, u32[]{:S(2)}) collective-permute-start(bf16[128,1152]{1,0:T(8,128)(2,1)S(1)} %pad_maximum_fusion), channel_id=1, source_target_pairs={{64,79},{65,64},{66,65},{67,66},{68,67},{69,68},{70,69},{71,70},{7... | collective-permute-start | bytes 884744 | tf_op jit(solution)/shard_map/ppermute | solution.py:219
  32.9 9.5 %collective-permute-start.11 = (bf16[128,1024]{1,0:T(8,128)(2,1)S(1)}, bf16[128,1024]{1,0:T(8,128)(2,1)S(1)}, u32[]{:S(2)}, u32[]{:S(2)}) collective-permute-start(bf16[128,1024]{1,0:T(8,128)(2,1)S(1)} %collective-permute-done.10), channel_id=1, source_target_pairs={{64,79},{65,64},{66,65},{67,66},{68,67},{69,68},{70,69},{71,70},{7... | collective-permute-start | bytes 786440 | tf_op jit(solution)/shard_map/ppermute | solution.py:219
  36.1 9.8 %collective-permute-start.2 = (bf16[128,1152]{1,0:T(8,128)(2,1)S(1)}, bf16[128,1152]{1,0:T(8,128)(2,1)S(1)}, u32[]{:S(2)}, u32[]{:S(2)}) collective-permute-start(bf16[128,1152]{1,0:T(8,128)(2,1)S(1)} %collective-permute-done.1), channel_id=1, source_target_pairs={{64,79},{65,64},{66,65},{67,66},{68,67},{69,68},{70,69},{71,70},{7... | collective-permute-start | bytes 884744 | tf_op jit(solution)/shard_map/ppermute | solution.py:219
  42.4 9.5 %collective-permute-start.12 = (bf16[128,1024]{1,0:T(8,128)(2,1)S(1)}, bf16[128,1024]{1,0:T(8,128)(2,1)S(1)}, u32[]{:S(2)}, u32[]{:S(2)}) collective-permute-start(bf16[128,1024]{1,0:T(8,128)(2,1)S(1)} %collective-permute-done.11), channel_id=1, source_target_pairs={{64,79},{65,64},{66,65},{67,66},{68,67},{69,68},{70,69},{71,70},{7... | collective-permute-start | bytes 786440 | tf_op jit(solution)/shard_map/ppermute | solution.py:219
  45.9 9.8 %collective-permute-start.3 = (bf16[128,1152]{1,0:T(8,128)(2,1)S(1)}, bf16[128,1152]{1,0:T(8,128)(2,1)S(1)}, u32[]{:S(2)}, u32[]{:S(2)}) collective-permute-start(bf16[128,1152]{1,0:T(8,128)(2,1)S(1)} %collective-permute-done.2), channel_id=1, source_target_pairs={{64,79},{65,64},{66,65},{67,66},{68,67},{69,68},{70,69},{71,70},{7... | collective-permute-start | bytes 884744 | tf_op jit(solution)/shard_map/ppermute | solution.py:219
  51.9 9.5 %collective-permute-start.13 = (bf16[128,1024]{1,0:T(8,128)(2,1)S(1)}, bf16[128,1024]{1,0:T(8,128)(2,1)S(1)}, u32[]{:S(2)}, u32[]{:S(2)}) collective-permute-start(bf16[128,1024]{1,0:T(8,128)(2,1)S(1)} %collective-permute-done.12), channel_id=1, source_target_pairs={{64,79},{65,64},{66,65},{67,66},{68,67},{69,68},{70,69},{71,70},{7... | collective-permute-start | bytes 786440 | tf_op jit(solution)/shard_map/ppermute | solution.py:219
  55.7 9.8 %collective-permute-start.4 = (bf16[128,1152]{1,0:T(8,128)(2,1)S(1)}, bf16[128,1152]{1,0:T(8,128)(2,1)S(1)}, u32[]{:S(2)}, u32[]{:S(2)}) collective-permute-start(bf16[128,1152]{1,0:T(8,128)(2,1)S(1)} %collective-permute-done.3), channel_id=1, source_target_pairs={{64,79},{65,64},{66,65},{67,66},{68,67},{69,68},{70,69},{71,70},{7... | collective-permute-start | bytes 884744 | tf_op jit(solution)/shard_map/ppermute | solution.py:219
  61.3 9.5 %collective-permute-start.14 = (bf16[128,1024]{1,0:T(8,128)(2,1)S(1)}, bf16[128,1024]{1,0:T(8,128)(2,1)S(1)}, u32[]{:S(2)}, u32[]{:S(2)}) collective-permute-start(bf16[128,1024]{1,0:T(8,128)(2,1)S(1)} %collective-permute-done.13), channel_id=1, source_target_pairs={{64,79},{65,64},{66,65},{67,66},{68,67},{69,68},{70,69},{71,70},{7... | collective-permute-start | bytes 786440 | tf_op jit(solution)/shard_map/ppermute | solution.py:219
  65.5 9.8 %collective-permute-start.5 = (bf16[128,1152]{1,0:T(8,128)(2,1)S(1)}, bf16[128,1152]{1,0:T(8,128)(2,1)S(1)}, u32[]{:S(2)}, u32[]{:S(2)}) collective-permute-start(bf16[128,1152]{1,0:T(8,128)(2,1)S(1)} %collective-permute-done.4), channel_id=1, source_target_pairs={{64,79},{65,64},{66,65},{67,66},{68,67},{69,68},{70,69},{71,70},{7... | collective-permute-start | bytes 884744 | tf_op jit(solution)/shard_map/ppermute | solution.py:219
  70.8 9.5 %collective-permute-start.15 = (bf16[128,1024]{1,0:T(8,128)(2,1)S(1)}, bf16[128,1024]{1,0:T(8,128)(2,1)S(1)}, u32[]{:S(2)}, u32[]{:S(2)}) collective-permute-start(bf16[128,1024]{1,0:T(8,128)(2,1)S(1)} %collective-permute-done.14), channel_id=1, source_target_pairs={{64,79},{65,64},{66,65},{67,66},{68,67},{69,68},{70,69},{71,70},{7... | collective-permute-start | bytes 786440 | tf_op jit(solution)/shard_map/ppermute | solution.py:219
  75.3 9.8 %collective-permute-start.6 = (bf16[128,1152]{1,0:T(8,128)(2,1)S(1)}, bf16[128,1152]{1,0:T(8,128)(2,1)S(1)}, u32[]{:S(2)}, u32[]{:S(2)}) collective-permute-start(bf16[128,1152]{1,0:T(8,128)(2,1)S(1)} %collective-permute-done.5), channel_id=1, source_target_pairs={{64,79},{65,64},{66,65},{67,66},{68,67},{69,68},{70,69},{71,70},{7... | collective-permute-start | bytes 884744 | tf_op jit(solution)/shard_map/ppermute | solution.py:219
  80.2 9.5 %collective-permute-start.16 = (bf16[128,1024]{1,0:T(8,128)(2,1)S(1)}, bf16[128,1024]{1,0:T(8,128)(2,1)S(1)}, u32[]{:S(2)}, u32[]{:S(2)}) collective-permute-start(bf16[128,1024]{1,0:T(8,128)(2,1)S(1)} %collective-permute-done.15), channel_id=1, source_target_pairs={{64,79},{65,64},{66,65},{67,66},{68,67},{69,68},{70,69},{71,70},{7... | collective-permute-start | bytes 786440 | tf_op jit(solution)/shard_map/ppermute | solution.py:219
  85.2 9.8 %collective-permute-start.7 = (bf16[128,1152]{1,0:T(8,128)(2,1)S(1)}, bf16[128,1152]{1,0:T(8,128)(2,1)S(1)}, u32[]{:S(2)}, u32[]{:S(2)}) collective-permute-start(bf16[128,1152]{1,0:T(8,128)(2,1)S(1)} %collective-permute-done.6), channel_id=1, source_target_pairs={{64,79},{65,64},{66,65},{67,66},{68,67},{69,68},{70,69},{71,70},{7... | collective-permute-start | bytes 884744 | tf_op jit(solution)/shard_map/ppermute | solution.py:219
  116.4 10.0 %collective-permute-start.36 = (bf16[4,4,128,1152]{3,2,1,0:T(8,128)(2,1)}, bf16[4,4,128,1152]{3,2,1,0:T(8,128)(2,1)S(1)}, u32[]{:S(2)}, u32[]{:S(2)}) collective-permute-start(bf16[4,4,128,1152]{3,2,1,0:T(8,128)(2,1)} %get-tuple-element.20), channel_id=1, source_target_pairs={{0,64},{64,0},{1,65},{65,1},{2,66},{66,2},{3,67},{67,3},{4,68},{68... | collective-permute-start | bytes 14155784 | tf_op jit(solution)/shard_map/ppermute | solution.py:223
  163.5 9.5 %collective-permute-start.30 = (bf16[128,1024]{1,0:T(8,128)(2,1)S(1)}, bf16[128,1024]{1,0:T(8,128)(2,1)S(1)}, u32[]{:S(2)}, u32[]{:S(2)}) collective-permute-start(bf16[128,1024]{1,0:T(8,128)(2,1)S(1)} %add_convert_fusion.14), channel_id=1, source_target_pairs={{64,65},{65,66},{66,67},{67,68},{68,69},{69,70},{70,71},{71,72},{7... | collective-permute-start | bytes 786440 | tf_op jit(solution)/shard_map/ppermute | solution.py:219
  174.0 9.8 %collective-permute-start.31 = (bf16[128,1024]{1,0:T(8,128)(2,1)S(1)}, bf16[128,1024]{1,0:T(8,128)(2,1)S(1)}, u32[]{:S(2)}, u32[]{:S(2)}) collective-permute-start(bf16[128,1024]{1,0:T(8,128)(2,1)S(1)} %add_convert_fusion.13), channel_id=1, source_target_pairs={{64,65},{65,66},{66,67},{67,68},{68,69},{69,70},{70,71},{71,72},{7... | collective-permute-start | bytes 786440 | tf_op jit(solution)/shard_map/ppermute | solution.py:219
  180.7 9.5 %collective-permute-start.22 = (bf16[128,1152]{1,0:T(8,128)(2,1)S(1)}, bf16[128,1152]{1,0:T(8,128)(2,1)S(1)}, u32[]{:S(2)}, u32[]{:S(2)}) collective-permute-start(bf16[128,1152]{1,0:T(8,128)(2,1)S(1)} %add_convert_fusion.5), channel_id=1, source_target_pairs={{64,65},{65,66},{66,67},{67,68},{68,69},{69,70},{70,71},{71,72},{7... | collective-permute-start | bytes 884744 | tf_op jit(solution)/shard_map/ppermute | solution.py:219
  184.9 9.8 %collective-permute-start.32 = (bf16[128,1024]{1,0:T(8,128)(2,1)S(1)}, bf16[128,1024]{1,0:T(8,128)(2,1)S(1)}, u32[]{:S(2)}, u32[]{:S(2)}) collective-permute-start(bf16[128,1024]{1,0:T(8,128)(2,1)S(1)} %add_convert_fusion.12), channel_id=1, source_target_pairs={{64,65},{65,66},{66,67},{67,68},{68,69},{69,70},{70,71},{71,72},{7... | collective-permute-start | bytes 786440 | tf_op jit(solution)/shard_map/ppermute | solution.py:219
  191.2 9.5 %collective-permute-start.23 = (bf16[128,1152]{1,0:T(8,128)(2,1)S(1)}, bf16[128,1152]{1,0:T(8,128)(2,1)S(1)}, u32[]{:S(2)}, u32[]{:S(2)}) collective-permute-start(bf16[128,1152]{1,0:T(8,128)(2,1)S(1)} %add_convert_fusion.4), channel_id=1, source_target_pairs={{64,65},{65,66},{66,67},{67,68},{68,69},{69,70},{70,71},{71,72},{7... | collective-permute-start | bytes 884744 | tf_op jit(solution)/shard_map/ppermute | solution.py:219
  195.8 9.8 %collective-permute-start.33 = (bf16[128,1024]{1,0:T(8,128)(2,1)S(1)}, bf16[128,1024]{1,0:T(8,128)(2,1)S(1)}, u32[]{:S(2)}, u32[]{:S(2)}) collective-permute-start(bf16[128,1024]{1,0:T(8,128)(2,1)S(1)} %add_convert_fusion.11), channel_id=1, source_target_pairs={{64,65},{65,66},{66,67},{67,68},{68,69},{69,70},{70,71},{71,72},{7... | collective-permute-start | bytes 786440 | tf_op jit(solution)/shard_map/ppermute | solution.py:219
  206.6 9.8 %collective-permute-start.34 = (bf16[128,1024]{1,0:T(8,128)(2,1)S(1)}, bf16[128,1024]{1,0:T(8,128)(2,1)S(1)}, u32[]{:S(2)}, u32[]{:S(2)}) collective-permute-start(bf16[128,1024]{1,0:T(8,128)(2,1)S(1)} %add_convert_fusion.10), channel_id=1, source_target_pairs={{64,65},{65,66},{66,67},{67,68},{68,69},{69,70},{70,71},{71,72},{7... | collective-permute-start | bytes 786440 | tf_op jit(solution)/shard_map/ppermute | solution.py:219
  (16 other events, 108.1 us)
Sparse Core Ops, SparseCore 0:
  11.1 74.9 all-gather.1
  132.5 92.5 reduce-scatter.1
